TPU v7x, 128 devices: a whole 4x4x4 slice. The times are simulated.
128 devices in a mesh: ctx: 16 (over z, y_lo, core), exp: 8 (over x, y_hi).
Axes of the slice: x: 4, y: 4 (y_hi: 2, y_lo: 2; y = y_hi * 2 + y_lo), z: 4, core: 2. Of those that a mesh axis runs over, the one named last changes fastest.
Arguments:
- queries: bfloat16 [8, 2048, 2048], P('exp', 'ctx'), may hold values from -18 to 18
- keys: bfloat16 [8, 2048, 2048], P('exp', 'ctx'), may hold values from -18 to 18
- values: bfloat16 [8, 2048, 2048], P('exp', 'ctx'), may hold values from -7 to 7
- segment_ids: int32 [8, 2048], P('exp', 'ctx'), may hold values from 0 to 2, never falling along the last dimension, each value on 1 to 1024 neighbouring positions
- hidden_in: bfloat16 [8, 2048, 2048], P('exp', 'ctx'), may hold values from -6 to 6
- out_weight: bfloat16 [2048, 2048], replicated, may hold values from -0.125 to 0.125
- norm_gain: float32 [2048], replicated, may hold values from 0.25 to 1.75
- expert_ids: int32 [8, 2048, 6], P('exp', 'ctx'), may hold values from 0 to 63, all different within a row; in each aligned block of 128 rows (0 to 127, 128 to 255, ..., all dimensions but the last counted through in order) at most 16 rows name the same one
- gate_codes: int32 [8, 2048, 6], P('exp', 'ctx'), may hold values from 1 to 64
- w_in: bfloat16 [128, 2048, 1408], P(('ctx', 'exp')), may hold values from -0.125 to 0.125
- w_down: bfloat16 [128, 704, 2048], P(('ctx', 'exp')), may hold values from -0.15625 to 0.15625
Outputs:
- layer_out: bfloat16 [8, 2048, 2048], P('exp', 'ctx')
Inputs may be any that keep to these rules, and one draw needn't show every extreme that they name: `segment_ids`: segment numbers never fall along a stream; every segment has at most 1024 positions and some segment of each stream has exactly 1024. `expert_ids`: each token names 6 different experts; among the tokens of one device no expert is named more than 16 times, and some device reaches 16.
All inputs are finite; a program needn't handle non-finite values.
Results may differ from a plain program's by a relative error of at most 0.0095.
Values may be sent and summed in bfloat16 or wider, within the bound.
No kernel may reach another device: no remote copies, remote signals or barrier semaphores. Data moves between devices by JAX's collectives and lax.ppermute only.
A program may use at most 128 MiB of HBM per device.

v0:
```python
import jax
import jax.numpy as jnp
from jax import lax
from jax.experimental import pallas as pl
from jax.experimental.pallas import tpu as pltpu
from jax.sharding import PartitionSpec as P

D = 2048
HEADS = 16
HEAD_DIM = 128
TOPK = 6
ROWS = 128
EXPERTS = 64
SLOTS = 16
HALF = 704
SEG_MOST = 1024
SEG_ROWS = 16
PACK_ROWS = 3 * ROWS + SEG_ROWS
Q_BLOCK = 256
NEG_FILL = -1e30

VMEM = pl.BlockSpec(memory_space=pltpu.VMEM)
f32 = jnp.float32
bf16 = jnp.bfloat16


def params(mib):
    return pltpu.CompilerParams(vmem_limit_bytes=mib << 20)


def pack_kernel(q_ref, k_ref, v_ref, seg_ref, out_ref):
    seg = jnp.broadcast_to(seg_ref[...].astype(f32), (SEG_ROWS, ROWS)).astype(bf16)
    for head in range(HEADS):
        lanes = slice(head * HEAD_DIM, (head + 1) * HEAD_DIM)
        out_ref[head, 0:ROWS, :] = q_ref[:, lanes]
        out_ref[head, ROWS : 2 * ROWS, :] = k_ref[:, lanes]
        out_ref[head, 2 * ROWS : 3 * ROWS, :] = v_ref[:, lanes]
        out_ref[head, 3 * ROWS :, :] = seg


def attend_kernel(x_ref, out_ref):
    blocks = x_ref.shape[0]
    seg = x_ref[:, 3 * ROWS :, :].astype(f32)
    first = (jnp.sum(jnp.where(seg < 0.5, 1.0, 0.0)) * (1.0 / SEG_ROWS)).astype(jnp.int32)
    second = (jnp.sum(jnp.where(seg < 1.5, 1.0, 0.0)) * (1.0 / SEG_ROWS)).astype(jnp.int32)
    per = Q_BLOCK // ROWS
    for block in range(blocks // per):
        start = block * per
        low = max(0, start - SEG_MOST // ROWS)
        high = start + per
        width = (high - low) * ROWS
        query = x_ref[start:high, 0:ROWS, :].reshape(Q_BLOCK, HEAD_DIM)
        key = x_ref[low:high, ROWS : 2 * ROWS, :].reshape(width, HEAD_DIM)
        value = x_ref[low:high, 2 * ROWS : 3 * ROWS, :].reshape(width, HEAD_DIM)
        scores = lax.dot_general(
            query, key, (((1,), (1,)), ((), ())), preferred_element_type=f32
        ) * HEAD_DIM ** (-0.5)
        row = start * ROWS + lax.broadcasted_iota(jnp.int32, (Q_BLOCK, 1), 0)
        column = low * ROWS + lax.broadcasted_iota(jnp.int32, (Q_BLOCK, width), 1)
        begin = jnp.where(row < first, 0, jnp.where(row < second, first, second))
        allowed = (column <= row) & (column >= begin)
        scores = jnp.where(allowed, scores, NEG_FILL)
        top = jnp.max(scores, axis=-1, keepdims=True)
        probs = jnp.exp(scores - top)
        total = jnp.sum(probs, axis=-1, keepdims=True)
        mixed = jnp.dot(probs.astype(bf16), value, preferred_element_type=f32)
        out_ref[start:high] = (mixed / total).astype(bf16).reshape(per, ROWS, HEAD_DIM)


def route_kernel(ids_ref, codes_ref, pick_ref, weight_ref):
    expert = lax.broadcasted_iota(jnp.int32, (EXPERTS, ROWS), 0)
    member = jnp.zeros((EXPERTS, ROWS), f32)
    code = jnp.zeros((EXPERTS, ROWS), f32)
    for k in range(TOPK):
        named = expert == ids_ref[k : k + 1, :]
        member = member + jnp.where(named, 1.0, 0.0)
        code = code + jnp.where(named, codes_ref[k : k + 1, :].astype(f32), 0.0)
    earlier = lax.broadcasted_iota(jnp.int32, (ROWS, ROWS), 0) < lax.broadcasted_iota(
        jnp.int32, (ROWS, ROWS), 1
    )
    rank = jnp.dot(
        member.astype(bf16), jnp.where(earlier, 1.0, 0.0).astype(bf16), preferred_element_type=f32
    )
    place = (member * (rank + 1.0)).astype(bf16)

    def spread(table, count):
        rows = EXPERTS * count
        own = lax.broadcasted_iota(jnp.int32, (rows, EXPERTS), 0) // count
        mine = own == lax.broadcasted_iota(jnp.int32, (rows, EXPERTS), 1)
        return jnp.dot(jnp.where(mine, 1.0, 0.0).astype(bf16), table, preferred_element_type=f32)

    def slot(rows):
        return ((lax.broadcasted_iota(jnp.int32, (rows, ROWS), 0) & (SLOTS - 1)) + 1).astype(f32)

    here = spread(place, SLOTS) == slot(EXPERTS * SLOTS)
    pick_ref[...] = jnp.where(here, 1.0, 0.0).astype(bf16)
    both = spread(place, 2 * SLOTS) == slot(EXPERTS * 2 * SLOTS)
    weight_ref[...] = jnp.where(both, spread(code.astype(bf16), 2 * SLOTS), 0.0).astype(bf16)


K_STEPS = 4
SEND_STEPS = 4


def project_kernel(heads_ref, weight_ref, hidden_ref, gain_ref, pick_ref, mixed_ref, send_ref, acc, rows, sems):
    step = pl.program_id(0)
    per = HEADS // K_STEPS
    part = jnp.concatenate([heads_ref[i] for i in range(per)], axis=1)
    product = jnp.dot(part, weight_ref[...], preferred_element_type=f32)

    @pl.when(step == 0)
    def _():
        acc[...] = product

    @pl.when(step > 0)
    def _():
        acc[...] += product

    @pl.when(step == K_STEPS - 1)
    def _():
        mixed = (hidden_ref[...].astype(f32) + acc[...]).astype(bf16)
        mixed_ref[...] = mixed
        wide = mixed.astype(f32)
        scale = lax.rsqrt(jnp.mean(wide * wide, axis=-1, keepdims=True) + 1e-06)
        normed = (wide * scale * gain_ref[...]).astype(bf16)
        count = EXPERTS // SEND_STEPS
        copies = []
        for chunk in range(SEND_STEPS):
            span = slice(chunk * count * SLOTS, (chunk + 1) * count * SLOTS)
            picked = jnp.dot(pick_ref[span, :], normed, preferred_element_type=f32)
            rows[chunk] = picked.astype(bf16).reshape(count, SLOTS, D)
            for half in range(2):
                copy = pltpu.make_async_copy(
                    rows.at[chunk],
                    send_ref.at[pl.ds(chunk * count, count), half],
                    sems.at[chunk, half],
                )
                copy.start()
                copies.append(copy)
        for copy in copies:
            copy.wait()


def expert_kernel(x_ref, in_ref, down_ref, out_ref):
    inner = jnp.dot(x_ref[...], in_ref[...], preferred_element_type=f32)
    gate = inner[:, :HALF]
    up = pltpu.roll(inner, HALF, axis=1)[:, :HALF]
    act = (gate / (1.0 + jnp.exp(-gate)) * up).astype(bf16)
    out_ref[...] = jnp.dot(act, down_ref[...], preferred_element_type=f32).astype(bf16)


def combine_kernel(rows_ref, weight_ref, mixed_ref, out_ref, acc, total):
    step = pl.program_id(0)
    over = (((0,), (0,)), ((), ()))
    weight = weight_ref[...]
    product = lax.dot_general(weight, rows_ref[...], over, preferred_element_type=f32)
    ones = jnp.ones((weight.shape[0], ROWS), bf16)
    count = lax.dot_general(weight, ones, over, preferred_element_type=f32)

    @pl.when(step == 0)
    def _():
        acc[...] = product
        total[...] = count

    @pl.when(step > 0)
    def _():
        acc[...] += product
        total[...] += count

    @pl.when(step == pl.num_programs(0) - 1)
    def _():
        routed = acc[...] / (total[:, 0:1] * 0.5)
        out_ref[...] = (mixed_ref[...].astype(f32) + routed).astype(bf16)


def local(
    queries,
    keys,
    values,
    segment_ids,
    hidden_in,
    out_weight,
    norm_gain,
    expert_ids,
    gate_codes,
    w_in,
    w_down,
):
    owners = 2 * EXPERTS
    shape = jax.ShapeDtypeStruct
    packed = pl.pallas_call(
        pack_kernel,
        out_shape=shape((HEADS, PACK_ROWS, HEAD_DIM), bf16),
        in_specs=[VMEM] * 4,
        out_specs=VMEM,
        name="pack",
    )(queries[0], keys[0], values[0], segment_ids)
    swapped = lax.all_to_all(packed, "ctx", split_axis=0, concat_axis=0, tiled=True)
    attended = pl.pallas_call(
        attend_kernel,
        out_shape=shape((HEADS, ROWS, HEAD_DIM), bf16),
        in_specs=[VMEM],
        out_specs=VMEM,
        compiler_params=params(40),
        name="attend",
    )(swapped)
    heads = lax.all_to_all(attended, "ctx", split_axis=0, concat_axis=0, tiled=True)
    pick, weight = pl.pallas_call(
        route_kernel,
        out_shape=(
            shape((EXPERTS * SLOTS, ROWS), bf16),
            shape((owners * SLOTS, ROWS), bf16),
        ),
        in_specs=[VMEM] * 2,
        out_specs=(VMEM, VMEM),
        name="route",
    )(expert_ids[0].T, gate_codes[0].T)
    per = HEADS // K_STEPS
    mixed, send = pl.pallas_call(
        project_kernel,
        grid=(K_STEPS,),
        out_shape=(
            shape((ROWS, D), bf16),
            shape((EXPERTS, 2, SLOTS, D), bf16),
        ),
        in_specs=[
            pl.BlockSpec((per, ROWS, HEAD_DIM), lambda i: (i, 0, 0)),
            pl.BlockSpec((D // K_STEPS, D), lambda i: (i, 0)),
            pl.BlockSpec((ROWS, D), lambda i: (0, 0)),
            pl.BlockSpec((1, D), lambda i: (0, 0)),
            pl.BlockSpec((EXPERTS * SLOTS, ROWS), lambda i: (0, 0)),
        ],
        out_specs=(
            pl.BlockSpec((ROWS, D), lambda i: (0, 0)),
            pl.BlockSpec(memory_space=pl.ANY),
        ),
        scratch_shapes=[
            pltpu.VMEM((ROWS, D), f32),
            pltpu.VMEM((SEND_STEPS, EXPERTS // SEND_STEPS, SLOTS, D), bf16),
            pltpu.SemaphoreType.DMA((SEND_STEPS, 2)),
        ],
        compiler_params=params(40),
        name="project",
    )(heads, out_weight, hidden_in[0], norm_gain[None], pick)
    arrived = lax.all_to_all(
        send.reshape(owners, SLOTS, D), ("ctx", "exp"), split_axis=0, concat_axis=0, tiled=True
    )
    block = 256
    results = pl.pallas_call(
        expert_kernel,
        grid=(owners * SLOTS // block,),
        out_shape=shape((owners * SLOTS, D), bf16),
        in_specs=[
            pl.BlockSpec((block, D), lambda i: (i, 0)),
            pl.BlockSpec((D, 2 * HALF), lambda i: (0, 0), pipeline_mode=pl.Buffered(1)),
            pl.BlockSpec((HALF, D), lambda i: (0, 0), pipeline_mode=pl.Buffered(1)),
        ],
        out_specs=pl.BlockSpec((block, D), lambda i: (i, 0)),
        compiler_params=params(48),
        name="experts",
    )(arrived.reshape(owners * SLOTS, D), w_in[0], w_down[0])
    returned = lax.all_to_all(
        results.reshape(owners, SLOTS, D), ("ctx", "exp"), split_axis=0, concat_axis=0, tiled=True
    )
    layer_out = pl.pallas_call(
        combine_kernel,
        grid=(owners * SLOTS // block,),
        out_shape=shape((ROWS, D), bf16),
        in_specs=[
            pl.BlockSpec((block, D), lambda i: (i, 0)),
            pl.BlockSpec((block, ROWS), lambda i: (i, 0)),
            pl.BlockSpec((ROWS, D), lambda i: (0, 0)),
        ],
        out_specs=pl.BlockSpec((ROWS, D), lambda i: (0, 0)),
        scratch_shapes=[pltpu.VMEM((ROWS, D), f32), pltpu.VMEM((ROWS, ROWS), f32)],
        compiler_params=params(40),
        name="combine",
    )(returned.reshape(owners * SLOTS, D), weight, mixed)
    return layer_out[None]


def solution(mesh):
    placed = (
        P("exp", "ctx", None),
        P("exp", "ctx", None),
        P("exp", "ctx", None),
        P("exp", "ctx"),
        P("exp", "ctx", None),
        P(),
        P(),
        P("exp", "ctx", None),
        P("exp", "ctx", None),
        P(("ctx", "exp"), None, None),
        P(("ctx", "exp"), None, None),
    )
    return jax.shard_map(
        local, mesh=mesh, in_specs=placed, out_specs=P("exp", "ctx", None), check_vma=False
    )
```

profile of v0, /device:TPU:1, one launch (start us, length us, event | category | flops | bytes accessed | tf_op | source)
XLA Modules:
  0.0 298.7 jit_solution(16774309647809586971)
XLA Ops:
  0.0 0.0 copy-start.5
  0.0 0.0 copy-start.6
  0.0 0.0 copy-start.4
  0.0 0.0 copy-start.1
  0.0 2.9 pack.1
  2.9 30.3 %all_to_all.20.x_ref = bf16[16,400,128]{2,1,0:T(8,128)(2,1)S(1)} all-to-all(bf16[16,400,128]{2,1,0:T(8,128)(2,1)} %pack.1), channel_id=1, replica_groups=mesh['ctx'=16,'exp'=8] {'ctx'}, dimensions={0} | all-to-all | bytes 3276800 | tf_op jit(solution)/shard_map/all_to_all | solution.py:198
  33.2 5.1 %attend.1 = bf16[16,128,128]{2,1,0:T(8,128)(2,1)} custom-call(bf16[16,400,128]{2,1,0:T(8,128)(2,1)S(1)} %all_to_all.20.x_ref), custom_call_target="tpu_custom_call" | custom-call | tf_op jit(solution)/shard_map/attend/pallas_call | solution.py:199
  38.3 3.8 %all-to-all-start.1 = ((bf16[16,128,128]{2,1,0:T(8,128)(2,1)}), bf16[16,128,128]{2,1,0:T(8,128)(2,1)S(1)}, u32[]{:S(2)}, u32[]{:S(2)}) async-start(bf16[16,128,128]{2,1,0:T(8,128)(2,1)} %attend.1), calls=%async_computation.1 | async-start | bytes 1048576 | tf_op jit(solution)/shard_map/all_to_all | solution.py:207
  42.1 0.0 copy-done.5
  42.1 0.0 copy-done.6
  42.1 0.6 copy_bitcast_fusion
  42.7 2.1 route.1
  44.9 7.0 %all-to-all-done.1.heads_ref = bf16[16,128,128]{2,1,0:T(8,128)(2,1)S(1)} async-done(((bf16[16,128,128]{2,1,0:T(8,128)(2,1)}), bf16[16,128,128]{2,1,0:T(8,128)(2,1)S(1)}, u32[]{:S(2)}, u32[]{:S(2)}) %all-to-all-start.1) | async-done | bytes 524320 | tf_op jit(solution)/shard_map/all_to_all | solution.py:207
  51.9 0.0 copy-done.4
  51.9 0.0 copy-done.1
  51.9 0.0 copy-start.3
  51.9 0.9 copy-done.3
  52.8 7.7 %project.1 = (bf16[128,2048]{1,0:T(8,128)(2,1)S(1)}, bf16[64,2,16,2048]{3,2,1,0:T(8,128)(2,1)S(1)}) custom-call(bf16[16,128,128]{2,1,0:T(8,128)(2,1)S(1)} %all-to-all-done.1.heads_ref, bf16[2048,2048]{1,0:T(8,128)(2,1)} %weight_ref.1, bf16[128,2048]{1,0:T(8,128)(2,1)S(1)} %bitcast.23, f32[1,2048]{1,0:T(1,128)S(1)} %bitcast.24, bf16[1024,128]{1,0:T(8,128)(2,1)S(1)} %copy-done.3), custom_call_target="tpu_custom_call" | custom-call | tf_op jit(solution)/shard_map/project/pallas_call | solution.py:219
  60.5 0.0 copy-start
  60.5 105.2 %all_to_all.21 = bf16[128,16,2048]{2,1,0:T(8,128)(2,1)} all-to-all(bf16[128,16,2048]{2,1,0:T(8,128)(2,1)S(1)} %bitcast.21), channel_id=1, replica_groups=mesh['ctx'=16,'exp'=8] {'ctx','exp'}, dimensions={0} | all-to-all | bytes 16777216 | tf_op jit(solution)/shard_map/all_to_all | solution.py:245
  165.8 0.0 copy-done
  165.8 25.6 %experts.1 = bf16[2048,2048]{1,0:T(8,128)(2,1)} custom-call(bf16[2048,2048]{1,0:T(8,128)(2,1)} %bitcast.25, bf16[2048,1408]{1,0:T(8,128)(2,1)} %bitcast.27, bf16[704,2048]{1,0:T(8,128)(2,1)S(1)} %bitcast.22), custom_call_target="tpu_custom_call" | custom-call | tf_op jit(solution)/shard_map/experts/pallas_call | solution.py:249
  191.4 0.0 copy-start.2
  191.4 102.6 %all_to_all.22 = bf16[128,16,2048]{2,1,0:T(8,128)(2,1)S(1)} all-to-all(bf16[128,16,2048]{2,1,0:T(8,128)(2,1)} %bitcast.26), channel_id=1, replica_groups=mesh['ctx'=16,'exp'=8] {'ctx','exp'}, dimensions={0} | all-to-all | bytes 16777216 | tf_op jit(solution)/shard_map/all_to_all | solution.py:262
  294.0 0.0 copy-done.2
  294.0 4.7 %combine.1 = bf16[128,2048]{1,0:T(8,128)(2,1)} custom-call(bf16[2048,2048]{1,0:T(8,128)(2,1)S(1)} %bitcast.20, bf16[2048,128]{1,0:T(8,128)(2,1)S(1)} %copy-done.2, bf16[128,2048]{1,0:T(8,128)(2,1)S(1)} %get-tuple-element.12.mixed_ref), custom_call_target="tpu_custom_call" | custom-call | tf_op jit(solution)/shard_map/combine/pallas_call | solution.py:265
Async XLA Ops:
  0.0 42.1 %copy-start.5 = (s32[1,128,6]{1,0,2:T(1,128)S(1)}, s32[1,128,6]{1,0,2:T(1,128)}, u32[]{:S(2)}) copy-start(s32[1,128,6]{1,0,2:T(1,128)} %param.19) | copy-start | bytes 9220
  0.0 42.1 %copy-start.6 = (s32[1,128,6]{1,0,2:T(1,128)S(1)}, s32[1,128,6]{1,0,2:T(1,128)}, u32[]{:S(2)}) copy-start(s32[1,128,6]{1,0,2:T(1,128)} %param.18) | copy-start | bytes 9220
  0.0 51.9 %copy-start.4 = (f32[2048]{0:T(1024)S(1)}, f32[2048]{0:T(1024)}, u32[]{:S(2)}) copy-start(f32[2048]{0:T(1024)} %param.17) | copy-start | bytes 24580
  0.0 51.9 %copy-start.1 = (bf16[1,128,2048]{2,1,0:T(8,128)(2,1)S(1)}, bf16[1,128,2048]{2,1,0:T(8,128)(2,1)}, u32[]{:S(2)}) copy-start(bf16[1,128,2048]{2,1,0:T(8,128)(2,1)} %param.15) | copy-start | bytes 1572868
  38.3 13.6 %all-to-all-start.1 = ((bf16[16,128,128]{2,1,0:T(8,128)(2,1)}), bf16[16,128,128]{2,1,0:T(8,128)(2,1)S(1)}, u32[]{:S(2)}, u32[]{:S(2)}) async-start(bf16[16,128,128]{2,1,0:T(8,128)(2,1)} %attend.1), calls=%async_computation.1 | async-start | bytes 1048576 | tf_op jit(solution)/shard_map/all_to_all | solution.py:207
  51.9 1.0 copy-start.3
  60.5 105.3 %copy-start = (bf16[1,704,2048]{2,1,0:T(8,128)(2,1)S(1)}, bf16[1,704,2048]{2,1,0:T(8,128)(2,1)}, u32[]{:S(2)}) copy-start(bf16[1,704,2048]{2,1,0:T(8,128)(2,1)} %param.21) | copy-start | bytes 8650756
  191.4 102.6 %copy-start.2 = (bf16[2048,128]{1,0:T(8,128)(2,1)S(1)}, bf16[2048,128]{1,0:T(8,128)(2,1)}, u32[]{:S(2)}) copy-start(bf16[2048,128]{1,0:T(8,128)(2,1)} %get-tuple-element.11.weight_ref) | copy-start | bytes 1572868
where the time goes:
time: 299 us
  blocking collectives  238 us (80%)
  Pallas kernels  48.1 us (16%)
  waiting for transfers between devices  7 us (2%)
  starting transfers between devices  3.8 us (1%)
    all_to_all x1, blocking collectives, local(): lax.all_to_all(send.reshape(owners, SLOTS, D), ('ctx', 'exp'), split_axis...  105 us
    all_to_all x1, blocking collectives, local(): lax.all_to_all(results.reshape(owners, SLOTS, D), ('ctx', 'exp'), split_a...  103 us
    all_to_all x1, blocking collectives, local(): lax.all_to_all(packed, 'ctx', split_axis=0, concat_axis=0, tiled=True)  30.3 us
    pallas_call x1, Pallas kernels, local(): pl.pallas_call(expert_kernel, grid=(owners * SLOTS // block,), out_shape=...  25.6 us
    pallas_call x1, Pallas kernels, local(): pl.pallas_call(project_kernel, grid=(K_STEPS,), out_shape=(shape((ROWS, D...  7.71 us
    all_to_all x1, waiting for transfers between devices, local(): lax.all_to_all(attended, 'ctx', split_axis=0, concat_axis=0, tiled=True)  7 us
  transfers between devices with their start and end apart: 1, of which 1 were waited for; matrix products, arithmetic and copies ran while one was open for 0% of the time, Pallas kernels for 1%

commit v1 on v0

--- a/solution.py
+++ b/solution.py
@@ -1,8 +1,11 @@
+import math
+
 import jax
 import jax.numpy as jnp
 from jax import lax
 from jax.experimental import pallas as pl
 from jax.experimental.pallas import tpu as pltpu
+from jax.sharding import Mesh
 from jax.sharding import PartitionSpec as P
 
 D = 2048
@@ -17,11 +20,41 @@
 SEG_ROWS = 16
 PACK_ROWS = 3 * ROWS + SEG_ROWS
 Q_BLOCK = 256
+X_BLOCK = 512
 NEG_FILL = -1e30
 
 VMEM = pl.BlockSpec(memory_space=pltpu.VMEM)
 f32 = jnp.float32
 bf16 = jnp.bfloat16
+
+
+SIZES = (4, 2, 2, 4, 2)
+AXES = ("z", "yl", "c", "x", "yh")
+POSITIONS = ("z", "yl", "c")
+STREAM = ("x", "yh")
+PLACES = ("z", "yl", "x", "yh")
+
+
+def moves(target):
+    pairs = []
+    for number in range(math.prod(SIZES)):
+        rest, spot = number, []
+        for size in reversed(SIZES):
+            spot.append(rest % size)
+            rest //= size
+        goal = 0
+        for size, value in zip(SIZES, target(*reversed(spot))):
+            goal = goal * size + value
+        pairs.append((number, goal))
+    return pairs
+
+
+def weight_target(z, yl, c, x, yh):
+    return (z, 1 - yl, yh, x, c)
+
+
+def core_target(z, yl, c, x, yh):
+    return (z, yl, 1 - c, x, yh)
 
 
 def params(mib):
@@ -67,12 +100,16 @@
         out_ref[start:high] = (mixed / total).astype(bf16).reshape(per, ROWS, HEAD_DIM)
 
 
+def place_of(expert):
+    return (expert & 48) | (8 - (expert & 8)) | ((expert & 3) << 1) | ((expert >> 2) & 1)
+
+
 def route_kernel(ids_ref, codes_ref, pick_ref, weight_ref):
     expert = lax.broadcasted_iota(jnp.int32, (EXPERTS, ROWS), 0)
     member = jnp.zeros((EXPERTS, ROWS), f32)
     code = jnp.zeros((EXPERTS, ROWS), f32)
     for k in range(TOPK):
-        named = expert == ids_ref[k : k + 1, :]
+        named = expert == place_of(ids_ref[k : k + 1, :])
         member = member + jnp.where(named, 1.0, 0.0)
         code = code + jnp.where(named, codes_ref[k : k + 1, :].astype(f32), 0.0)
     earlier = lax.broadcasted_iota(jnp.int32, (ROWS, ROWS), 0) < lax.broadcasted_iota(
@@ -81,21 +118,16 @@
     rank = jnp.dot(
         member.astype(bf16), jnp.where(earlier, 1.0, 0.0).astype(bf16), preferred_element_type=f32
     )
-    place = (member * (rank + 1.0)).astype(bf16)
-
-    def spread(table, count):
-        rows = EXPERTS * count
-        own = lax.broadcasted_iota(jnp.int32, (rows, EXPERTS), 0) // count
-        mine = own == lax.broadcasted_iota(jnp.int32, (rows, EXPERTS), 1)
-        return jnp.dot(jnp.where(mine, 1.0, 0.0).astype(bf16), table, preferred_element_type=f32)
-
-    def slot(rows):
-        return ((lax.broadcasted_iota(jnp.int32, (rows, ROWS), 0) & (SLOTS - 1)) + 1).astype(f32)
-
-    here = spread(place, SLOTS) == slot(EXPERTS * SLOTS)
+    rows = EXPERTS * SLOTS
+    own = lax.broadcasted_iota(jnp.int32, (rows, EXPERTS), 0) // SLOTS
+    mine = own == lax.broadcasted_iota(jnp.int32, (rows, EXPERTS), 1)
+    mine = jnp.where(mine, 1.0, 0.0).astype(bf16)
+    place = jnp.dot(mine, (member * (rank + 1.0)).astype(bf16), preferred_element_type=f32)
+    codes = jnp.dot(mine, code.astype(bf16), preferred_element_type=f32)
+    slot = (lax.broadcasted_iota(jnp.int32, (rows, ROWS), 0) & (SLOTS - 1)) + 1
+    here = place == slot.astype(f32)
     pick_ref[...] = jnp.where(here, 1.0, 0.0).astype(bf16)
-    both = spread(place, 2 * SLOTS) == slot(EXPERTS * 2 * SLOTS)
-    weight_ref[...] = jnp.where(both, spread(code.astype(bf16), 2 * SLOTS), 0.0).astype(bf16)
+    weight_ref[...] = jnp.where(here, codes, 0.0).astype(bf16)
 
 
 K_STEPS = 4
@@ -129,24 +161,44 @@
             span = slice(chunk * count * SLOTS, (chunk + 1) * count * SLOTS)
             picked = jnp.dot(pick_ref[span, :], normed, preferred_element_type=f32)
             rows[chunk] = picked.astype(bf16).reshape(count, SLOTS, D)
-            for half in range(2):
-                copy = pltpu.make_async_copy(
-                    rows.at[chunk],
-                    send_ref.at[pl.ds(chunk * count, count), half],
-                    sems.at[chunk, half],
-                )
-                copy.start()
-                copies.append(copy)
+            copy = pltpu.make_async_copy(
+                rows.at[chunk], send_ref.at[pl.ds(chunk * count, count)], sems.at[chunk]
+            )
+            copy.start()
+            copies.append(copy)
         for copy in copies:
             copy.wait()
 
 
-def expert_kernel(x_ref, in_ref, down_ref, out_ref):
-    inner = jnp.dot(x_ref[...], in_ref[...], preferred_element_type=f32)
-    gate = inner[:, :HALF]
-    up = pltpu.roll(inner, HALF, axis=1)[:, :HALF]
-    act = (gate / (1.0 + jnp.exp(-gate)) * up).astype(bf16)
-    out_ref[...] = jnp.dot(act, down_ref[...], preferred_element_type=f32).astype(bf16)
+def expert_kernel(x_any, in_a, in_b, down_a, down_b, out_any, x, w_in, w_down, act, out, sems, out_sems):
+    blocks = x.shape[0]
+    copies = [pltpu.make_async_copy(x_any, x, sems.at[0])]
+    for half, (source, down) in enumerate(((in_a, down_a), (in_b, down_b))):
+        copies.append(pltpu.make_async_copy(source, w_in.at[half], sems.at[1 + half]))
+    for half, down in enumerate((down_a, down_b)):
+        copies.append(pltpu.make_async_copy(down, w_down.at[half], sems.at[3 + half]))
+    for copy in copies:
+        copy.start()
+    copies[0].wait()
+    for half in range(2):
+        copies[1 + half].wait()
+        for block in range(blocks):
+            inner = jnp.dot(x[block], w_in[half], preferred_element_type=f32)
+            gate = inner[:, :HALF]
+            up = pltpu.roll(inner, HALF, axis=1)[:, :HALF]
+            act[half, block] = (gate / (1.0 + jnp.exp(-gate)) * up).astype(bf16)
+    copies[3].wait()
+    copies[4].wait()
+    sends = []
+    for block in range(blocks):
+        total = jnp.dot(act[0, block], w_down[0], preferred_element_type=f32)
+        total = total + jnp.dot(act[1, block], w_down[1], preferred_element_type=f32)
+        out[block] = total.astype(bf16)
+        send = pltpu.make_async_copy(out.at[block], out_any.at[block], out_sems.at[block])
+        send.start()
+        sends.append(send)
+    for send in sends:
+        send.wait()
 
 
 def combine_kernel(rows_ref, weight_ref, mixed_ref, out_ref, acc, total):
@@ -169,7 +221,7 @@
 
     @pl.when(step == pl.num_programs(0) - 1)
     def _():
-        routed = acc[...] / (total[:, 0:1] * 0.5)
+        routed = acc[...] / total[:, 0:1]
         out_ref[...] = (mixed_ref[...].astype(f32) + routed).astype(bf16)
 
 
@@ -186,8 +238,11 @@
     w_in,
     w_down,
 ):
-    owners = 2 * EXPERTS
     shape = jax.ShapeDtypeStruct
+    moved_in = lax.ppermute(w_in[0], AXES, moves(weight_target))
+    moved_down = lax.ppermute(w_down[0], AXES, moves(weight_target))
+    other_in = lax.ppermute(moved_in, AXES, moves(core_target))
+    other_down = lax.ppermute(moved_down, AXES, moves(core_target))
     packed = pl.pallas_call(
         pack_kernel,
         out_shape=shape((HEADS, PACK_ROWS, HEAD_DIM), bf16),
@@ -195,7 +250,7 @@
         out_specs=VMEM,
         name="pack",
     )(queries[0], keys[0], values[0], segment_ids)
-    swapped = lax.all_to_all(packed, "ctx", split_axis=0, concat_axis=0, tiled=True)
+    swapped = lax.all_to_all(packed, POSITIONS, split_axis=0, concat_axis=0, tiled=True)
     attended = pl.pallas_call(
         attend_kernel,
         out_shape=shape((HEADS, ROWS, HEAD_DIM), bf16),
@@ -204,12 +259,12 @@
         compiler_params=params(40),
         name="attend",
     )(swapped)
-    heads = lax.all_to_all(attended, "ctx", split_axis=0, concat_axis=0, tiled=True)
+    heads = lax.all_to_all(attended, POSITIONS, split_axis=0, concat_axis=0, tiled=True)
     pick, weight = pl.pallas_call(
         route_kernel,
         out_shape=(
             shape((EXPERTS * SLOTS, ROWS), bf16),
-            shape((owners * SLOTS, ROWS), bf16),
+            shape((EXPERTS * SLOTS, ROWS), bf16),
         ),
         in_specs=[VMEM] * 2,
         out_specs=(VMEM, VMEM),
@@ -221,7 +276,7 @@
         grid=(K_STEPS,),
         out_shape=(
             shape((ROWS, D), bf16),
-            shape((EXPERTS, 2, SLOTS, D), bf16),
+            shape((EXPERTS, SLOTS, D), bf16),
         ),
         in_specs=[
             pl.BlockSpec((per, ROWS, HEAD_DIM), lambda i: (i, 0, 0)),
@@ -232,39 +287,43 @@
         ],
         out_specs=(
             pl.BlockSpec((ROWS, D), lambda i: (0, 0)),
-            pl.BlockSpec(memory_space=pl.ANY),
+            pl.BlockSpec(memory_space=pltpu.HBM),
         ),
         scratch_shapes=[
             pltpu.VMEM((ROWS, D), f32),
             pltpu.VMEM((SEND_STEPS, EXPERTS // SEND_STEPS, SLOTS, D), bf16),
-            pltpu.SemaphoreType.DMA((SEND_STEPS, 2)),
+            pltpu.SemaphoreType.DMA((SEND_STEPS,)),
         ],
         compiler_params=params(40),
         name="project",
     )(heads, out_weight, hidden_in[0], norm_gain[None], pick)
-    arrived = lax.all_to_all(
-        send.reshape(owners, SLOTS, D), ("ctx", "exp"), split_axis=0, concat_axis=0, tiled=True
+    arrived = lax.all_to_all(send, PLACES, split_axis=0, concat_axis=0, tiled=True)
+    blocks = EXPERTS * SLOTS // X_BLOCK
+    anywhere = pl.BlockSpec(memory_space=pl.ANY)
+    results = pl.pallas_call(
+        expert_kernel,
+        out_shape=shape((blocks, X_BLOCK, D), bf16),
+        in_specs=[anywhere] * 5,
+        out_specs=anywhere,
+        scratch_shapes=[
+            pltpu.VMEM((blocks, X_BLOCK, D), bf16),
+            pltpu.VMEM((2, D, 2 * HALF), bf16),
+            pltpu.VMEM((2, HALF, D), bf16),
+            pltpu.VMEM((2, blocks, X_BLOCK, HALF), bf16),
+            pltpu.VMEM((blocks, X_BLOCK, D), bf16),
+            pltpu.SemaphoreType.DMA((5,)),
+            pltpu.SemaphoreType.DMA((blocks,)),
+        ],
+        compiler_params=params(56),
+        name="experts",
+    )(arrived.reshape(blocks, X_BLOCK, D), moved_in, other_in, moved_down, other_down)
+    returned = lax.all_to_all(
+        results.reshape(EXPERTS, SLOTS, D), PLACES, split_axis=0, concat_axis=0, tiled=True
     )
     block = 256
-    results = pl.pallas_call(
-        expert_kernel,
-        grid=(owners * SLOTS // block,),
-        out_shape=shape((owners * SLOTS, D), bf16),
-        in_specs=[
-            pl.BlockSpec((block, D), lambda i: (i, 0)),
-            pl.BlockSpec((D, 2 * HALF), lambda i: (0, 0), pipeline_mode=pl.Buffered(1)),
-            pl.BlockSpec((HALF, D), lambda i: (0, 0), pipeline_mode=pl.Buffered(1)),
-        ],
-        out_specs=pl.BlockSpec((block, D), lambda i: (i, 0)),
-        compiler_params=params(48),
-        name="experts",
-    )(arrived.reshape(owners * SLOTS, D), w_in[0], w_down[0])
-    returned = lax.all_to_all(
-        results.reshape(owners, SLOTS, D), ("ctx", "exp"), split_axis=0, concat_axis=0, tiled=True
-    )
     layer_out = pl.pallas_call(
         combine_kernel,
-        grid=(owners * SLOTS // block,),
+        grid=(EXPERTS * SLOTS // block,),
         out_shape=shape((ROWS, D), bf16),
         in_specs=[
             pl.BlockSpec((block, D), lambda i: (i, 0)),
@@ -275,24 +334,13 @@
         scratch_shapes=[pltpu.VMEM((ROWS, D), f32), pltpu.VMEM((ROWS, ROWS), f32)],
         compiler_params=params(40),
         name="combine",
-    )(returned.reshape(owners * SLOTS, D), weight, mixed)
+    )(returned.reshape(EXPERTS * SLOTS, D), weight, mixed)
     return layer_out[None]
 
 
 def solution(mesh):
-    placed = (
-        P("exp", "ctx", None),
-        P("exp", "ctx", None),
-        P("exp", "ctx", None),
-        P("exp", "ctx"),
-        P("exp", "ctx", None),
-        P(),
-        P(),
-        P("exp", "ctx", None),
-        P("exp", "ctx", None),
-        P(("ctx", "exp"), None, None),
-        P(("ctx", "exp"), None, None),
-    )
-    return jax.shard_map(
-        local, mesh=mesh, in_specs=placed, out_specs=P("exp", "ctx", None), check_vma=False
-    )
+    parts = Mesh(mesh.devices.reshape(SIZES), AXES)
+    rows = P(STREAM, POSITIONS, None)
+    owned = P((*POSITIONS, *STREAM), None, None)
+    placed = (rows, rows, rows, P(STREAM, POSITIONS), rows, P(), P(), rows, rows, owned, owned)
+    return jax.shard_map(local, mesh=parts, in_specs=placed, out_specs=rows, check_vma=False)

time: 299 us -> 286 us (0.957)
  blocking collectives: 238 us -> 60.3 us
  waiting for transfers between devices: 7 us -> 137 us
  starting transfers between devices: 3.8 us -> 36.1 us
  local copies, waits for them, and re-layouts: 1.57 us -> 6.91 us
  Pallas kernels: 48.1 us -> 43.1 us
    all_to_all x3 -> x1, blocking collectives: 238 us -> 60.3 us  [local(): lax.all_to_all(results.reshape(EXPERTS, SLOTS, D), PLACES, split_axis=0,...]
    all_to_all x1 -> x3, waiting for transfers between devices: 7 us -> 78.6 us  [the longest x1 46.6 us: local(): lax.all_to_all(send, PLACES, split_axis=0, concat_axis=0, tiled=True)]
    ppermute x0 -> x4, waiting for transfers between devices: none -> 58.8 us  [the longest x1 53.6 us: local(): moved_in = lax.ppermute(w_in[0], AXES, moves(weight_target))]
    all_to_all x1 -> x3, starting transfers between devices: 3.8 us -> 20.8 us  [the longest x1 7.98 us: local(): lax.all_to_all(send, PLACES, split_axis=0, concat_axis=0, tiled=True)]
    ppermute x0 -> x4, starting transfers between devices: none -> 15.4 us  [the longest x1 8.36 us: local(): other_in = lax.ppermute(moved_in, AXES, moves(core_target))]
    unnamed x14 -> x16, local copies, waits for them, and re-layouts: 0.98 us -> 6.31 us
    pallas_call x1, Pallas kernels: 7.71 us -> 4.44 us  [local(): pl.pallas_call(project_kernel, grid=(K_STEPS,), out_shape=(shape((ROWS, D...]
  transfers between devices with their start and end apart: 1 -> 7, of which waited for: 1 -> 5; matrix products, arithmetic and copies ran while one was open for 0% -> 0% of each run, Pallas kernels for 1% -> 5%
where the time goes in v1:
time: 286 us; the launch traced here: 284 us
  waiting for transfers between devices  137 us (48%)
  blocking collectives  60.3 us (21%)
  Pallas kernels  43.1 us (15%)
  starting transfers between devices  36.1 us (13%)
  local copies, waits for them, and re-layouts  6.91 us (2%)
    all_to_all x1, blocking collectives, local(): lax.all_to_all(results.reshape(EXPERTS, SLOTS, D), PLACES, split_axis=0,...  60.3 us
    ppermute x1, waiting for transfers between devices, local(): moved_in = lax.ppermute(w_in[0], AXES, moves(weight_target))  53.6 us
    all_to_all x1, waiting for transfers between devices, local(): lax.all_to_all(send, PLACES, split_axis=0, concat_axis=0, tiled=True)  46.6 us
    pallas_call x1, Pallas kernels, local(): pl.pallas_call(expert_kernel, out_shape=shape((blocks, X_BLOCK, D), bf16)...  25.9 us
    all_to_all x1, waiting for transfers between devices, local(): lax.all_to_all(attended, POSITIONS, split_axis=0, concat_axis=0, tiled=True)  23.8 us
    ppermute x1, starting transfers between devices, local(): other_in = lax.ppermute(moved_in, AXES, moves(core_target))  8.36 us
    all_to_all x1, waiting for transfers between devices, local(): lax.all_to_all(packed, POSITIONS, split_axis=0, concat_axis=0, tiled=True)  8.28 us
    all_to_all x1, starting transfers between devices, local(): lax.all_to_all(send, PLACES, split_axis=0, concat_axis=0, tiled=True)  7.98 us
  transfers between devices with their start and end apart: 7, of which 5 were waited for; matrix products, arithmetic and copies ran while one was open for 0% of the time, Pallas kernels for 5%

profile of v1, /device:TPU:1, one launch (start us, length us, event | category | flops | bytes accessed | tf_op | source)
XLA Modules:
  0.0 283.9 jit_solution(15446141075720824831)
XLA Ops:
  0.0 4.1 %collective-permute-start = (bf16[2048,1408]{1,0:T(8,128)(2,1)}, bf16[2048,1408]{1,0:T(8,128)(2,1)}, u32[]{:S(2)}, u32[]{:S(2)}) collective-permute-start(bf16[2048,1408]{1,0:T(8,128)(2,1)} %bitcast.26), channel_id=1, source_target_pairs={{0,16},{1,24},{2,18},{3,26},{4,20},{5,28},{6,22},{7,30},{8,17},{9,... | collective-permute-start | bytes 17301512 | tf_op jit(solution)/shard_map/ppermute | solution.py:242
  4.1 3.0 %pack.1 = bf16[16,400,128]{2,1,0:T(8,128)(2,1)} custom-call(bf16[128,2048]{1,0:T(8,128)(2,1)} %bitcast.23, bf16[128,2048]{1,0:T(8,128)(2,1)} %bitcast.24, bf16[128,2048]{1,0:T(8,128)(2,1)} %bitcast.25, s32[1,128]{1,0:T(1,128)} %seg_ref.1), custom_call_target="tpu_custom_call" | custom-call | tf_op jit(solution)/shard_map/pack/pallas_call | solution.py:246
  7.1 5.4 %all-to-all-start = ((bf16[16,400,128]{2,1,0:T(8,128)(2,1)}), bf16[16,400,128]{2,1,0:T(8,128)(2,1)S(1)}, u32[]{:S(2)}, u32[]{:S(2)}) async-start(bf16[16,400,128]{2,1,0:T(8,128)(2,1)} %pack.1), calls=%async_computation | async-start | bytes 3276800 | tf_op jit(solution)/shard_map/all_to_all | solution.py:253
  12.5 1.4 collective-permute-start.2
  13.9 53.6 %collective-permute-done.in_a = bf16[2048,1408]{1,0:T(8,128)(2,1)} collective-permute-done((bf16[2048,1408]{1,0:T(8,128)(2,1)}, bf16[2048,1408]{1,0:T(8,128)(2,1)}, u32[]{:S(2)}, u32[]{:S(2)}) %collective-permute-start) | collective-permute-done | bytes 5767200 | tf_op jit(solution)/shard_map/ppermute | solution.py:242
  67.5 8.4 %collective-permute-start.1 = (bf16[2048,1408]{1,0:T(8,128)(2,1)}, bf16[2048,1408]{1,0:T(8,128)(2,1)}, u32[]{:S(2)}, u32[]{:S(2)}) collective-permute-start(bf16[2048,1408]{1,0:T(8,128)(2,1)} %collective-permute-done.in_a), channel_id=1, source_target_pairs={{0,8},{1,9},{2,10},{3,11},{4,12},{5,13},{6,14},{7,15},{8,0},{9,1},... | collective-permute-start | bytes 17301512 | tf_op jit(solution)/shard_map/ppermute | solution.py:244
  75.8 8.3 %all-to-all-done.x_ref = bf16[16,400,128]{2,1,0:T(8,128)(2,1)S(1)} async-done(((bf16[16,400,128]{2,1,0:T(8,128)(2,1)}), bf16[16,400,128]{2,1,0:T(8,128)(2,1)S(1)}, u32[]{:S(2)}, u32[]{:S(2)}) %all-to-all-start) | async-done | bytes 1638432 | tf_op jit(solution)/shard_map/all_to_all | solution.py:253
  84.1 5.1 %attend.1 = bf16[16,128,128]{2,1,0:T(8,128)(2,1)} custom-call(bf16[16,400,128]{2,1,0:T(8,128)(2,1)S(1)} %all-to-all-done.x_ref), custom_call_target="tpu_custom_call" | custom-call | tf_op jit(solution)/shard_map/attend/pallas_call | solution.py:254
  89.2 7.3 %all-to-all-start.1 = ((bf16[16,128,128]{2,1,0:T(8,128)(2,1)}), bf16[16,128,128]{2,1,0:T(8,128)(2,1)S(1)}, u32[]{:S(2)}, u32[]{:S(2)}) async-start(bf16[16,128,128]{2,1,0:T(8,128)(2,1)} %attend.1), calls=%async_computation.1 | async-start | bytes 1048576 | tf_op jit(solution)/shard_map/all_to_all | solution.py:262
  96.6 0.0 copy-done.6
  96.6 0.0 copy-done.7
  96.6 0.6 copy_bitcast_fusion
  97.2 1.9 route.1
  99.1 23.8 %all-to-all-done.1.heads_ref = bf16[16,128,128]{2,1,0:T(8,128)(2,1)S(1)} async-done(((bf16[16,128,128]{2,1,0:T(8,128)(2,1)}), bf16[16,128,128]{2,1,0:T(8,128)(2,1)S(1)}, u32[]{:S(2)}, u32[]{:S(2)}) %all-to-all-start.1) | async-done | bytes 524320 | tf_op jit(solution)/shard_map/all_to_all | solution.py:262
  122.9 0.0 copy-done.2
  122.9 0.0 copy-done.5
  122.9 3.4 %copy-done = bf16[2048,2048]{1,0:T(8,128)(2,1)S(1)} copy-done((bf16[2048,2048]{1,0:T(8,128)(2,1)S(1)}, bf16[2048,2048]{1,0:T(8,128)(2,1)}, u32[]{:S(2)}) %copy-start) | copy-done | bytes 8388632
  126.3 0.9 copy-done.3
  127.2 4.4 %project.1 = (bf16[128,2048]{1,0:T(8,128)(2,1)S(1)}, bf16[64,16,2048]{2,1,0:T(8,128)(2,1)S(1)}) custom-call(bf16[16,128,128]{2,1,0:T(8,128)(2,1)S(1)} %all-to-all-done.1.heads_ref, bf16[2048,2048]{1,0:T(8,128)(2,1)S(1)} %copy-done, bf16[128,2048]{1,0:T(8,128)(2,1)S(1)} %bitcast.20, f32[1,2048]{1,0:T(1,128)S(1)} %bitcast.21, bf16[1024,128]{1,0:T(8,128)(2,1)S(1)} %copy-done.3), custom_call_target="tpu_custom_call" | custom-call | tf_op jit(solution)/shard_map/project/pallas_call | solution.py:274
  131.7 0.0 copy-start.1
  131.7 2.0 copy-done.1
  133.6 8.0 %all-to-all-start.2 = ((bf16[64,16,2048]{2,1,0:T(8,128)(2,1)}), bf16[64,16,2048]{2,1,0:T(8,128)(2,1)}, u32[]{:S(2)}, u32[]{:S(2)}) async-start(bf16[64,16,2048]{2,1,0:T(8,128)(2,1)} %copy-done.1), calls=%async_computation.2 | async-start | bytes 8388608 | tf_op jit(solution)/shard_map/all_to_all | solution.py:300
  141.6 0.0 collective-permute-done.2.down_a
  141.6 1.5 collective-permute-start.3
  143.1 5.3 %collective-permute-done.3.down_b = bf16[704,2048]{1,0:T(8,128)(2,1)} collective-permute-done((bf16[704,2048]{1,0:T(8,128)(2,1)}, bf16[704,2048]{1,0:T(8,128)(2,1)}, u32[]{:S(2)}, u32[]{:S(2)}) %collective-permute-start.3) | collective-permute-done | bytes 2883616 | tf_op jit(solution)/shard_map/ppermute | solution.py:245
  148.4 46.6 %all-to-all-done.2 = bf16[64,16,2048]{2,1,0:T(8,128)(2,1)} async-done(((bf16[64,16,2048]{2,1,0:T(8,128)(2,1)}), bf16[64,16,2048]{2,1,0:T(8,128)(2,1)}, u32[]{:S(2)}, u32[]{:S(2)}) %all-to-all-start.2) | async-done | bytes 4194336 | tf_op jit(solution)/shard_map/all_to_all | solution.py:300
  195.0 0.0 collective-permute-done.1.in_b
  195.0 25.9 %experts.1 = bf16[2,512,2048]{2,1,0:T(8,128)(2,1)} custom-call(bf16[2,512,2048]{2,1,0:T(8,128)(2,1)} %bitcast.7.x_any, bf16[2048,1408]{1,0:T(8,128)(2,1)} %collective-permute-done.in_a, bf16[2048,1408]{1,0:T(8,128)(2,1)} %collective-permute-done.1.in_b, bf16[704,2048]{1,0:T(8,128)(2,1)} %collective-permute-done.2.down_a, ...), custom_call_target="tpu_custom_call" | custom-call | tf_op jit(solution)/shard_map/experts/pallas_call | solution.py:303
  220.8 0.0 copy-start.4
  220.8 60.3 %all_to_all.20 = bf16[64,16,2048]{2,1,0:T(8,128)(2,1)S(1)} all-to-all(bf16[64,16,2048]{2,1,0:T(8,128)(2,1)} %bitcast.22), channel_id=1, replica_groups=mesh['z'=4,'yl'=2,'c'=2,'x'=4,'yh'=2] {'z','yl','x','yh'}, dimensions={0} | all-to-all | bytes 8388608 | tf_op jit(solution)/shard_map/all_to_all | solution.py:320
  281.1 0.0 copy-done.4
  281.1 2.8 combine.1
  (6 shorter events, 0.0 us)
Async XLA Ops:
  0.0 67.5 %collective-permute-start = (bf16[2048,1408]{1,0:T(8,128)(2,1)}, bf16[2048,1408]{1,0:T(8,128)(2,1)}, u32[]{:S(2)}, u32[]{:S(2)}) collective-permute-start(bf16[2048,1408]{1,0:T(8,128)(2,1)} %bitcast.26), channel_id=1, source_target_pairs={{0,16},{1,24},{2,18},{3,26},{4,20},{5,28},{6,22},{7,30},{8,17},{9,... | collective-permute-start | bytes 17301512 | tf_op jit(solution)/shard_map/ppermute | solution.py:242
  4.1 92.5 %copy-start.6 = (s32[1,128,6]{1,0,2:T(1,128)S(1)}, s32[1,128,6]{1,0,2:T(1,128)}, u32[]{:S(2)}) copy-start(s32[1,128,6]{1,0,2:T(1,128)} %param.19) | copy-start | bytes 9220
  4.1 92.5 %copy-start.7 = (s32[1,128,6]{1,0,2:T(1,128)S(1)}, s32[1,128,6]{1,0,2:T(1,128)}, u32[]{:S(2)}) copy-start(s32[1,128,6]{1,0,2:T(1,128)} %param.18) | copy-start | bytes 9220
  4.1 118.8 %copy-start.2 = (bf16[1,128,2048]{2,1,0:T(8,128)(2,1)S(1)}, bf16[1,128,2048]{2,1,0:T(8,128)(2,1)}, u32[]{:S(2)}) copy-start(bf16[1,128,2048]{2,1,0:T(8,128)(2,1)} %param.15) | copy-start | bytes 1572868
  4.1 118.8 %copy-start.5 = (f32[2048]{0:T(1024)S(1)}, f32[2048]{0:T(1024)}, u32[]{:S(2)}) copy-start(f32[2048]{0:T(1024)} %param.17) | copy-start | bytes 24580
  7.1 77.0 %all-to-all-start = ((bf16[16,400,128]{2,1,0:T(8,128)(2,1)}), bf16[16,400,128]{2,1,0:T(8,128)(2,1)S(1)}, u32[]{:S(2)}, u32[]{:S(2)}) async-start(bf16[16,400,128]{2,1,0:T(8,128)(2,1)} %pack.1), calls=%async_computation | async-start | bytes 3276800 | tf_op jit(solution)/shard_map/all_to_all | solution.py:253
  12.5 129.1 %collective-permute-start.2 = (bf16[704,2048]{1,0:T(8,128)(2,1)}, bf16[704,2048]{1,0:T(8,128)(2,1)}, u32[]{:S(2)}, u32[]{:S(2)}) collective-permute-start(bf16[704,2048]{1,0:T(8,128)(2,1)} %bitcast.27), channel_id=1, source_target_pairs={{0,16},{1,24},{2,18},{3,26},{4,20},{5,28},{6,22},{7,30},{8,17},{9,... | collective-permute-start | bytes 8650760 | tf_op jit(solution)/shard_map/ppermute | solution.py:243
  67.5 127.5 %collective-permute-start.1 = (bf16[2048,1408]{1,0:T(8,128)(2,1)}, bf16[2048,1408]{1,0:T(8,128)(2,1)}, u32[]{:S(2)}, u32[]{:S(2)}) collective-permute-start(bf16[2048,1408]{1,0:T(8,128)(2,1)} %collective-permute-done.in_a), channel_id=1, source_target_pairs={{0,8},{1,9},{2,10},{3,11},{4,12},{5,13},{6,14},{7,15},{8,0},{9,1},... | collective-permute-start | bytes 17301512 | tf_op jit(solution)/shard_map/ppermute | solution.py:244
  89.2 33.6 %all-to-all-start.1 = ((bf16[16,128,128]{2,1,0:T(8,128)(2,1)}), bf16[16,128,128]{2,1,0:T(8,128)(2,1)S(1)}, u32[]{:S(2)}, u32[]{:S(2)}) async-start(bf16[16,128,128]{2,1,0:T(8,128)(2,1)} %attend.1), calls=%async_computation.1 | async-start | bytes 1048576 | tf_op jit(solution)/shard_map/all_to_all | solution.py:262
  122.9 3.4 %copy-start = (bf16[2048,2048]{1,0:T(8,128)(2,1)S(1)}, bf16[2048,2048]{1,0:T(8,128)(2,1)}, u32[]{:S(2)}) copy-start(bf16[2048,2048]{1,0:T(8,128)(2,1)} %weight_ref.1) | copy-start | bytes 25165828
  126.3 0.9 copy-start.3
  131.7 2.0 copy-start.1
  133.6 61.3 %all-to-all-start.2 = ((bf16[64,16,2048]{2,1,0:T(8,128)(2,1)}), bf16[64,16,2048]{2,1,0:T(8,128)(2,1)}, u32[]{:S(2)}, u32[]{:S(2)}) async-start(bf16[64,16,2048]{2,1,0:T(8,128)(2,1)} %copy-done.1), calls=%async_computation.2 | async-start | bytes 8388608 | tf_op jit(solution)/shard_map/all_to_all | solution.py:300
  141.6 6.8 %collective-permute-start.3 = (bf16[704,2048]{1,0:T(8,128)(2,1)}, bf16[704,2048]{1,0:T(8,128)(2,1)}, u32[]{:S(2)}, u32[]{:S(2)}) collective-permute-start(bf16[704,2048]{1,0:T(8,128)(2,1)} %collective-permute-done.2.down_a), channel_id=1, source_target_pairs={{0,8},{1,9},{2,10},{3,11},{4,12},{5,13},{6,14},{7,15},{8,0},{9,1},... | collective-permute-start | bytes 8650760 | tf_op jit(solution)/shard_map/ppermute | solution.py:245
  220.8 60.3 %copy-start.4 = (bf16[1024,128]{1,0:T(8,128)(2,1)S(1)}, bf16[1024,128]{1,0:T(8,128)(2,1)}, u32[]{:S(2)}) copy-start(bf16[1024,128]{1,0:T(8,128)(2,1)} %get-tuple-element.11.weight_ref) | copy-start | bytes 786436

commit v2 on v1

--- a/solution.py
+++ b/solution.py
@@ -21,6 +21,7 @@
 PACK_ROWS = 3 * ROWS + SEG_ROWS
 Q_BLOCK = 256
 X_BLOCK = 512
+PIECES = (256, 384, 448, 960)
 NEG_FILL = -1e30
 
 VMEM = pl.BlockSpec(memory_space=pltpu.VMEM)
@@ -170,27 +171,42 @@
             copy.wait()
 
 
-def expert_kernel(x_any, in_a, in_b, down_a, down_b, out_any, x, w_in, w_down, act, out, sems, out_sems):
-    blocks = x.shape[0]
-    copies = [pltpu.make_async_copy(x_any, x, sems.at[0])]
-    for half, (source, down) in enumerate(((in_a, down_a), (in_b, down_b))):
-        copies.append(pltpu.make_async_copy(source, w_in.at[half], sems.at[1 + half]))
-    for half, down in enumerate((down_a, down_b)):
-        copies.append(pltpu.make_async_copy(down, w_down.at[half], sems.at[3 + half]))
+def inner_kernel(*refs):
+    pieces = len(PIECES)
+    x_any, first, second = refs[0], refs[1 : 1 + pieces], refs[1 + pieces : 1 + 2 * pieces]
+    act, x, w_in, sems = refs[1 + 2 * pieces :]
+    load = pltpu.make_async_copy(x_any, x, sems.at[2, 0])
+    load.start()
+    copies = []
+    for half, parts in enumerate((first, second)):
+        start = 0
+        for number, (part, count) in enumerate(zip(parts, PIECES)):
+            goal = w_in.at[half, pl.ds(start, count)]
+            copies.append(pltpu.make_async_copy(part, goal, sems.at[half, number]))
+            start += count
     for copy in copies:
         copy.start()
-    copies[0].wait()
+    load.wait()
     for half in range(2):
-        copies[1 + half].wait()
-        for block in range(blocks):
+        for number in range(pieces):
+            copies[half * pieces + number].wait()
+        for block in range(x.shape[0]):
             inner = jnp.dot(x[block], w_in[half], preferred_element_type=f32)
             gate = inner[:, :HALF]
             up = pltpu.roll(inner, HALF, axis=1)[:, :HALF]
             act[half, block] = (gate / (1.0 + jnp.exp(-gate)) * up).astype(bf16)
-    copies[3].wait()
-    copies[4].wait()
+
+
+def down_kernel(act, down_a, down_b, out_any, w_down, out, sems, out_sems):
+    copies = []
+    for half, down in enumerate((down_a, down_b)):
+        copies.append(pltpu.make_async_copy(down, w_down.at[half], sems.at[half]))
+    for copy in copies:
+        copy.start()
+    for copy in copies:
+        copy.wait()
     sends = []
-    for block in range(blocks):
+    for block in range(out.shape[0]):
         total = jnp.dot(act[0, block], w_down[0], preferred_element_type=f32)
         total = total + jnp.dot(act[1, block], w_down[1], preferred_element_type=f32)
         out[block] = total.astype(bf16)
@@ -239,15 +255,20 @@
     w_down,
 ):
     shape = jax.ShapeDtypeStruct
-    moved_in = lax.ppermute(w_in[0], AXES, moves(weight_target))
+    gate_up, start, moved, other = w_in[0], 0, [], []
+    for count in PIECES:
+        piece = lax.slice_in_dim(gate_up, start, start + count)
+        moved.append(lax.ppermute(piece, AXES, moves(weight_target)))
+        other.append(lax.ppermute(moved[-1], AXES, moves(core_target)))
+        start += count
     moved_down = lax.ppermute(w_down[0], AXES, moves(weight_target))
-    other_in = lax.ppermute(moved_in, AXES, moves(core_target))
     other_down = lax.ppermute(moved_down, AXES, moves(core_target))
     packed = pl.pallas_call(
         pack_kernel,
         out_shape=shape((HEADS, PACK_ROWS, HEAD_DIM), bf16),
         in_specs=[VMEM] * 4,
         out_specs=VMEM,
+        compiler_params=params(60),
         name="pack",
     )(queries[0], keys[0], values[0], segment_ids)
     swapped = lax.all_to_all(packed, POSITIONS, split_axis=0, concat_axis=0, tiled=True)
@@ -268,6 +289,7 @@
         ),
         in_specs=[VMEM] * 2,
         out_specs=(VMEM, VMEM),
+        compiler_params=params(60),
         name="route",
     )(expert_ids[0].T, gate_codes[0].T)
     per = HEADS // K_STEPS
@@ -294,29 +316,39 @@
             pltpu.VMEM((SEND_STEPS, EXPERTS // SEND_STEPS, SLOTS, D), bf16),
             pltpu.SemaphoreType.DMA((SEND_STEPS,)),
         ],
-        compiler_params=params(40),
+        compiler_params=params(55),
         name="project",
     )(heads, out_weight, hidden_in[0], norm_gain[None], pick)
     arrived = lax.all_to_all(send, PLACES, split_axis=0, concat_axis=0, tiled=True)
     blocks = EXPERTS * SLOTS // X_BLOCK
     anywhere = pl.BlockSpec(memory_space=pl.ANY)
-    results = pl.pallas_call(
-        expert_kernel,
-        out_shape=shape((blocks, X_BLOCK, D), bf16),
-        in_specs=[anywhere] * 5,
-        out_specs=anywhere,
+    act = pl.pallas_call(
+        inner_kernel,
+        out_shape=shape((2, blocks, X_BLOCK, HALF), bf16),
+        in_specs=[anywhere] * (1 + 2 * len(PIECES)),
+        out_specs=VMEM,
         scratch_shapes=[
             pltpu.VMEM((blocks, X_BLOCK, D), bf16),
             pltpu.VMEM((2, D, 2 * HALF), bf16),
+            pltpu.SemaphoreType.DMA((3, len(PIECES))),
+        ],
+        compiler_params=params(58),
+        name="inner",
+    )(arrived.reshape(blocks, X_BLOCK, D), *moved, *other)
+    results = pl.pallas_call(
+        down_kernel,
+        out_shape=shape((blocks, X_BLOCK, D), bf16),
+        in_specs=[VMEM, anywhere, anywhere],
+        out_specs=anywhere,
+        scratch_shapes=[
             pltpu.VMEM((2, HALF, D), bf16),
-            pltpu.VMEM((2, blocks, X_BLOCK, HALF), bf16),
             pltpu.VMEM((blocks, X_BLOCK, D), bf16),
-            pltpu.SemaphoreType.DMA((5,)),
+            pltpu.SemaphoreType.DMA((2,)),
             pltpu.SemaphoreType.DMA((blocks,)),
         ],
-        compiler_params=params(56),
-        name="experts",
-    )(arrived.reshape(blocks, X_BLOCK, D), moved_in, other_in, moved_down, other_down)
+        compiler_params=params(58),
+        name="down",
+    )(act, moved_down, other_down)
     returned = lax.all_to_all(
         results.reshape(EXPERTS, SLOTS, D), PLACES, split_axis=0, concat_axis=0, tiled=True
     )
@@ -332,7 +364,7 @@
         ],
         out_specs=pl.BlockSpec((ROWS, D), lambda i: (0, 0)),
         scratch_shapes=[pltpu.VMEM((ROWS, D), f32), pltpu.VMEM((ROWS, ROWS), f32)],
-        compiler_params=params(40),
+        compiler_params=params(12),
         name="combine",
     )(returned.reshape(EXPERTS * SLOTS, D), weight, mixed)
     return layer_out[None]

time: 286 us -> 304 us (1.063)
  Pallas kernels: 43.1 us -> 54 us
  local copies, waits for them, and re-layouts: 6.91 us -> 13.8 us
  starting transfers between devices: 36.1 us -> 40.3 us
  waiting for transfers between devices: 137 us -> 133 us
    all_to_all x1, waiting for transfers between devices: 46.6 us -> 0.01 us  [local(): lax.all_to_all(send, PLACES, split_axis=0, concat_axis=0, tiled=True)]
    all_to_all x1, waiting for transfers between devices: 23.8 us -> 53.6 us  [local(): lax.all_to_all(attended, POSITIONS, split_axis=0, concat_axis=0, tiled=True)]
    ppermute x2 -> x8, waiting for transfers between devices: 53.6 us -> 64.1 us  [the longest x4 62.3 us: local(): moved.append(lax.ppermute(piece, AXES, moves(weight_target)))]
    slice x0 -> x4, local copies, waits for them, and re-layouts: none -> 7.33 us  [local(): piece = lax.slice_in_dim(gate_up, start, start + count)]
    all_to_all x1, waiting for transfers between devices: 8.28 us -> 15.5 us  [local(): lax.all_to_all(packed, POSITIONS, split_axis=0, concat_axis=0, tiled=True)]
    pallas_call x1 -> x2, Pallas kernels: 25.9 us -> 32.2 us  [the longest x1 19.4 us: local(): pl.pallas_call(inner_kernel, out_shape=shape((2, blocks, X_BLOCK, HALF),...]
    ppermute x1, waiting for transfers between devices: 5.25 us -> 0.01 us  [local(): other_down = lax.ppermute(moved_down, AXES, moves(core_target))]
    pallas_call x1, Pallas kernels: 4.44 us -> 9.03 us  [local(): pl.pallas_call(project_kernel, grid=(K_STEPS,), out_shape=(shape((ROWS, D...]
  transfers between devices with their start and end apart: 7 -> 13, of which waited for: 5 -> 6; matrix products, arithmetic and copies ran while one was open for 0% -> 3% of each run, Pallas kernels for 5% -> 12%
where the time goes in v2:
time: 304 us; the launch traced here: 303 us
  waiting for transfers between devices  133 us (44%)
  blocking collectives  61.7 us (20%)
  Pallas kernels  54 us (18%)
  starting transfers between devices  40.3 us (13%)
  local copies, waits for them, and re-layouts  13.8 us (5%)
    ppermute x4, waiting for transfers between devices, local(): moved.append(lax.ppermute(piece, AXES, moves(weight_target)))  62.3 us
    all_to_all x1, blocking collectives, local(): lax.all_to_all(results.reshape(EXPERTS, SLOTS, D), PLACES, split_axis=0,...  61.7 us
    all_to_all x1, waiting for transfers between devices, local(): lax.all_to_all(attended, POSITIONS, split_axis=0, concat_axis=0, tiled=True)  53.6 us
    pallas_call x1, Pallas kernels, local(): pl.pallas_call(inner_kernel, out_shape=shape((2, blocks, X_BLOCK, HALF),...  19.4 us
    all_to_all x1, waiting for transfers between devices, local(): lax.all_to_all(packed, POSITIONS, split_axis=0, concat_axis=0, tiled=True)  15.5 us
    pallas_call x1, Pallas kernels, local(): pl.pallas_call(down_kernel, out_shape=shape((blocks, X_BLOCK, D), bf16),...  12.8 us
    ppermute x4, starting transfers between devices, local(): other.append(lax.ppermute(moved[-1], AXES, moves(core_target)))  10.5 us
    pallas_call x1, Pallas kernels, local(): pl.pallas_call(project_kernel, grid=(K_STEPS,), out_shape=(shape((ROWS, D...  9.03 us
  transfers between devices with their start and end apart: 13, of which 6 were waited for; matrix products, arithmetic and copies ran while one was open for 3% of the time, Pallas kernels for 12%

profile of v2, /device:TPU:1, one launch (start us, length us, event | category | flops | bytes accessed | tf_op | source)
XLA Modules:
  0.0 303.1 jit_solution(12496218066986960763)
XLA Ops:
  0.0 2.9 pack.1
  2.9 7.8 %all-to-all-start = ((bf16[16,400,128]{2,1,0:T(8,128)(2,1)}), bf16[16,400,128]{2,1,0:T(8,128)(2,1)S(1)}, u32[]{:S(2)}, u32[]{:S(2)}) async-start(bf16[16,400,128]{2,1,0:T(8,128)(2,1)} %pack.1), calls=%async_computation | async-start | bytes 3276800 | tf_op jit(solution)/shard_map/all_to_all | solution.py:274
  10.7 3.1 %collective-permute-start.8 = (bf16[704,2048]{1,0:T(8,128)(2,1)}, bf16[704,2048]{1,0:T(8,128)(2,1)}, u32[]{:S(2)}, u32[]{:S(2)}) collective-permute-start(bf16[704,2048]{1,0:T(8,128)(2,1)} %bitcast.33), channel_id=1, source_target_pairs={{0,16},{1,24},{2,18},{3,26},{4,20},{5,28},{6,22},{7,30},{8,17},{9,... | collective-permute-start | bytes 8650760 | tf_op jit(solution)/shard_map/ppermute | solution.py:264
  13.8 3.5 %slice_bitcast_fusion = bf16[960,1408]{1,0:T(8,128)(2,1)} fusion(bf16[1,2048,1408]{2,1,0:T(8,128)(2,1)} %param.20), kind=kLoop, calls=%fused_computation | loop fusion | bytes 5406720 | tf_op jit(solution)/shard_map/slice | solution.py:260
  17.3 15.5 %all-to-all-done.x_ref = bf16[16,400,128]{2,1,0:T(8,128)(2,1)S(1)} async-done(((bf16[16,400,128]{2,1,0:T(8,128)(2,1)}), bf16[16,400,128]{2,1,0:T(8,128)(2,1)S(1)}, u32[]{:S(2)}, u32[]{:S(2)}) %all-to-all-start) | async-done | bytes 1638432 | tf_op jit(solution)/shard_map/all_to_all | solution.py:274
  32.7 5.1 %attend.1 = bf16[16,128,128]{2,1,0:T(8,128)(2,1)} custom-call(bf16[16,400,128]{2,1,0:T(8,128)(2,1)S(1)} %all-to-all-done.x_ref), custom_call_target="tpu_custom_call" | custom-call | tf_op jit(solution)/shard_map/attend/pallas_call | solution.py:275
  37.9 4.3 %all-to-all-start.1 = ((bf16[16,128,128]{2,1,0:T(8,128)(2,1)}), bf16[16,128,128]{2,1,0:T(8,128)(2,1)S(1)}, u32[]{:S(2)}, u32[]{:S(2)}) async-start(bf16[16,128,128]{2,1,0:T(8,128)(2,1)} %attend.1), calls=%async_computation.1 | async-start | bytes 1048576 | tf_op jit(solution)/shard_map/all_to_all | solution.py:283
  42.8 1.9 route.1
  44.7 53.6 %all-to-all-done.1.heads_ref = bf16[16,128,128]{2,1,0:T(8,128)(2,1)S(1)} async-done(((bf16[16,128,128]{2,1,0:T(8,128)(2,1)}), bf16[16,128,128]{2,1,0:T(8,128)(2,1)S(1)}, u32[]{:S(2)}, u32[]{:S(2)}) %all-to-all-start.1) | async-done | bytes 524320 | tf_op jit(solution)/shard_map/all_to_all | solution.py:283
  98.4 0.8 copy-done.3
  99.2 9.0 %project.1 = (bf16[128,2048]{1,0:T(8,128)(2,1)}, bf16[64,16,2048]{2,1,0:T(8,128)(2,1)}) custom-call(bf16[16,128,128]{2,1,0:T(8,128)(2,1)} %copy-done.3, bf16[2048,2048]{1,0:T(8,128)(2,1)} %weight_ref.1, bf16[128,2048]{1,0:T(8,128)(2,1)} %bitcast.28, f32[1,2048]{1,0:T(1,128)} %bitcast.32, bf16[1024,128]{1,0:T(8,128)(2,1)} %get-tuple-element.9.pick_ref), custom_call_target="tpu_custom_call" | custom-call | tf_op jit(solution)/shard_map/project/pallas_call | solution.py:296
  108.2 8.6 %all-to-all-start.2 = ((bf16[64,16,2048]{2,1,0:T(8,128)(2,1)}), bf16[64,16,2048]{2,1,0:T(8,128)(2,1)}, u32[]{:S(2)}, u32[]{:S(2)}) async-start(bf16[64,16,2048]{2,1,0:T(8,128)(2,1)} %get-tuple-element.10), calls=%async_computation.2 | async-start | bytes 8388608 | tf_op jit(solution)/shard_map/all_to_all | solution.py:322
  117.6 1.4 slice_bitcast_fusion.1
  119.0 2.8 collective-permute-start.2
  121.8 1.3 slice_bitcast_fusion.2
  123.5 1.2 slice_bitcast_fusion.3
  124.6 2.8 collective-permute-start
  127.4 50.6 %collective-permute-done.2.refs_3_ = bf16[448,1408]{1,0:T(8,128)(2,1)S(1)} collective-permute-done((bf16[448,1408]{1,0:T(8,128)(2,1)S(1)}, bf16[448,1408]{1,0:T(8,128)(2,1)S(1)}, u32[]{:S(2)}, u32[]{:S(2)}) %collective-permute-start.2) | collective-permute-done | bytes 1261600 | tf_op jit(solution)/shard_map/ppermute | solution.py:261
  178.0 1.1 copy-done.4
  179.1 3.3 %collective-permute-start.6 = (bf16[448,1408]{1,0:T(8,128)(2,1)S(1)}, bf16[448,1408]{1,0:T(8,128)(2,1)S(1)}, u32[]{:S(2)}, u32[]{:S(2)}) collective-permute-start(bf16[448,1408]{1,0:T(8,128)(2,1)S(1)} %collective-permute-done.2.refs_3_), channel_id=1, source_target_pairs={{0,8},{1,9},{2,10},{3,11},{4,12},{5,13},{6,14},{7,15},{8,0},{9,1},... | collective-permute-start | bytes 3784712 | tf_op jit(solution)/shard_map/ppermute | solution.py:262
  182.4 7.3 %collective-permute-done.1.refs_2_ = bf16[384,1408]{1,0:T(8,128)(2,1)S(1)} collective-permute-done((bf16[384,1408]{1,0:T(8,128)(2,1)S(1)}, bf16[384,1408]{1,0:T(8,128)(2,1)S(1)}, u32[]{:S(2)}, u32[]{:S(2)}) %collective-permute-start.1) | collective-permute-done | bytes 1081376 | tf_op jit(solution)/shard_map/ppermute | solution.py:261
  189.6 3.3 %collective-permute-start.5 = (bf16[384,1408]{1,0:T(8,128)(2,1)S(1)}, bf16[384,1408]{1,0:T(8,128)(2,1)S(1)}, u32[]{:S(2)}, u32[]{:S(2)}) collective-permute-start(bf16[384,1408]{1,0:T(8,128)(2,1)S(1)} %collective-permute-done.1.refs_2_), channel_id=1, source_target_pairs={{0,8},{1,9},{2,10},{3,11},{4,12},{5,13},{6,14},{7,15},{8,0},{9,1},... | collective-permute-start | bytes 3244040 | tf_op jit(solution)/shard_map/ppermute | solution.py:262
  192.9 4.5 %collective-permute-done.refs_1_ = bf16[256,1408]{1,0:T(8,128)(2,1)S(1)} collective-permute-done((bf16[256,1408]{1,0:T(8,128)(2,1)S(1)}, bf16[256,1408]{1,0:T(8,128)(2,1)S(1)}, u32[]{:S(2)}, u32[]{:S(2)}) %collective-permute-start) | collective-permute-done | bytes 720928 | tf_op jit(solution)/shard_map/ppermute | solution.py:261
  197.3 3.3 %collective-permute-start.4 = (bf16[256,1408]{1,0:T(8,128)(2,1)S(1)}, bf16[256,1408]{1,0:T(8,128)(2,1)S(1)}, u32[]{:S(2)}, u32[]{:S(2)}) collective-permute-start(bf16[256,1408]{1,0:T(8,128)(2,1)S(1)} %collective-permute-done.refs_1_), channel_id=1, source_target_pairs={{0,8},{1,9},{2,10},{3,11},{4,12},{5,13},{6,14},{7,15},{8,0},{9,1},... | collective-permute-start | bytes 2162696 | tf_op jit(solution)/shard_map/ppermute | solution.py:262
  200.6 1.8 collective-permute-done.4.refs_5_
  202.5 0.8 copy-done.9
  203.7 1.1 copy-done.5
  204.7 19.4 %inner.1.act = bf16[2,2,512,704]{3,2,1,0:T(8,128)(2,1)} custom-call(bf16[2,512,2048]{2,1,0:T(8,128)(2,1)} %bitcast.7.refs_0_, bf16[256,1408]{1,0:T(8,128)(2,1)} %copy-done.8, bf16[384,1408]{1,0:T(8,128)(2,1)} %copy-done.6, bf16[448,1408]{1,0:T(8,128)(2,1)} %copy-done.4, bf16[960,1408]{1,0:T(8,128)(2,1)} %collective-permute-done.3.refs_4_, ...), custom_call_target="tpu_custom_call" | custom-call | tf_op jit(solution)/shard_map/inner/pallas_call | solution.py:325
  224.1 1.7 copy-done.2
  225.8 12.8 %down.1 = bf16[2,512,2048]{2,1,0:T(8,128)(2,1)} custom-call(bf16[2,2,512,704]{3,2,1,0:T(8,128)(2,1)} %inner.1.act, bf16[704,2048]{1,0:T(8,128)(2,1)} %collective-permute-done.8.down_a, bf16[704,2048]{1,0:T(8,128)(2,1)} %copy-done.2), custom_call_target="tpu_custom_call" | custom-call | tf_op jit(solution)/shard_map/down/pallas_call | solution.py:338
  238.7 61.7 %all_to_all.20 = bf16[64,16,2048]{2,1,0:T(8,128)(2,1)S(1)} all-to-all(bf16[64,16,2048]{2,1,0:T(8,128)(2,1)} %bitcast.27), channel_id=1, replica_groups=mesh['z'=4,'yl'=2,'c'=2,'x'=4,'yh'=2] {'z','yl','x','yh'}, dimensions={0} | all-to-all | bytes 8388608 | tf_op jit(solution)/shard_map/all_to_all | solution.py:352
  300.4 2.8 combine.1
  (31 shorter events, 2.1 us)
Async XLA Ops:
  2.9 29.9 %all-to-all-start = ((bf16[16,400,128]{2,1,0:T(8,128)(2,1)}), bf16[16,400,128]{2,1,0:T(8,128)(2,1)S(1)}, u32[]{:S(2)}, u32[]{:S(2)}) async-start(bf16[16,400,128]{2,1,0:T(8,128)(2,1)} %pack.1), calls=%async_computation | async-start | bytes 3276800 | tf_op jit(solution)/shard_map/all_to_all | solution.py:274
  10.7 106.8 %collective-permute-start.8 = (bf16[704,2048]{1,0:T(8,128)(2,1)}, bf16[704,2048]{1,0:T(8,128)(2,1)}, u32[]{:S(2)}, u32[]{:S(2)}) collective-permute-start(bf16[704,2048]{1,0:T(8,128)(2,1)} %bitcast.33), channel_id=1, source_target_pairs={{0,16},{1,24},{2,18},{3,26},{4,20},{5,28},{6,22},{7,30},{8,17},{9,... | collective-permute-start | bytes 8650760 | tf_op jit(solution)/shard_map/ppermute | solution.py:264
  17.3 25.0 %copy-start.10 = (s32[1,128,6]{1,0,2:T(1,128)S(1)}, s32[1,128,6]{1,0,2:T(1,128)}, u32[]{:S(2)}) copy-start(s32[1,128,6]{1,0,2:T(1,128)} %param.19) | copy-start | bytes 9220
  17.3 25.0 %copy-start.11 = (s32[1,128,6]{1,0,2:T(1,128)S(1)}, s32[1,128,6]{1,0,2:T(1,128)}, u32[]{:S(2)}) copy-start(s32[1,128,6]{1,0,2:T(1,128)} %param.18) | copy-start | bytes 9220
  17.3 99.6 %collective-permute-start.3 = (bf16[960,1408]{1,0:T(8,128)(2,1)}, bf16[960,1408]{1,0:T(8,128)(2,1)}, u32[]{:S(2)}, u32[]{:S(2)}) collective-permute-start(bf16[960,1408]{1,0:T(8,128)(2,1)} %slice_bitcast_fusion), channel_id=1, source_target_pairs={{0,16},{1,24},{2,18},{3,26},{4,20},{5,28},{6,22},{7,30},{8,17},{9,... | collective-permute-start | bytes 8110088 | tf_op jit(solution)/shard_map/ppermute | solution.py:261
  37.9 60.5 %all-to-all-start.1 = ((bf16[16,128,128]{2,1,0:T(8,128)(2,1)}), bf16[16,128,128]{2,1,0:T(8,128)(2,1)S(1)}, u32[]{:S(2)}, u32[]{:S(2)}) async-start(bf16[16,128,128]{2,1,0:T(8,128)(2,1)} %attend.1), calls=%async_computation.1 | async-start | bytes 1048576 | tf_op jit(solution)/shard_map/all_to_all | solution.py:283
  98.4 0.8 copy-start.3
  108.2 96.5 %all-to-all-start.2 = ((bf16[64,16,2048]{2,1,0:T(8,128)(2,1)}), bf16[64,16,2048]{2,1,0:T(8,128)(2,1)}, u32[]{:S(2)}, u32[]{:S(2)}) async-start(bf16[64,16,2048]{2,1,0:T(8,128)(2,1)} %get-tuple-element.10), calls=%async_computation.2 | async-start | bytes 8388608 | tf_op jit(solution)/shard_map/all_to_all | solution.py:322
  116.8 87.9 %collective-permute-start.7 = (bf16[960,1408]{1,0:T(8,128)(2,1)}, bf16[960,1408]{1,0:T(8,128)(2,1)}, u32[]{:S(2)}, u32[]{:S(2)}) collective-permute-start(bf16[960,1408]{1,0:T(8,128)(2,1)} %collective-permute-done.3.refs_4_), channel_id=1, source_target_pairs={{0,8},{1,9},{2,10},{3,11},{4,12},{5,13},{6,14},{7,15},{8,0},{9,1},... | collective-permute-start | bytes 8110088 | tf_op jit(solution)/shard_map/ppermute | solution.py:262
  117.5 106.6 %collective-permute-start.9 = (bf16[704,2048]{1,0:T(8,128)(2,1)}, bf16[704,2048]{1,0:T(8,128)(2,1)S(1)}, u32[]{:S(2)}, u32[]{:S(2)}) collective-permute-start(bf16[704,2048]{1,0:T(8,128)(2,1)} %collective-permute-done.8.down_a), channel_id=1, source_target_pairs={{0,8},{1,9},{2,10},{3,11},{4,12},{5,13},{6,14},{7,15},{8,0},{9,1},... | collective-permute-start | bytes 8650760 | tf_op jit(solution)/shard_map/ppermute | solution.py:265
  119.0 59.0 %collective-permute-start.2 = (bf16[448,1408]{1,0:T(8,128)(2,1)S(1)}, bf16[448,1408]{1,0:T(8,128)(2,1)S(1)}, u32[]{:S(2)}, u32[]{:S(2)}) collective-permute-start(bf16[448,1408]{1,0:T(8,128)(2,1)S(1)} %slice_bitcast_fusion.1), channel_id=1, source_target_pairs={{0,16},{1,24},{2,18},{3,26},{4,20},{5,28},{6,22},{7,30},{8,17},{9,... | collective-permute-start | bytes 3784712 | tf_op jit(solution)/shard_map/ppermute | solution.py:261
  123.1 66.5 %collective-permute-start.1 = (bf16[384,1408]{1,0:T(8,128)(2,1)S(1)}, bf16[384,1408]{1,0:T(8,128)(2,1)S(1)}, u32[]{:S(2)}, u32[]{:S(2)}) collective-permute-start(bf16[384,1408]{1,0:T(8,128)(2,1)S(1)} %slice_bitcast_fusion.2), channel_id=1, source_target_pairs={{0,16},{1,24},{2,18},{3,26},{4,20},{5,28},{6,22},{7,30},{8,17},{9,... | collective-permute-start | bytes 3244040 | tf_op jit(solution)/shard_map/ppermute | solution.py:261
  124.6 72.7 %collective-permute-start = (bf16[256,1408]{1,0:T(8,128)(2,1)S(1)}, bf16[256,1408]{1,0:T(8,128)(2,1)S(1)}, u32[]{:S(2)}, u32[]{:S(2)}) collective-permute-start(bf16[256,1408]{1,0:T(8,128)(2,1)S(1)} %slice_bitcast_fusion.3), channel_id=1, source_target_pairs={{0,16},{1,24},{2,18},{3,26},{4,20},{5,28},{6,22},{7,30},{8,17},{9,... | collective-permute-start | bytes 2162696 | tf_op jit(solution)/shard_map/ppermute | solution.py:261
  178.0 1.1 copy-start.4
  179.1 23.3 %collective-permute-start.6 = (bf16[448,1408]{1,0:T(8,128)(2,1)S(1)}, bf16[448,1408]{1,0:T(8,128)(2,1)S(1)}, u32[]{:S(2)}, u32[]{:S(2)}) collective-permute-start(bf16[448,1408]{1,0:T(8,128)(2,1)S(1)} %collective-permute-done.2.refs_3_), channel_id=1, source_target_pairs={{0,8},{1,9},{2,10},{3,11},{4,12},{5,13},{6,14},{7,15},{8,0},{9,1},... | collective-permute-start | bytes 3784712 | tf_op jit(solution)/shard_map/ppermute | solution.py:262
  189.6 12.8 %copy-start.6 = (bf16[384,1408]{1,0:T(8,128)(2,1)}, bf16[384,1408]{1,0:T(8,128)(2,1)S(1)}, u32[]{:S(2)}) copy-start(bf16[384,1408]{1,0:T(8,128)(2,1)S(1)} %collective-permute-done.1.refs_2_) | copy-start | bytes 3244036
  189.6 12.8 %collective-permute-start.5 = (bf16[384,1408]{1,0:T(8,128)(2,1)S(1)}, bf16[384,1408]{1,0:T(8,128)(2,1)S(1)}, u32[]{:S(2)}, u32[]{:S(2)}) collective-permute-start(bf16[384,1408]{1,0:T(8,128)(2,1)S(1)} %collective-permute-done.1.refs_2_), channel_id=1, source_target_pairs={{0,8},{1,9},{2,10},{3,11},{4,12},{5,13},{6,14},{7,15},{8,0},{9,1},... | collective-permute-start | bytes 3244040 | tf_op jit(solution)/shard_map/ppermute | solution.py:262
  197.3 5.1 %copy-start.8 = (bf16[256,1408]{1,0:T(8,128)(2,1)}, bf16[256,1408]{1,0:T(8,128)(2,1)S(1)}, u32[]{:S(2)}) copy-start(bf16[256,1408]{1,0:T(8,128)(2,1)S(1)} %collective-permute-done.refs_1_) | copy-start | bytes 2162692
  197.3 5.1 %collective-permute-start.4 = (bf16[256,1408]{1,0:T(8,128)(2,1)S(1)}, bf16[256,1408]{1,0:T(8,128)(2,1)S(1)}, u32[]{:S(2)}, u32[]{:S(2)}) collective-permute-start(bf16[256,1408]{1,0:T(8,128)(2,1)S(1)} %collective-permute-done.refs_1_), channel_id=1, source_target_pairs={{0,8},{1,9},{2,10},{3,11},{4,12},{5,13},{6,14},{7,15},{8,0},{9,1},... | collective-permute-start | bytes 2162696 | tf_op jit(solution)/shard_map/ppermute | solution.py:262
  202.4 0.9 copy-start.9
  202.4 1.2 copy-start.7
  203.7 1.1 copy-start.5
  224.1 1.7 copy-start.2
  238.6 61.7 %copy-start = (bf16[128,2048]{1,0:T(8,128)(2,1)S(1)}, bf16[128,2048]{1,0:T(8,128)(2,1)}, u32[]{:S(2)}) copy-start(bf16[128,2048]{1,0:T(8,128)(2,1)} %get-tuple-element.12.mixed_ref) | copy-start | bytes 1572868
  238.6 61.7 %copy-start.1 = (bf16[1024,128]{1,0:T(8,128)(2,1)S(1)}, bf16[1024,128]{1,0:T(8,128)(2,1)}, u32[]{:S(2)}) copy-start(bf16[1024,128]{1,0:T(8,128)(2,1)} %get-tuple-element.11.weight_ref) | copy-start | bytes 786436

commit v3 on v2

--- a/solution.py
+++ b/solution.py
@@ -22,6 +22,8 @@
 Q_BLOCK = 256
 X_BLOCK = 512
 PIECES = (256, 384, 448, 960)
+SPOTS = 16
+Y_SIZE = 4
 NEG_FILL = -1e30
 
 VMEM = pl.BlockSpec(memory_space=pltpu.VMEM)
@@ -132,10 +134,9 @@
 
 
 K_STEPS = 4
-SEND_STEPS = 4
-
-
-def project_kernel(heads_ref, weight_ref, hidden_ref, gain_ref, pick_ref, mixed_ref, send_ref, acc, rows, sems):
+
+
+def project_kernel(heads_ref, weight_ref, hidden_ref, gain_ref, pick_ref, mixed_ref, share_ref, acc):
     step = pl.program_id(0)
     per = HEADS // K_STEPS
     part = jnp.concatenate([heads_ref[i] for i in range(per)], axis=1)
@@ -144,6 +145,13 @@
     @pl.when(step == 0)
     def _():
         acc[...] = product
+        for yl in range(2):
+            for yh in range(2):
+                for spot in range(SPOTS):
+                    place = (spot // 4) * 16 + yl * 8 + (spot % 4) * 2 + yh
+                    lanes = slice(spot * ROWS, (spot + 1) * ROWS)
+                    picks = pick_ref[place * SLOTS : (place + 1) * SLOTS, :]
+                    share_ref[yl * 2 + yh, ROWS:, lanes] = picks
 
     @pl.when(step > 0)
     def _():
@@ -156,25 +164,30 @@
         wide = mixed.astype(f32)
         scale = lax.rsqrt(jnp.mean(wide * wide, axis=-1, keepdims=True) + 1e-06)
         normed = (wide * scale * gain_ref[...]).astype(bf16)
-        count = EXPERTS // SEND_STEPS
-        copies = []
-        for chunk in range(SEND_STEPS):
-            span = slice(chunk * count * SLOTS, (chunk + 1) * count * SLOTS)
-            picked = jnp.dot(pick_ref[span, :], normed, preferred_element_type=f32)
-            rows[chunk] = picked.astype(bf16).reshape(count, SLOTS, D)
-            copy = pltpu.make_async_copy(
-                rows.at[chunk], send_ref.at[pl.ds(chunk * count, count)], sems.at[chunk]
-            )
-            copy.start()
-            copies.append(copy)
-        for copy in copies:
-            copy.wait()
-
-
-def inner_kernel(*refs):
+        for number in range(Y_SIZE):
+            share_ref[number, 0:ROWS, :] = normed
+
+
+def fill_kernel(share_ref, send_ref, rows, sems):
+    copies = []
+    for source in range(Y_SIZE):
+        picks = [share_ref[source, ROWS:, i * ROWS : (i + 1) * ROWS] for i in range(SPOTS)]
+        picked = jnp.dot(
+            jnp.concatenate(picks, axis=0), share_ref[source, 0:ROWS, :], preferred_element_type=f32
+        )
+        rows[source] = picked.astype(bf16).reshape(SPOTS, SLOTS, D)
+        copy = pltpu.make_async_copy(rows.at[source], send_ref.at[:, source], sems.at[source])
+        copy.start()
+        copies.append(copy)
+    for copy in copies:
+        copy.wait()
+
+
+def expert_kernel(*refs):
     pieces = len(PIECES)
     x_any, first, second = refs[0], refs[1 : 1 + pieces], refs[1 + pieces : 1 + 2 * pieces]
-    act, x, w_in, sems = refs[1 + 2 * pieces :]
+    down_a, down_b, out_any, x, w_in, w_down, act, out, sems, out_sems = refs[1 + 2 * pieces :]
+    blocks = x.shape[0]
     load = pltpu.make_async_copy(x_any, x, sems.at[2, 0])
     load.start()
     copies = []
@@ -184,35 +197,33 @@
             goal = w_in.at[half, pl.ds(start, count)]
             copies.append(pltpu.make_async_copy(part, goal, sems.at[half, number]))
             start += count
+    for half, down in enumerate((down_a, down_b)):
+        copies.append(pltpu.make_async_copy(down, w_down.at[half], sems.at[2, 1 + half]))
     for copy in copies:
         copy.start()
     load.wait()
     for half in range(2):
         for number in range(pieces):
             copies[half * pieces + number].wait()
-        for block in range(x.shape[0]):
+        for block in range(blocks):
             inner = jnp.dot(x[block], w_in[half], preferred_element_type=f32)
             gate = inner[:, :HALF]
             up = pltpu.roll(inner, HALF, axis=1)[:, :HALF]
             act[half, block] = (gate / (1.0 + jnp.exp(-gate)) * up).astype(bf16)
-
-
-def down_kernel(act, down_a, down_b, out_any, w_down, out, sems, out_sems):
-    copies = []
-    for half, down in enumerate((down_a, down_b)):
-        copies.append(pltpu.make_async_copy(down, w_down.at[half], sems.at[half]))
-    for copy in copies:
-        copy.start()
-    for copy in copies:
-        copy.wait()
+    copies[2 * pieces].wait()
+    copies[2 * pieces + 1].wait()
     sends = []
-    for block in range(out.shape[0]):
+    spots = SPOTS // blocks
+    for block in range(blocks):
         total = jnp.dot(act[0, block], w_down[0], preferred_element_type=f32)
         total = total + jnp.dot(act[1, block], w_down[1], preferred_element_type=f32)
-        out[block] = total.astype(bf16)
-        send = pltpu.make_async_copy(out.at[block], out_any.at[block], out_sems.at[block])
-        send.start()
-        sends.append(send)
+        out[block] = total.astype(bf16).reshape(spots, 2, 2, SLOTS, D)
+        for near in range(spots):
+            spot = block * spots + near
+            goal = out_any.at[spot // 4, :, spot % 4]
+            send = pltpu.make_async_copy(out.at[block, near], goal, out_sems.at[spot])
+            send.start()
+            sends.append(send)
     for send in sends:
         send.wait()
 
@@ -293,12 +304,12 @@
         name="route",
     )(expert_ids[0].T, gate_codes[0].T)
     per = HEADS // K_STEPS
-    mixed, send = pl.pallas_call(
+    mixed, share = pl.pallas_call(
         project_kernel,
         grid=(K_STEPS,),
         out_shape=(
             shape((ROWS, D), bf16),
-            shape((EXPERTS, SLOTS, D), bf16),
+            shape((Y_SIZE, ROWS + SLOTS, D), bf16),
         ),
         in_specs=[
             pl.BlockSpec((per, ROWS, HEAD_DIM), lambda i: (i, 0, 0)),
@@ -309,46 +320,47 @@
         ],
         out_specs=(
             pl.BlockSpec((ROWS, D), lambda i: (0, 0)),
-            pl.BlockSpec(memory_space=pltpu.HBM),
+            pl.BlockSpec((Y_SIZE, ROWS + SLOTS, D), lambda i: (0, 0, 0)),
         ),
-        scratch_shapes=[
-            pltpu.VMEM((ROWS, D), f32),
-            pltpu.VMEM((SEND_STEPS, EXPERTS // SEND_STEPS, SLOTS, D), bf16),
-            pltpu.SemaphoreType.DMA((SEND_STEPS,)),
-        ],
-        compiler_params=params(55),
+        scratch_shapes=[pltpu.VMEM((ROWS, D), f32)],
+        compiler_params=params(53),
         name="project",
     )(heads, out_weight, hidden_in[0], norm_gain[None], pick)
-    arrived = lax.all_to_all(send, PLACES, split_axis=0, concat_axis=0, tiled=True)
+    shared = lax.all_to_all(share, ("yl", "yh"), split_axis=0, concat_axis=0, tiled=True)
+    send = pl.pallas_call(
+        fill_kernel,
+        out_shape=shape((SPOTS, Y_SIZE, SLOTS, D), bf16),
+        in_specs=[VMEM],
+        out_specs=pl.BlockSpec(memory_space=pl.ANY),
+        scratch_shapes=[
+            pltpu.VMEM((Y_SIZE, SPOTS, SLOTS, D), bf16),
+            pltpu.SemaphoreType.DMA((Y_SIZE,)),
+        ],
+        compiler_params=params(50),
+        name="fill",
+    )(shared)
+    arrived = lax.all_to_all(
+        send.reshape(SPOTS, Y_SIZE * SLOTS, D), ("z", "x"), split_axis=0, concat_axis=0, tiled=True
+    )
     blocks = EXPERTS * SLOTS // X_BLOCK
     anywhere = pl.BlockSpec(memory_space=pl.ANY)
-    act = pl.pallas_call(
-        inner_kernel,
-        out_shape=shape((2, blocks, X_BLOCK, HALF), bf16),
-        in_specs=[anywhere] * (1 + 2 * len(PIECES)),
-        out_specs=VMEM,
+    results = pl.pallas_call(
+        expert_kernel,
+        out_shape=shape((4, 2, 4, 2, SLOTS, D), bf16),
+        in_specs=[anywhere] * (3 + 2 * len(PIECES)),
+        out_specs=anywhere,
         scratch_shapes=[
             pltpu.VMEM((blocks, X_BLOCK, D), bf16),
             pltpu.VMEM((2, D, 2 * HALF), bf16),
+            pltpu.VMEM((2, HALF, D), bf16),
+            pltpu.VMEM((2, blocks, X_BLOCK, HALF), bf16),
+            pltpu.VMEM((blocks, SPOTS // blocks, 2, 2, SLOTS, D), bf16),
             pltpu.SemaphoreType.DMA((3, len(PIECES))),
+            pltpu.SemaphoreType.DMA((SPOTS,)),
         ],
-        compiler_params=params(58),
-        name="inner",
-    )(arrived.reshape(blocks, X_BLOCK, D), *moved, *other)
-    results = pl.pallas_call(
-        down_kernel,
-        out_shape=shape((blocks, X_BLOCK, D), bf16),
-        in_specs=[VMEM, anywhere, anywhere],
-        out_specs=anywhere,
-        scratch_shapes=[
-            pltpu.VMEM((2, HALF, D), bf16),
-            pltpu.VMEM((blocks, X_BLOCK, D), bf16),
-            pltpu.SemaphoreType.DMA((2,)),
-            pltpu.SemaphoreType.DMA((blocks,)),
-        ],
-        compiler_params=params(58),
-        name="down",
-    )(act, moved_down, other_down)
+        compiler_params=params(52),
+        name="experts",
+    )(arrived.reshape(blocks, X_BLOCK, D), *moved, *other, moved_down, other_down)
     returned = lax.all_to_all(
         results.reshape(EXPERTS, SLOTS, D), PLACES, split_axis=0, concat_axis=0, tiled=True
     )

time: 304 us -> 285 us (0.938)
  blocking collectives: 61.7 us -> 102 us
  waiting for transfers between devices: 133 us -> 92.7 us
  starting transfers between devices: 40.3 us -> 30.8 us
  Pallas kernels: 54 us -> 48.5 us
  local copies, waits for them, and re-layouts: 13.8 us -> 9.57 us
    all_to_all x0 -> x1, blocking collectives: none -> 45.2 us  [local(): lax.all_to_all(share, ('yl', 'yh'), split_axis=0, concat_axis=0, tiled=True)]
    all_to_all x1, waiting for transfers between devices: 53.6 us -> 19 us  [local(): lax.all_to_all(attended, POSITIONS, split_axis=0, concat_axis=0, tiled=True)]
    ppermute x4, waiting for transfers between devices: 62.3 us -> 30.1 us  [local(): moved.append(lax.ppermute(piece, AXES, moves(weight_target)))]
    all_to_all x1, waiting for transfers between devices: 0.01 us -> 22.5 us  [local(): lax.all_to_all(send.reshape(SPOTS, Y_SIZE * SLOTS, D), ('z', 'x'), split_...]
    ppermute x4, starting transfers between devices: 10.5 us -> 0.09 us  [local(): other.append(lax.ppermute(moved[-1], AXES, moves(core_target)))]
    all_to_all x1, blocking collectives: 61.7 us -> 57.2 us  [local(): lax.all_to_all(results.reshape(EXPERTS, SLOTS, D), PLACES, split_axis=0,...]
    pallas_call x2, Pallas kernels: 32.2 us -> 28.5 us  [the longest x1 26 us: local(): pl.pallas_call(expert_kernel, out_shape=shape((4, 2, 4, 2, SLOTS, D), bf1...]
    all_to_all x1, waiting for transfers between devices: 15.5 us -> 19 us  [local(): lax.all_to_all(packed, POSITIONS, split_axis=0, concat_axis=0, tiled=True)]
  transfers between devices with their start and end apart: 13 -> 13, of which waited for: 6 -> 7; matrix products, arithmetic and copies ran while one was open for 3% -> 2% of each run, Pallas kernels for 12% -> 6%
where the time goes in v3:
time: 285 us; the launch traced here: 284 us
  blocking collectives  102 us (36%)
  waiting for transfers between devices  92.7 us (33%)
  Pallas kernels  48.5 us (17%)
  starting transfers between devices  30.8 us (11%)
  local copies, waits for them, and re-layouts  9.57 us (3%)
    all_to_all x1, blocking collectives, local(): lax.all_to_all(results.reshape(EXPERTS, SLOTS, D), PLACES, split_axis=0,...  57.2 us
    all_to_all x1, blocking collectives, local(): lax.all_to_all(share, ('yl', 'yh'), split_axis=0, concat_axis=0, tiled=True)  45.2 us
    ppermute x4, waiting for transfers between devices, local(): moved.append(lax.ppermute(piece, AXES, moves(weight_target)))  30.1 us
    pallas_call x1, Pallas kernels, local(): pl.pallas_call(expert_kernel, out_shape=shape((4, 2, 4, 2, SLOTS, D), bf1...  26 us
    all_to_all x1, waiting for transfers between devices, local(): lax.all_to_all(send.reshape(SPOTS, Y_SIZE * SLOTS, D), ('z', 'x'), split_...  22.5 us
    all_to_all x1, waiting for transfers between devices, local(): lax.all_to_all(attended, POSITIONS, split_axis=0, concat_axis=0, tiled=True)  19 us
    all_to_all x1, waiting for transfers between devices, local(): lax.all_to_all(packed, POSITIONS, split_axis=0, concat_axis=0, tiled=True)  19 us
    ppermute x4, starting transfers between devices, local(): moved.append(lax.ppermute(piece, AXES, moves(weight_target)))  8.65 us
  transfers between devices with their start and end apart: 13, of which 7 were waited for; matrix products, arithmetic and copies ran while one was open for 2% of the time, Pallas kernels for 6%

profile of v3, /device:TPU:1, one launch (start us, length us, event | category | flops | bytes accessed | tf_op | source)
XLA Modules:
  0.0 284.2 jit_solution(5769052629984764601)
XLA Ops:
  0.0 2.9 %pack.1 = bf16[16,400,128]{2,1,0:T(8,128)(2,1)} custom-call(bf16[128,2048]{1,0:T(8,128)(2,1)} %bitcast.32, bf16[128,2048]{1,0:T(8,128)(2,1)} %bitcast.33, bf16[128,2048]{1,0:T(8,128)(2,1)} %bitcast.34, s32[1,128]{1,0:T(1,128)} %seg_ref.1), custom_call_target="tpu_custom_call" | custom-call | tf_op jit(solution)/shard_map/pack/pallas_call | solution.py:277
  2.9 7.8 %all-to-all-start = ((bf16[16,400,128]{2,1,0:T(8,128)(2,1)}), bf16[16,400,128]{2,1,0:T(8,128)(2,1)S(1)}, u32[]{:S(2)}, u32[]{:S(2)}) async-start(bf16[16,400,128]{2,1,0:T(8,128)(2,1)} %pack.1), calls=%async_computation | async-start | bytes 3276800 | tf_op jit(solution)/shard_map/all_to_all | solution.py:285
  10.7 3.1 %collective-permute-start.8 = (bf16[704,2048]{1,0:T(8,128)(2,1)}, bf16[704,2048]{1,0:T(8,128)(2,1)}, u32[]{:S(2)}, u32[]{:S(2)}) collective-permute-start(bf16[704,2048]{1,0:T(8,128)(2,1)} %bitcast.35), channel_id=1, source_target_pairs={{0,16},{1,24},{2,18},{3,26},{4,20},{5,28},{6,22},{7,30},{8,17},{9,... | collective-permute-start | bytes 8650760 | tf_op jit(solution)/shard_map/ppermute | solution.py:275
  13.8 19.0 %all-to-all-done.x_ref = bf16[16,400,128]{2,1,0:T(8,128)(2,1)S(1)} async-done(((bf16[16,400,128]{2,1,0:T(8,128)(2,1)}), bf16[16,400,128]{2,1,0:T(8,128)(2,1)S(1)}, u32[]{:S(2)}, u32[]{:S(2)}) %all-to-all-start) | async-done | bytes 1638432 | tf_op jit(solution)/shard_map/all_to_all | solution.py:285
  32.8 5.1 %attend.1 = bf16[16,128,128]{2,1,0:T(8,128)(2,1)} custom-call(bf16[16,400,128]{2,1,0:T(8,128)(2,1)S(1)} %all-to-all-done.x_ref), custom_call_target="tpu_custom_call" | custom-call | tf_op jit(solution)/shard_map/attend/pallas_call | solution.py:286
  37.9 4.3 %all-to-all-start.1 = ((bf16[16,128,128]{2,1,0:T(8,128)(2,1)}), bf16[16,128,128]{2,1,0:T(8,128)(2,1)S(1)}, u32[]{:S(2)}, u32[]{:S(2)}) async-start(bf16[16,128,128]{2,1,0:T(8,128)(2,1)} %attend.1), calls=%async_computation.1 | async-start | bytes 1048576 | tf_op jit(solution)/shard_map/all_to_all | solution.py:294
  42.2 2.0 slice_bitcast_fusion
  44.2 3.7 %collective-permute-start.3 = (bf16[960,1408]{1,0:T(8,128)(2,1)S(1)}, bf16[960,1408]{1,0:T(8,128)(2,1)}, u32[]{:S(2)}, u32[]{:S(2)}) collective-permute-start(bf16[960,1408]{1,0:T(8,128)(2,1)S(1)} %slice_bitcast_fusion), channel_id=1, source_target_pairs={{0,16},{1,24},{2,18},{3,26},{4,20},{5,28},{6,22},{7,30},{8,17},{9,... | collective-permute-start | bytes 8110088 | tf_op jit(solution)/shard_map/ppermute | solution.py:272
  48.0 0.6 copy_bitcast_fusion
  48.6 1.9 route.1
  50.5 19.0 %all-to-all-done.1.heads_ref = bf16[16,128,128]{2,1,0:T(8,128)(2,1)S(1)} async-done(((bf16[16,128,128]{2,1,0:T(8,128)(2,1)}), bf16[16,128,128]{2,1,0:T(8,128)(2,1)S(1)}, u32[]{:S(2)}, u32[]{:S(2)}) %all-to-all-start.1) | async-done | bytes 524320 | tf_op jit(solution)/shard_map/all_to_all | solution.py:294
  69.4 0.8 copy-done.3
  70.2 0.9 copy-done
  71.2 7.3 %project.1 = (bf16[128,2048]{1,0:T(8,128)(2,1)S(1)}, bf16[4,144,2048]{2,1,0:T(8,128)(2,1)}) custom-call(bf16[16,128,128]{2,1,0:T(8,128)(2,1)} %copy-done.3, bf16[2048,2048]{1,0:T(8,128)(2,1)} %weight_ref.1, bf16[128,2048]{1,0:T(8,128)(2,1)} %bitcast.31, f32[1,2048]{1,0:T(1,128)S(1)} %bitcast.28, bf16[1024,128]{1,0:T(8,128)(2,1)S(1)} %copy-done), custom_call_target="tpu_custom_call" | custom-call | tf_op jit(solution)/shard_map/project/pallas_call | solution.py:307
  78.5 45.2 %all_to_all.25.share_ref = bf16[4,144,2048]{2,1,0:T(8,128)(2,1)S(1)} all-to-all(bf16[4,144,2048]{2,1,0:T(8,128)(2,1)} %get-tuple-element.10), channel_id=1, replica_groups=mesh['z'=4,'yl'=2,'c'=2,'x'=4,'yh'=2] {'yl','yh'}, dimensions={0} | all-to-all | bytes 4718592 | tf_op jit(solution)/shard_map/all_to_all | solution.py:329
  123.7 2.5 fill.1
  126.1 6.3 %all-to-all-start.3 = ((bf16[16,64,2048]{2,1,0:T(8,128)(2,1)}), bf16[16,64,2048]{2,1,0:T(8,128)(2,1)}, u32[]{:S(2)}, u32[]{:S(2)}) async-start(bf16[16,64,2048]{2,1,0:T(8,128)(2,1)} %bitcast.30), calls=%async_computation.3 | async-start | bytes 8388608 | tf_op jit(solution)/shard_map/all_to_all | solution.py:342
  133.0 1.4 slice_bitcast_fusion.1
  134.4 1.8 collective-permute-start.2
  136.2 1.3 slice_bitcast_fusion.2
  137.6 1.3 collective-permute-start.1
  138.9 1.2 slice_bitcast_fusion.3
  140.0 1.8 collective-permute-start
  141.8 10.8 %collective-permute-done.2.refs_3_ = bf16[448,1408]{1,0:T(8,128)(2,1)S(1)} collective-permute-done((bf16[448,1408]{1,0:T(8,128)(2,1)S(1)}, bf16[448,1408]{1,0:T(8,128)(2,1)S(1)}, u32[]{:S(2)}, u32[]{:S(2)}) %collective-permute-start.2) | collective-permute-done | bytes 1261600 | tf_op jit(solution)/shard_map/ppermute | solution.py:272
  152.6 11.6 %collective-permute-done.1.refs_2_ = bf16[384,1408]{1,0:T(8,128)(2,1)S(1)} collective-permute-done((bf16[384,1408]{1,0:T(8,128)(2,1)S(1)}, bf16[384,1408]{1,0:T(8,128)(2,1)S(1)}, u32[]{:S(2)}, u32[]{:S(2)}) %collective-permute-start.1) | collective-permute-done | bytes 1081376 | tf_op jit(solution)/shard_map/ppermute | solution.py:272
  164.2 7.7 %collective-permute-done.refs_1_ = bf16[256,1408]{1,0:T(8,128)(2,1)S(1)} collective-permute-done((bf16[256,1408]{1,0:T(8,128)(2,1)S(1)}, bf16[256,1408]{1,0:T(8,128)(2,1)S(1)}, u32[]{:S(2)}, u32[]{:S(2)}) %collective-permute-start) | collective-permute-done | bytes 720928 | tf_op jit(solution)/shard_map/ppermute | solution.py:272
  172.0 2.2 collective-permute-done.4.refs_5_
  174.2 1.1 copy-done.5
  175.5 22.5 %all-to-all-done.3 = bf16[16,64,2048]{2,1,0:T(8,128)(2,1)} async-done(((bf16[16,64,2048]{2,1,0:T(8,128)(2,1)}), bf16[16,64,2048]{2,1,0:T(8,128)(2,1)}, u32[]{:S(2)}, u32[]{:S(2)}) %all-to-all-start.3) | async-done | bytes 4194336 | tf_op jit(solution)/shard_map/all_to_all | solution.py:342
  198.0 26.0 %experts.1 = bf16[4,2,4,2,16,2048]{5,4,3,2,1,0:T(8,128)(2,1)} custom-call(bf16[2,512,2048]{2,1,0:T(8,128)(2,1)} %bitcast.8.refs_0_, bf16[256,1408]{1,0:T(8,128)(2,1)S(1)} %collective-permute-done.refs_1_, bf16[384,1408]{1,0:T(8,128)(2,1)} %copy-done.6, bf16[448,1408]{1,0:T(8,128)(2,1)} %copy-done.4, bf16[960,1408]{1,0:T(8,128)(2,1)} %collective-permute-done.3.refs_4_, ...), custom_call_target="tpu_custom_call" | custom-call | tf_op jit(solution)/shard_map/experts/pallas_call | solution.py:347
  224.1 57.2 %all_to_all.26 = bf16[64,16,2048]{2,1,0:T(8,128)(2,1)S(1)} all-to-all(bf16[64,16,2048]{2,1,0:T(8,128)(2,1)} %bitcast.29), channel_id=1, replica_groups=mesh['z'=4,'yl'=2,'c'=2,'x'=4,'yh'=2] {'z','yl','x','yh'}, dimensions={0} | all-to-all | bytes 8388608 | tf_op jit(solution)/shard_map/all_to_all | solution.py:364
  281.4 2.8 combine.1
  (28 shorter events, 0.9 us)
Async XLA Ops:
  2.9 29.9 %all-to-all-start = ((bf16[16,400,128]{2,1,0:T(8,128)(2,1)}), bf16[16,400,128]{2,1,0:T(8,128)(2,1)S(1)}, u32[]{:S(2)}, u32[]{:S(2)}) async-start(bf16[16,400,128]{2,1,0:T(8,128)(2,1)} %pack.1), calls=%async_computation | async-start | bytes 3276800 | tf_op jit(solution)/shard_map/all_to_all | solution.py:285
  10.7 121.8 %collective-permute-start.8 = (bf16[704,2048]{1,0:T(8,128)(2,1)}, bf16[704,2048]{1,0:T(8,128)(2,1)}, u32[]{:S(2)}, u32[]{:S(2)}) collective-permute-start(bf16[704,2048]{1,0:T(8,128)(2,1)} %bitcast.35), channel_id=1, source_target_pairs={{0,16},{1,24},{2,18},{3,26},{4,20},{5,28},{6,22},{7,30},{8,17},{9,... | collective-permute-start | bytes 8650760 | tf_op jit(solution)/shard_map/ppermute | solution.py:275
  37.9 31.6 %all-to-all-start.1 = ((bf16[16,128,128]{2,1,0:T(8,128)(2,1)}), bf16[16,128,128]{2,1,0:T(8,128)(2,1)S(1)}, u32[]{:S(2)}, u32[]{:S(2)}) async-start(bf16[16,128,128]{2,1,0:T(8,128)(2,1)} %attend.1), calls=%async_computation.1 | async-start | bytes 1048576 | tf_op jit(solution)/shard_map/all_to_all | solution.py:294
  42.2 5.7 %copy-start.8 = (s32[1,128,6]{1,0,2:T(1,128)S(1)}, s32[1,128,6]{1,0,2:T(1,128)}, u32[]{:S(2)}) copy-start(s32[1,128,6]{1,0,2:T(1,128)} %param.19) | copy-start | bytes 9220
  42.2 5.7 %copy-start.9 = (s32[1,128,6]{1,0,2:T(1,128)S(1)}, s32[1,128,6]{1,0,2:T(1,128)}, u32[]{:S(2)}) copy-start(s32[1,128,6]{1,0,2:T(1,128)} %param.18) | copy-start | bytes 9220
  42.2 28.0 %copy-start.2 = (f32[2048]{0:T(1024)S(1)}, f32[2048]{0:T(1024)}, u32[]{:S(2)}) copy-start(f32[2048]{0:T(1024)} %param.17) | copy-start | bytes 24580
  44.2 88.2 %collective-permute-start.3 = (bf16[960,1408]{1,0:T(8,128)(2,1)S(1)}, bf16[960,1408]{1,0:T(8,128)(2,1)}, u32[]{:S(2)}, u32[]{:S(2)}) collective-permute-start(bf16[960,1408]{1,0:T(8,128)(2,1)S(1)} %slice_bitcast_fusion), channel_id=1, source_target_pairs={{0,16},{1,24},{2,18},{3,26},{4,20},{5,28},{6,22},{7,30},{8,17},{9,... | collective-permute-start | bytes 8110088 | tf_op jit(solution)/shard_map/ppermute | solution.py:272
  69.4 0.8 copy-start.3
  70.2 1.0 copy-start
  126.1 71.9 %all-to-all-start.3 = ((bf16[16,64,2048]{2,1,0:T(8,128)(2,1)}), bf16[16,64,2048]{2,1,0:T(8,128)(2,1)}, u32[]{:S(2)}, u32[]{:S(2)}) async-start(bf16[16,64,2048]{2,1,0:T(8,128)(2,1)} %bitcast.30), calls=%async_computation.3 | async-start | bytes 8388608 | tf_op jit(solution)/shard_map/all_to_all | solution.py:342
  132.5 42.8 %collective-permute-start.7 = (bf16[960,1408]{1,0:T(8,128)(2,1)}, bf16[960,1408]{1,0:T(8,128)(2,1)}, u32[]{:S(2)}, u32[]{:S(2)}) collective-permute-start(bf16[960,1408]{1,0:T(8,128)(2,1)} %collective-permute-done.3.refs_4_), channel_id=1, source_target_pairs={{0,8},{1,9},{2,10},{3,11},{4,12},{5,13},{6,14},{7,15},{8,0},{9,1},... | collective-permute-start | bytes 8110088 | tf_op jit(solution)/shard_map/ppermute | solution.py:273
  132.6 43.0 %collective-permute-start.9 = (bf16[704,2048]{1,0:T(8,128)(2,1)}, bf16[704,2048]{1,0:T(8,128)(2,1)}, u32[]{:S(2)}, u32[]{:S(2)}) collective-permute-start(bf16[704,2048]{1,0:T(8,128)(2,1)} %collective-permute-done.8.refs_9_), channel_id=1, source_target_pairs={{0,8},{1,9},{2,10},{3,11},{4,12},{5,13},{6,14},{7,15},{8,0},{9,1},... | collective-permute-start | bytes 8650760 | tf_op jit(solution)/shard_map/ppermute | solution.py:276
  134.4 18.2 %collective-permute-start.2 = (bf16[448,1408]{1,0:T(8,128)(2,1)S(1)}, bf16[448,1408]{1,0:T(8,128)(2,1)S(1)}, u32[]{:S(2)}, u32[]{:S(2)}) collective-permute-start(bf16[448,1408]{1,0:T(8,128)(2,1)S(1)} %slice_bitcast_fusion.1), channel_id=1, source_target_pairs={{0,16},{1,24},{2,18},{3,26},{4,20},{5,28},{6,22},{7,30},{8,17},{9,... | collective-permute-start | bytes 3784712 | tf_op jit(solution)/shard_map/ppermute | solution.py:272
  137.6 26.7 %collective-permute-start.1 = (bf16[384,1408]{1,0:T(8,128)(2,1)S(1)}, bf16[384,1408]{1,0:T(8,128)(2,1)S(1)}, u32[]{:S(2)}, u32[]{:S(2)}) collective-permute-start(bf16[384,1408]{1,0:T(8,128)(2,1)S(1)} %slice_bitcast_fusion.2), channel_id=1, source_target_pairs={{0,16},{1,24},{2,18},{3,26},{4,20},{5,28},{6,22},{7,30},{8,17},{9,... | collective-permute-start | bytes 3244040 | tf_op jit(solution)/shard_map/ppermute | solution.py:272
  140.0 31.9 %collective-permute-start = (bf16[256,1408]{1,0:T(8,128)(2,1)S(1)}, bf16[256,1408]{1,0:T(8,128)(2,1)S(1)}, u32[]{:S(2)}, u32[]{:S(2)}) collective-permute-start(bf16[256,1408]{1,0:T(8,128)(2,1)S(1)} %slice_bitcast_fusion.3), channel_id=1, source_target_pairs={{0,16},{1,24},{2,18},{3,26},{4,20},{5,28},{6,22},{7,30},{8,17},{9,... | collective-permute-start | bytes 2162696 | tf_op jit(solution)/shard_map/ppermute | solution.py:272
  152.6 45.4 %copy-start.4 = (bf16[448,1408]{1,0:T(8,128)(2,1)}, bf16[448,1408]{1,0:T(8,128)(2,1)S(1)}, u32[]{:S(2)}) copy-start(bf16[448,1408]{1,0:T(8,128)(2,1)S(1)} %collective-permute-done.2.refs_3_) | copy-start | bytes 3784708
  152.6 21.5 %collective-permute-start.6 = (bf16[448,1408]{1,0:T(8,128)(2,1)S(1)}, bf16[448,1408]{1,0:T(8,128)(2,1)S(1)}, u32[]{:S(2)}, u32[]{:S(2)}) collective-permute-start(bf16[448,1408]{1,0:T(8,128)(2,1)S(1)} %collective-permute-done.2.refs_3_), channel_id=1, source_target_pairs={{0,8},{1,9},{2,10},{3,11},{4,12},{5,13},{6,14},{7,15},{8,0},{9,1},... | collective-permute-start | bytes 3784712 | tf_op jit(solution)/shard_map/ppermute | solution.py:273
  164.2 11.0 %copy-start.6 = (bf16[384,1408]{1,0:T(8,128)(2,1)}, bf16[384,1408]{1,0:T(8,128)(2,1)S(1)}, u32[]{:S(2)}) copy-start(bf16[384,1408]{1,0:T(8,128)(2,1)S(1)} %collective-permute-done.1.refs_2_) | copy-start | bytes 3244036
  164.2 9.9 %collective-permute-start.5 = (bf16[384,1408]{1,0:T(8,128)(2,1)S(1)}, bf16[384,1408]{1,0:T(8,128)(2,1)S(1)}, u32[]{:S(2)}, u32[]{:S(2)}) collective-permute-start(bf16[384,1408]{1,0:T(8,128)(2,1)S(1)} %collective-permute-done.1.refs_2_), channel_id=1, source_target_pairs={{0,8},{1,9},{2,10},{3,11},{4,12},{5,13},{6,14},{7,15},{8,0},{9,1},... | collective-permute-start | bytes 3244040 | tf_op jit(solution)/shard_map/ppermute | solution.py:273
  172.0 2.2 collective-permute-start.4
  174.1 1.4 copy-start.7
  174.2 1.1 copy-start.5
  224.1 57.3 %copy-start.1 = (bf16[1024,128]{1,0:T(8,128)(2,1)S(1)}, bf16[1024,128]{1,0:T(8,128)(2,1)}, u32[]{:S(2)}) copy-start(bf16[1024,128]{1,0:T(8,128)(2,1)} %get-tuple-element.11.weight_ref) | copy-start | bytes 786436

commit v4 on v3

--- a/solution.py
+++ b/solution.py
@@ -27,6 +27,7 @@
 NEG_FILL = -1e30
 
 VMEM = pl.BlockSpec(memory_space=pltpu.VMEM)
+SMEM = pl.BlockSpec(memory_space=pltpu.SMEM)
 f32 = jnp.float32
 bf16 = jnp.bfloat16
 
@@ -58,6 +59,14 @@
 
 def core_target(z, yl, c, x, yh):
     return (z, yl, 1 - c, x, yh)
+
+
+def along_y(distance):
+    def target(z, yl, c, x, yh):
+        y = (yl + 2 * yh + distance) % Y_SIZE
+        return (z, y % 2, c, x, y // 2)
+
+    return target
 
 
 def params(mib):
@@ -107,36 +116,47 @@
     return (expert & 48) | (8 - (expert & 8)) | ((expert & 3) << 1) | ((expert >> 2) & 1)
 
 
-def route_kernel(ids_ref, codes_ref, pick_ref, weight_ref):
-    expert = lax.broadcasted_iota(jnp.int32, (EXPERTS, ROWS), 0)
-    member = jnp.zeros((EXPERTS, ROWS), f32)
-    code = jnp.zeros((EXPERTS, ROWS), f32)
-    for k in range(TOPK):
-        named = expert == place_of(ids_ref[k : k + 1, :])
-        member = member + jnp.where(named, 1.0, 0.0)
-        code = code + jnp.where(named, codes_ref[k : k + 1, :].astype(f32), 0.0)
+def reach_of(expert, y):
+    distance = (1 - ((expert >> 3) & 1) + ((expert >> 1) & 2) - y) & 3
+    return (distance << 4) | ((expert >> 2) & 12) | (expert & 3)
+
+
+def route_kernel(y_ref, ids_ref, codes_ref, pick_ref, weight_ref):
+    number = lax.broadcasted_iota(jnp.int32, (EXPERTS, ROWS), 0)
     earlier = lax.broadcasted_iota(jnp.int32, (ROWS, ROWS), 0) < lax.broadcasted_iota(
         jnp.int32, (ROWS, ROWS), 1
     )
-    rank = jnp.dot(
-        member.astype(bf16), jnp.where(earlier, 1.0, 0.0).astype(bf16), preferred_element_type=f32
-    )
+    earlier = jnp.where(earlier, 1.0, 0.0).astype(bf16)
     rows = EXPERTS * SLOTS
     own = lax.broadcasted_iota(jnp.int32, (rows, EXPERTS), 0) // SLOTS
     mine = own == lax.broadcasted_iota(jnp.int32, (rows, EXPERTS), 1)
     mine = jnp.where(mine, 1.0, 0.0).astype(bf16)
-    place = jnp.dot(mine, (member * (rank + 1.0)).astype(bf16), preferred_element_type=f32)
+    slot = (lax.broadcasted_iota(jnp.int32, (rows, ROWS), 0) & (SLOTS - 1)) + 1
+    ids = ids_ref[...]
+
+    def ordered(names):
+        member = jnp.zeros((EXPERTS, ROWS), f32)
+        code = jnp.zeros((EXPERTS, ROWS), f32)
+        for k in range(TOPK):
+            named = number == names[k : k + 1, :]
+            member = member + jnp.where(named, 1.0, 0.0)
+            code = code + jnp.where(named, codes_ref[k : k + 1, :].astype(f32), 0.0)
+        rank = jnp.dot(member.astype(bf16), earlier, preferred_element_type=f32)
+        place = jnp.dot(mine, (member * (rank + 1.0)).astype(bf16), preferred_element_type=f32)
+        return place == slot.astype(f32), code
+
+    here, _ = ordered(reach_of(ids, y_ref[0]))
+    pick_ref[...] = jnp.where(here, 1.0, 0.0).astype(bf16)
+    here, code = ordered(place_of(ids))
     codes = jnp.dot(mine, code.astype(bf16), preferred_element_type=f32)
-    slot = (lax.broadcasted_iota(jnp.int32, (rows, ROWS), 0) & (SLOTS - 1)) + 1
-    here = place == slot.astype(f32)
-    pick_ref[...] = jnp.where(here, 1.0, 0.0).astype(bf16)
     weight_ref[...] = jnp.where(here, codes, 0.0).astype(bf16)
 
 
 K_STEPS = 4
 
 
-def project_kernel(heads_ref, weight_ref, hidden_ref, gain_ref, pick_ref, mixed_ref, share_ref, acc):
+def project_kernel(heads_ref, weight_ref, hidden_ref, gain_ref, pick_ref, mixed_ref, *rest):
+    shares, own_ref, acc = rest[:3], rest[3], rest[4]
     step = pl.program_id(0)
     per = HEADS // K_STEPS
     part = jnp.concatenate([heads_ref[i] for i in range(per)], axis=1)
@@ -145,13 +165,11 @@
     @pl.when(step == 0)
     def _():
         acc[...] = product
-        for yl in range(2):
-            for yh in range(2):
-                for spot in range(SPOTS):
-                    place = (spot // 4) * 16 + yl * 8 + (spot % 4) * 2 + yh
-                    lanes = slice(spot * ROWS, (spot + 1) * ROWS)
-                    picks = pick_ref[place * SLOTS : (place + 1) * SLOTS, :]
-                    share_ref[yl * 2 + yh, ROWS:, lanes] = picks
+        for distance in range(1, Y_SIZE):
+            for spot in range(SPOTS):
+                lanes = slice(spot * ROWS, (spot + 1) * ROWS)
+                first = (distance * SPOTS + spot) * SLOTS
+                shares[distance - 1][ROWS:, lanes] = pick_ref[first : first + SLOTS, :]
 
     @pl.when(step > 0)
     def _():
@@ -164,16 +182,18 @@
         wide = mixed.astype(f32)
         scale = lax.rsqrt(jnp.mean(wide * wide, axis=-1, keepdims=True) + 1e-06)
         normed = (wide * scale * gain_ref[...]).astype(bf16)
-        for number in range(Y_SIZE):
-            share_ref[number, 0:ROWS, :] = normed
-
-
-def fill_kernel(share_ref, send_ref, rows, sems):
+        for share_ref in shares:
+            share_ref[0:ROWS, :] = normed
+        picked = jnp.dot(pick_ref[: SPOTS * SLOTS, :], normed, preferred_element_type=f32)
+        own_ref[...] = picked.astype(bf16).reshape(SPOTS, SLOTS, D)
+
+
+def fill_kernel(near_ref, far_ref, back_ref, send_ref, rows, sems):
     copies = []
-    for source in range(Y_SIZE):
-        picks = [share_ref[source, ROWS:, i * ROWS : (i + 1) * ROWS] for i in range(SPOTS)]
+    for source, share_ref in enumerate((near_ref, back_ref, far_ref)):
+        picks = [share_ref[ROWS:, i * ROWS : (i + 1) * ROWS] for i in range(SPOTS)]
         picked = jnp.dot(
-            jnp.concatenate(picks, axis=0), share_ref[source, 0:ROWS, :], preferred_element_type=f32
+            jnp.concatenate(picks, axis=0), share_ref[0:ROWS, :], preferred_element_type=f32
         )
         rows[source] = picked.astype(bf16).reshape(SPOTS, SLOTS, D)
         copy = pltpu.make_async_copy(rows.at[source], send_ref.at[:, source], sems.at[source])
@@ -183,13 +203,26 @@
         copy.wait()
 
 
+def origin(unit):
+    if unit < SPOTS:
+        return unit, 0
+    return (unit - SPOTS) // 3, (3, 1, 2)[(unit - SPOTS) % 3]
+
+
 def expert_kernel(*refs):
     pieces = len(PIECES)
-    x_any, first, second = refs[0], refs[1 : 1 + pieces], refs[1 + pieces : 1 + 2 * pieces]
-    down_a, down_b, out_any, x, w_in, w_down, act, out, sems, out_sems = refs[1 + 2 * pieces :]
-    blocks = x.shape[0]
-    load = pltpu.make_async_copy(x_any, x, sems.at[2, 0])
-    load.start()
+    y_ref, own_any, x_any, refs = refs[0], refs[1], refs[2], refs[3:]
+    first, second = refs[:pieces], refs[pieces : 2 * pieces]
+    down_a, down_b, out_any, x, w_in, w_down, act, out, sems, out_sems = refs[2 * pieces :]
+    y = y_ref[0]
+    blocks = x.shape[0] // X_BLOCK
+    own_rows = SPOTS * SLOTS
+    loads = [
+        pltpu.make_async_copy(own_any, x.at[pl.ds(0, own_rows)], sems.at[2, 0]),
+        pltpu.make_async_copy(x_any, x.at[pl.ds(own_rows, 3 * own_rows)], sems.at[2, 3]),
+    ]
+    for load in loads:
+        load.start()
     copies = []
     for half, parts in enumerate((first, second)):
         start = 0
@@ -201,27 +234,31 @@
         copies.append(pltpu.make_async_copy(down, w_down.at[half], sems.at[2, 1 + half]))
     for copy in copies:
         copy.start()
-    load.wait()
+    for load in loads:
+        load.wait()
     for half in range(2):
         for number in range(pieces):
             copies[half * pieces + number].wait()
         for block in range(blocks):
-            inner = jnp.dot(x[block], w_in[half], preferred_element_type=f32)
+            rows = x[block * X_BLOCK : (block + 1) * X_BLOCK, :]
+            inner = jnp.dot(rows, w_in[half], preferred_element_type=f32)
             gate = inner[:, :HALF]
             up = pltpu.roll(inner, HALF, axis=1)[:, :HALF]
             act[half, block] = (gate / (1.0 + jnp.exp(-gate)) * up).astype(bf16)
     copies[2 * pieces].wait()
     copies[2 * pieces + 1].wait()
     sends = []
-    spots = SPOTS // blocks
+    units = X_BLOCK // SLOTS
     for block in range(blocks):
         total = jnp.dot(act[0, block], w_down[0], preferred_element_type=f32)
         total = total + jnp.dot(act[1, block], w_down[1], preferred_element_type=f32)
-        out[block] = total.astype(bf16).reshape(spots, 2, 2, SLOTS, D)
-        for near in range(spots):
-            spot = block * spots + near
-            goal = out_any.at[spot // 4, :, spot % 4]
-            send = pltpu.make_async_copy(out.at[block, near], goal, out_sems.at[spot])
+        out[block] = total.astype(bf16).reshape(units, SLOTS, D)
+        for near in range(units):
+            unit = block * units + near
+            spot, ahead = origin(unit)
+            from_y = (y + ahead) & 3
+            goal = out_any.at[spot // 4, from_y & 1, spot % 4, from_y >> 1]
+            send = pltpu.make_async_copy(out.at[block, near], goal, out_sems.at[unit])
             send.start()
             sends.append(send)
     for send in sends:
@@ -266,6 +303,7 @@
     w_down,
 ):
     shape = jax.ShapeDtypeStruct
+    y = (lax.axis_index("yl") + 2 * lax.axis_index("yh")).astype(jnp.int32)[None]
     gate_up, start, moved, other = w_in[0], 0, [], []
     for count in PIECES:
         piece = lax.slice_in_dim(gate_up, start, start + count)
@@ -298,18 +336,22 @@
             shape((EXPERTS * SLOTS, ROWS), bf16),
             shape((EXPERTS * SLOTS, ROWS), bf16),
         ),
-        in_specs=[VMEM] * 2,
+        in_specs=[SMEM, VMEM, VMEM],
         out_specs=(VMEM, VMEM),
         compiler_params=params(60),
         name="route",
-    )(expert_ids[0].T, gate_codes[0].T)
+    )(y, expert_ids[0].T, gate_codes[0].T)
     per = HEADS // K_STEPS
-    mixed, share = pl.pallas_call(
+    share_shape = (ROWS + SLOTS, D)
+    mixed, *shares, own = pl.pallas_call(
         project_kernel,
         grid=(K_STEPS,),
         out_shape=(
             shape((ROWS, D), bf16),
-            shape((Y_SIZE, ROWS + SLOTS, D), bf16),
+            shape(share_shape, bf16),
+            shape(share_shape, bf16),
+            shape(share_shape, bf16),
+            shape((SPOTS, SLOTS, D), bf16),
         ),
         in_specs=[
             pl.BlockSpec((per, ROWS, HEAD_DIM), lambda i: (i, 0, 0)),
@@ -320,47 +362,62 @@
         ],
         out_specs=(
             pl.BlockSpec((ROWS, D), lambda i: (0, 0)),
-            pl.BlockSpec((Y_SIZE, ROWS + SLOTS, D), lambda i: (0, 0, 0)),
+            pl.BlockSpec(share_shape, lambda i: (0, 0)),
+            pl.BlockSpec(share_shape, lambda i: (0, 0)),
+            pl.BlockSpec(share_shape, lambda i: (0, 0)),
+            pl.BlockSpec((SPOTS, SLOTS, D), lambda i: (0, 0, 0)),
         ),
         scratch_shapes=[pltpu.VMEM((ROWS, D), f32)],
         compiler_params=params(53),
         name="project",
     )(heads, out_weight, hidden_in[0], norm_gain[None], pick)
-    shared = lax.all_to_all(share, ("yl", "yh"), split_axis=0, concat_axis=0, tiled=True)
+    arriving = []
+    for distance, share in enumerate(shares, 1):
+        arriving.append(lax.ppermute(share, AXES, moves(along_y(distance))))
+    arrived_own = lax.all_to_all(own, ("z", "x"), split_axis=0, concat_axis=0, tiled=True)
+    near, far, back = arriving
     send = pl.pallas_call(
         fill_kernel,
-        out_shape=shape((SPOTS, Y_SIZE, SLOTS, D), bf16),
-        in_specs=[VMEM],
+        out_shape=shape((SPOTS, 3, SLOTS, D), bf16),
+        in_specs=[VMEM] * 3,
         out_specs=pl.BlockSpec(memory_space=pl.ANY),
         scratch_shapes=[
-            pltpu.VMEM((Y_SIZE, SPOTS, SLOTS, D), bf16),
-            pltpu.SemaphoreType.DMA((Y_SIZE,)),
+            pltpu.VMEM((3, SPOTS, SLOTS, D), bf16),
+            pltpu.SemaphoreType.DMA((3,)),
         ],
         compiler_params=params(50),
         name="fill",
-    )(shared)
+    )(near, far, back)
     arrived = lax.all_to_all(
-        send.reshape(SPOTS, Y_SIZE * SLOTS, D), ("z", "x"), split_axis=0, concat_axis=0, tiled=True
+        send.reshape(SPOTS, 3 * SLOTS, D), ("z", "x"), split_axis=0, concat_axis=0, tiled=True
     )
     blocks = EXPERTS * SLOTS // X_BLOCK
     anywhere = pl.BlockSpec(memory_space=pl.ANY)
     results = pl.pallas_call(
         expert_kernel,
         out_shape=shape((4, 2, 4, 2, SLOTS, D), bf16),
-        in_specs=[anywhere] * (3 + 2 * len(PIECES)),
+        in_specs=[SMEM] + [anywhere] * (4 + 2 * len(PIECES)),
         out_specs=anywhere,
         scratch_shapes=[
-            pltpu.VMEM((blocks, X_BLOCK, D), bf16),
+            pltpu.VMEM((EXPERTS * SLOTS, D), bf16),
             pltpu.VMEM((2, D, 2 * HALF), bf16),
             pltpu.VMEM((2, HALF, D), bf16),
             pltpu.VMEM((2, blocks, X_BLOCK, HALF), bf16),
-            pltpu.VMEM((blocks, SPOTS // blocks, 2, 2, SLOTS, D), bf16),
+            pltpu.VMEM((blocks, X_BLOCK // SLOTS, SLOTS, D), bf16),
             pltpu.SemaphoreType.DMA((3, len(PIECES))),
-            pltpu.SemaphoreType.DMA((SPOTS,)),
+            pltpu.SemaphoreType.DMA((EXPERTS,)),
         ],
         compiler_params=params(52),
         name="experts",
-    )(arrived.reshape(blocks, X_BLOCK, D), *moved, *other, moved_down, other_down)
+    )(
+        y,
+        arrived_own.reshape(SPOTS * SLOTS, D),
+        arrived.reshape(3 * SPOTS * SLOTS, D),
+        *moved,
+        *other,
+        moved_down,
+        other_down,
+    )
     returned = lax.all_to_all(
         results.reshape(EXPERTS, SLOTS, D), PLACES, split_axis=0, concat_axis=0, tiled=True
     )

time: 285 us -> 290 us (1.018)
  blocking collectives: 102 us -> 58.6 us
  waiting for transfers between devices: 92.7 us -> 129 us
  starting transfers between devices: 30.8 us -> 39.4 us
  local copies, waits for them, and re-layouts: 9.57 us -> 12.8 us
    all_to_all x1 -> x0, blocking collectives: 45.2 us -> none  [local(): lax.all_to_all(share, ('yl', 'yh'), split_axis=0, concat_axis=0, tiled=True)]
    all_to_all x1, waiting for transfers between devices: 19 us -> 53.5 us  [local(): lax.all_to_all(attended, POSITIONS, split_axis=0, concat_axis=0, tiled=True)]
    ppermute x0 -> x3, waiting for transfers between devices: none -> 24.1 us  [local(): arriving.append(lax.ppermute(share, AXES, moves(along_y(distance))))]
    all_to_all x1 -> x2, waiting for transfers between devices: 22.5 us -> 4.65 us  [the longest x1 4.65 us: local(): lax.all_to_all(send.reshape(SPOTS, 3 * SLOTS, D), ('z', 'x'), split_axis=...]
    all_to_all x1 -> x2, starting transfers between devices: 6.3 us -> 11.5 us  [the longest x1 6.64 us: local(): lax.all_to_all(send.reshape(SPOTS, 3 * SLOTS, D), ('z', 'x'), split_axis=...]
    ppermute x0 -> x3, starting transfers between devices: none -> 4.99 us  [local(): arriving.append(lax.ppermute(share, AXES, moves(along_y(distance))))]
    all_to_all x1, waiting for transfers between devices: 19 us -> 15.4 us  [local(): lax.all_to_all(packed, POSITIONS, split_axis=0, concat_axis=0, tiled=True)]
  transfers between devices with their start and end apart: 13 -> 17, of which waited for: 7 -> 9; matrix products, arithmetic and copies ran while one was open for 2% -> 3% of each run, Pallas kernels for 6% -> 6%
where the time goes in v4:
time: 290 us; the launch traced here: 289 us
  waiting for transfers between devices  129 us (44%)
  blocking collectives  58.6 us (20%)
  Pallas kernels  49.1 us (17%)
  starting transfers between devices  39.4 us (14%)
  local copies, waits for them, and re-layouts  12.8 us (4%)
    all_to_all x1, blocking collectives, local(): lax.all_to_all(results.reshape(EXPERTS, SLOTS, D), PLACES, split_axis=0,...  58.6 us
    all_to_all x1, waiting for transfers between devices, local(): lax.all_to_all(attended, POSITIONS, split_axis=0, concat_axis=0, tiled=True)  53.5 us
    ppermute x4, waiting for transfers between devices, local(): moved.append(lax.ppermute(piece, AXES, moves(weight_target)))  28.8 us
    pallas_call x1, Pallas kernels, local(): pl.pallas_call(expert_kernel, out_shape=shape((4, 2, 4, 2, SLOTS, D), bf1...  26.4 us
    ppermute x3, waiting for transfers between devices, local(): arriving.append(lax.ppermute(share, AXES, moves(along_y(distance))))  24.1 us
    all_to_all x1, waiting for transfers between devices, local(): lax.all_to_all(packed, POSITIONS, split_axis=0, concat_axis=0, tiled=True)  15.4 us
    all_to_all x1, starting transfers between devices, local(): lax.all_to_all(packed, POSITIONS, split_axis=0, concat_axis=0, tiled=True)  7.83 us
    pallas_call x1, Pallas kernels, local(): pl.pallas_call(project_kernel, grid=(K_STEPS,), out_shape=(shape((ROWS, D...  7.71 us
  transfers between devices with their start and end apart: 17, of which 9 were waited for; matrix products, arithmetic and copies ran while one was open for 3% of the time, Pallas kernels for 6%

profile of v4, /device:TPU:1, one launch (start us, length us, event | category | flops | bytes accessed | tf_op | source)
XLA Modules:
  0.0 288.7 jit_solution(14077424934929550778)
XLA Ops:
  0.0 2.9 %pack.1 = bf16[16,400,128]{2,1,0:T(8,128)(2,1)} custom-call(bf16[128,2048]{1,0:T(8,128)(2,1)} %bitcast.35, bf16[128,2048]{1,0:T(8,128)(2,1)} %bitcast.36, bf16[128,2048]{1,0:T(8,128)(2,1)} %bitcast.37, s32[1,128]{1,0:T(1,128)} %seg_ref.1), custom_call_target="tpu_custom_call" | custom-call | tf_op jit(solution)/shard_map/pack/pallas_call | solution.py:315
  2.9 7.8 %all-to-all-start = ((bf16[16,400,128]{2,1,0:T(8,128)(2,1)}), bf16[16,400,128]{2,1,0:T(8,128)(2,1)S(1)}, u32[]{:S(2)}, u32[]{:S(2)}) async-start(bf16[16,400,128]{2,1,0:T(8,128)(2,1)} %pack.1), calls=%async_computation | async-start | bytes 3276800 | tf_op jit(solution)/shard_map/all_to_all | solution.py:323
  10.7 3.1 %collective-permute-start.11 = (bf16[704,2048]{1,0:T(8,128)(2,1)}, bf16[704,2048]{1,0:T(8,128)(2,1)}, u32[]{:S(2)}, u32[]{:S(2)}) collective-permute-start(bf16[704,2048]{1,0:T(8,128)(2,1)} %bitcast.38), channel_id=1, source_target_pairs={{0,16},{1,24},{2,18},{3,26},{4,20},{5,28},{6,22},{7,30},{8,17},{9,... | collective-permute-start | bytes 8650760 | tf_op jit(solution)/shard_map/ppermute | solution.py:313
  13.8 3.6 %slice_bitcast_fusion = bf16[960,1408]{1,0:T(8,128)(2,1)} fusion(bf16[1,2048,1408]{2,1,0:T(8,128)(2,1)} %param.20), kind=kLoop, calls=%fused_computation | loop fusion | bytes 5406720 | tf_op jit(solution)/shard_map/slice | solution.py:309
  17.4 15.4 %all-to-all-done.x_ref = bf16[16,400,128]{2,1,0:T(8,128)(2,1)S(1)} async-done(((bf16[16,400,128]{2,1,0:T(8,128)(2,1)}), bf16[16,400,128]{2,1,0:T(8,128)(2,1)S(1)}, u32[]{:S(2)}, u32[]{:S(2)}) %all-to-all-start) | async-done | bytes 1638432 | tf_op jit(solution)/shard_map/all_to_all | solution.py:323
  32.8 5.2 %attend.1 = bf16[16,128,128]{2,1,0:T(8,128)(2,1)} custom-call(bf16[16,400,128]{2,1,0:T(8,128)(2,1)S(1)} %all-to-all-done.x_ref), custom_call_target="tpu_custom_call" | custom-call | tf_op jit(solution)/shard_map/attend/pallas_call | solution.py:324
  38.0 4.3 %all-to-all-start.1 = ((bf16[16,128,128]{2,1,0:T(8,128)(2,1)}), bf16[16,128,128]{2,1,0:T(8,128)(2,1)S(1)}, u32[]{:S(2)}, u32[]{:S(2)}) async-start(bf16[16,128,128]{2,1,0:T(8,128)(2,1)} %attend.1), calls=%async_computation.1 | async-start | bytes 1048576 | tf_op jit(solution)/shard_map/all_to_all | solution.py:332
  42.9 2.0 route.1
  44.9 53.5 %all-to-all-done.1.heads_ref = bf16[16,128,128]{2,1,0:T(8,128)(2,1)S(1)} async-done(((bf16[16,128,128]{2,1,0:T(8,128)(2,1)}), bf16[16,128,128]{2,1,0:T(8,128)(2,1)S(1)}, u32[]{:S(2)}, u32[]{:S(2)}) %all-to-all-start.1) | async-done | bytes 524320 | tf_op jit(solution)/shard_map/all_to_all | solution.py:332
  100.2 7.7 %project.1 = (bf16[128,2048]{1,0:T(8,128)(2,1)S(1)}, bf16[144,2048]{1,0:T(8,128)(2,1)}, bf16[144,2048]{1,0:T(8,128)(2,1)}, bf16[144,2048]{1,0:T(8,128)(2,1)}, bf16[16,16,2048]{2,1,0:T(8,128)(2,1)}) custom-call(bf16[16,128,128]{2,1,0:T(8,128)(2,1)} %copy-done.4, bf16[2048,2048]{1,0:T(8,128)(2,1)} %weight_ref.1, bf16[128,2048]{1,0:T(8,128)(2,1)} %bitcast.34, ...), custom_call_target="tpu_custom_call" | custom-call | tf_op jit(solution)/shard_map/project/pallas_call | solution.py:346
  107.9 4.8 %all-to-all-start.2 = ((bf16[16,16,2048]{2,1,0:T(8,128)(2,1)}), bf16[16,16,2048]{2,1,0:T(8,128)(2,1)S(1)}, u32[]{:S(2)}, u32[]{:S(2)}) async-start(bf16[16,16,2048]{2,1,0:T(8,128)(2,1)} %get-tuple-element.13), calls=%async_computation.2 | async-start | bytes 2097152 | tf_op jit(solution)/shard_map/all_to_all | solution.py:377
  113.3 2.9 %collective-permute-start.1 = (bf16[144,2048]{1,0:T(8,128)(2,1)}, bf16[144,2048]{1,0:T(8,128)(2,1)S(1)}, u32[]{:S(2)}, u32[]{:S(2)}) collective-permute-start(bf16[144,2048]{1,0:T(8,128)(2,1)} %get-tuple-element.15), channel_id=1, source_target_pairs={{0,1},{1,0},{2,3},{3,2},{4,5},{5,4},{6,7},{7,6},{8,9},{9,8},{10,11... | collective-permute-start | bytes 1769480 | tf_op jit(solution)/shard_map/ppermute | solution.py:376
  116.2 1.5 collective-permute-start.2
  117.7 10.2 %collective-permute-done.near_ref = bf16[144,2048]{1,0:T(8,128)(2,1)S(1)} collective-permute-done((bf16[144,2048]{1,0:T(8,128)(2,1)}, bf16[144,2048]{1,0:T(8,128)(2,1)S(1)}, u32[]{:S(2)}, u32[]{:S(2)}) %collective-permute-start) | collective-permute-done | bytes 589856 | tf_op jit(solution)/shard_map/ppermute | solution.py:376
  127.9 13.9 %collective-permute-done.1.far_ref = bf16[144,2048]{1,0:T(8,128)(2,1)S(1)} collective-permute-done((bf16[144,2048]{1,0:T(8,128)(2,1)}, bf16[144,2048]{1,0:T(8,128)(2,1)S(1)}, u32[]{:S(2)}, u32[]{:S(2)}) %collective-permute-start.1) | collective-permute-done | bytes 589856 | tf_op jit(solution)/shard_map/ppermute | solution.py:376
  141.8 2.1 fill.1
  143.9 1.6 collective-permute-start.10
  146.6 6.6 %all-to-all-start.3 = ((bf16[16,48,2048]{2,1,0:T(8,128)(2,1)}), bf16[16,48,2048]{2,1,0:T(8,128)(2,1)}, u32[]{:S(2)}, u32[]{:S(2)}) async-start(bf16[16,48,2048]{2,1,0:T(8,128)(2,1)} %bitcast.32), calls=%async_computation.3 | async-start | bytes 6291456 | tf_op jit(solution)/shard_map/all_to_all | solution.py:391
  153.3 1.4 slice_bitcast_fusion.1
  154.7 2.9 %collective-permute-start.5 = (bf16[448,1408]{1,0:T(8,128)(2,1)S(1)}, bf16[448,1408]{1,0:T(8,128)(2,1)S(1)}, u32[]{:S(2)}, u32[]{:S(2)}) collective-permute-start(bf16[448,1408]{1,0:T(8,128)(2,1)S(1)} %slice_bitcast_fusion.1), channel_id=1, source_target_pairs={{0,16},{1,24},{2,18},{3,26},{4,20},{5,28},{6,22},{7,30},{8,17},{9,... | collective-permute-start | bytes 3784712 | tf_op jit(solution)/shard_map/ppermute | solution.py:310
  157.5 1.3 slice_bitcast_fusion.2
  159.1 1.2 slice_bitcast_fusion.3
  160.3 2.9 %collective-permute-start.3 = (bf16[256,1408]{1,0:T(8,128)(2,1)S(1)}, bf16[256,1408]{1,0:T(8,128)(2,1)S(1)}, u32[]{:S(2)}, u32[]{:S(2)}) collective-permute-start(bf16[256,1408]{1,0:T(8,128)(2,1)S(1)} %slice_bitcast_fusion.3), channel_id=1, source_target_pairs={{0,16},{1,24},{2,18},{3,26},{4,20},{5,28},{6,22},{7,30},{8,17},{9,... | collective-permute-start | bytes 2162696 | tf_op jit(solution)/shard_map/ppermute | solution.py:310
  163.2 9.7 %collective-permute-done.5.refs_5_ = bf16[448,1408]{1,0:T(8,128)(2,1)S(1)} collective-permute-done((bf16[448,1408]{1,0:T(8,128)(2,1)S(1)}, bf16[448,1408]{1,0:T(8,128)(2,1)S(1)}, u32[]{:S(2)}, u32[]{:S(2)}) %collective-permute-start.5) | collective-permute-done | bytes 1261600 | tf_op jit(solution)/shard_map/ppermute | solution.py:310
  172.9 11.6 %collective-permute-done.4.refs_4_ = bf16[384,1408]{1,0:T(8,128)(2,1)S(1)} collective-permute-done((bf16[384,1408]{1,0:T(8,128)(2,1)S(1)}, bf16[384,1408]{1,0:T(8,128)(2,1)S(1)}, u32[]{:S(2)}, u32[]{:S(2)}) %collective-permute-start.4) | collective-permute-done | bytes 1081376 | tf_op jit(solution)/shard_map/ppermute | solution.py:310
  184.4 7.5 %collective-permute-done.3.refs_3_ = bf16[256,1408]{1,0:T(8,128)(2,1)S(1)} collective-permute-done((bf16[256,1408]{1,0:T(8,128)(2,1)S(1)}, bf16[256,1408]{1,0:T(8,128)(2,1)S(1)}, u32[]{:S(2)}, u32[]{:S(2)}) %collective-permute-start.3) | collective-permute-done | bytes 720928 | tf_op jit(solution)/shard_map/ppermute | solution.py:310
  192.0 2.2 collective-permute-done.7.refs_7_
  195.2 1.0 copy-done.6
  196.2 4.6 %all-to-all-done.3 = bf16[16,48,2048]{2,1,0:T(8,128)(2,1)} async-done(((bf16[16,48,2048]{2,1,0:T(8,128)(2,1)}), bf16[16,48,2048]{2,1,0:T(8,128)(2,1)}, u32[]{:S(2)}, u32[]{:S(2)}) %all-to-all-start.3) | async-done | bytes 3145760 | tf_op jit(solution)/shard_map/all_to_all | solution.py:391
  200.9 26.4 %experts.1 = bf16[4,2,4,2,16,2048]{5,4,3,2,1,0:T(8,128)(2,1)} custom-call(s32[1]{0:T(128)} %bitcast.y_ref.refs_0_, bf16[256,2048]{1,0:T(8,128)(2,1)} %bitcast.33, bf16[768,2048]{1,0:T(8,128)(2,1)} %bitcast.10.refs_2_, bf16[256,1408]{1,0:T(8,128)(2,1)S(1)} %collective-permute-done.3.refs_3_, bf16[384,1408]{1,0:T(8,128)(2,1)} %copy-done.7, ...), custom_call_target="tpu_custom_call" | custom-call | tf_op jit(solution)/shard_map/experts/pallas_call | solution.py:396
  227.3 58.6 %all_to_all.25 = bf16[64,16,2048]{2,1,0:T(8,128)(2,1)S(1)} all-to-all(bf16[64,16,2048]{2,1,0:T(8,128)(2,1)} %bitcast.31), channel_id=1, replica_groups=mesh['z'=4,'yl'=2,'c'=2,'x'=4,'yh'=2] {'z','yl','x','yh'}, dimensions={0} | all-to-all | bytes 8388608 | tf_op jit(solution)/shard_map/all_to_all | solution.py:421
  285.9 2.8 combine.1
  (37 shorter events, 5.3 us)
Async XLA Ops:
  2.9 29.9 %all-to-all-start = ((bf16[16,400,128]{2,1,0:T(8,128)(2,1)}), bf16[16,400,128]{2,1,0:T(8,128)(2,1)S(1)}, u32[]{:S(2)}, u32[]{:S(2)}) async-start(bf16[16,400,128]{2,1,0:T(8,128)(2,1)} %pack.1), calls=%async_computation | async-start | bytes 3276800 | tf_op jit(solution)/shard_map/all_to_all | solution.py:323
  10.7 134.8 %collective-permute-start.11 = (bf16[704,2048]{1,0:T(8,128)(2,1)}, bf16[704,2048]{1,0:T(8,128)(2,1)}, u32[]{:S(2)}, u32[]{:S(2)}) collective-permute-start(bf16[704,2048]{1,0:T(8,128)(2,1)} %bitcast.38), channel_id=1, source_target_pairs={{0,16},{1,24},{2,18},{3,26},{4,20},{5,28},{6,22},{7,30},{8,17},{9,... | collective-permute-start | bytes 8650760 | tf_op jit(solution)/shard_map/ppermute | solution.py:313
  17.4 24.9 %copy-start.9 = (s32[1,128,6]{1,0,2:T(1,128)S(1)}, s32[1,128,6]{1,0,2:T(1,128)}, u32[]{:S(2)}) copy-start(s32[1,128,6]{1,0,2:T(1,128)} %param.19) | copy-start | bytes 9220
  17.4 24.9 %copy-start.10 = (s32[1,128,6]{1,0,2:T(1,128)S(1)}, s32[1,128,6]{1,0,2:T(1,128)}, u32[]{:S(2)}) copy-start(s32[1,128,6]{1,0,2:T(1,128)} %param.18) | copy-start | bytes 9220
  17.4 81.8 %copy-start.2 = (f32[2048]{0:T(1024)S(1)}, f32[2048]{0:T(1024)}, u32[]{:S(2)}) copy-start(f32[2048]{0:T(1024)} %param.17) | copy-start | bytes 24580
  17.4 126.5 %collective-permute-start.6 = (bf16[960,1408]{1,0:T(8,128)(2,1)}, bf16[960,1408]{1,0:T(8,128)(2,1)}, u32[]{:S(2)}, u32[]{:S(2)}) collective-permute-start(bf16[960,1408]{1,0:T(8,128)(2,1)} %slice_bitcast_fusion), channel_id=1, source_target_pairs={{0,16},{1,24},{2,18},{3,26},{4,20},{5,28},{6,22},{7,30},{8,17},{9,... | collective-permute-start | bytes 8110088 | tf_op jit(solution)/shard_map/ppermute | solution.py:310
  38.0 60.4 %all-to-all-start.1 = ((bf16[16,128,128]{2,1,0:T(8,128)(2,1)}), bf16[16,128,128]{2,1,0:T(8,128)(2,1)S(1)}, u32[]{:S(2)}, u32[]{:S(2)}) async-start(bf16[16,128,128]{2,1,0:T(8,128)(2,1)} %attend.1), calls=%async_computation.1 | async-start | bytes 1048576 | tf_op jit(solution)/shard_map/all_to_all | solution.py:332
  98.4 0.8 copy-start.4
  99.2 1.0 copy-start
  107.9 37.8 %all-to-all-start.2 = ((bf16[16,16,2048]{2,1,0:T(8,128)(2,1)}), bf16[16,16,2048]{2,1,0:T(8,128)(2,1)S(1)}, u32[]{:S(2)}, u32[]{:S(2)}) async-start(bf16[16,16,2048]{2,1,0:T(8,128)(2,1)} %get-tuple-element.13), calls=%async_computation.2 | async-start | bytes 2097152 | tf_op jit(solution)/shard_map/all_to_all | solution.py:377
  112.7 15.2 %collective-permute-start = (bf16[144,2048]{1,0:T(8,128)(2,1)}, bf16[144,2048]{1,0:T(8,128)(2,1)S(1)}, u32[]{:S(2)}, u32[]{:S(2)}) collective-permute-start(bf16[144,2048]{1,0:T(8,128)(2,1)} %get-tuple-element.14), channel_id=1, source_target_pairs={{0,16},{1,17},{2,18},{3,19},{4,20},{5,21},{6,22},{7,23},{8,24},{9,... | collective-permute-start | bytes 1769480 | tf_op jit(solution)/shard_map/ppermute | solution.py:376
  113.3 28.5 %collective-permute-start.1 = (bf16[144,2048]{1,0:T(8,128)(2,1)}, bf16[144,2048]{1,0:T(8,128)(2,1)S(1)}, u32[]{:S(2)}, u32[]{:S(2)}) collective-permute-start(bf16[144,2048]{1,0:T(8,128)(2,1)} %get-tuple-element.15), channel_id=1, source_target_pairs={{0,1},{1,0},{2,3},{3,2},{4,5},{5,4},{6,7},{7,6},{8,9},{9,8},{10,11... | collective-permute-start | bytes 1769480 | tf_op jit(solution)/shard_map/ppermute | solution.py:376
  116.2 25.6 %collective-permute-start.2 = (bf16[144,2048]{1,0:T(8,128)(2,1)}, bf16[144,2048]{1,0:T(8,128)(2,1)S(1)}, u32[]{:S(2)}, u32[]{:S(2)}) collective-permute-start(bf16[144,2048]{1,0:T(8,128)(2,1)} %get-tuple-element.16), channel_id=1, source_target_pairs={{0,17},{1,16},{2,19},{3,18},{4,21},{5,20},{6,23},{7,22},{8,25},{9,... | collective-permute-start | bytes 1769480 | tf_op jit(solution)/shard_map/ppermute | solution.py:376
  143.9 52.3 %collective-permute-start.10 = (bf16[960,1408]{1,0:T(8,128)(2,1)}, bf16[960,1408]{1,0:T(8,128)(2,1)}, u32[]{:S(2)}, u32[]{:S(2)}) collective-permute-start(bf16[960,1408]{1,0:T(8,128)(2,1)} %collective-permute-done.6.refs_6_), channel_id=1, source_target_pairs={{0,8},{1,9},{2,10},{3,11},{4,12},{5,13},{6,14},{7,15},{8,0},{9,1},... | collective-permute-start | bytes 8110088 | tf_op jit(solution)/shard_map/ppermute | solution.py:311
  145.5 55.3 %collective-permute-start.12 = (bf16[704,2048]{1,0:T(8,128)(2,1)}, bf16[704,2048]{1,0:T(8,128)(2,1)}, u32[]{:S(2)}, u32[]{:S(2)}) collective-permute-start(bf16[704,2048]{1,0:T(8,128)(2,1)} %collective-permute-done.11.refs_11_), channel_id=1, source_target_pairs={{0,8},{1,9},{2,10},{3,11},{4,12},{5,13},{6,14},{7,15},{8,0},{9,1},... | collective-permute-start | bytes 8650760 | tf_op jit(solution)/shard_map/ppermute | solution.py:314
  145.6 1.0 copy-start.3
  146.6 54.3 %all-to-all-start.3 = ((bf16[16,48,2048]{2,1,0:T(8,128)(2,1)}), bf16[16,48,2048]{2,1,0:T(8,128)(2,1)}, u32[]{:S(2)}, u32[]{:S(2)}) async-start(bf16[16,48,2048]{2,1,0:T(8,128)(2,1)} %bitcast.32), calls=%async_computation.3 | async-start | bytes 6291456 | tf_op jit(solution)/shard_map/all_to_all | solution.py:391
  154.7 18.2 %collective-permute-start.5 = (bf16[448,1408]{1,0:T(8,128)(2,1)S(1)}, bf16[448,1408]{1,0:T(8,128)(2,1)S(1)}, u32[]{:S(2)}, u32[]{:S(2)}) collective-permute-start(bf16[448,1408]{1,0:T(8,128)(2,1)S(1)} %slice_bitcast_fusion.1), channel_id=1, source_target_pairs={{0,16},{1,24},{2,18},{3,26},{4,20},{5,28},{6,22},{7,30},{8,17},{9,... | collective-permute-start | bytes 3784712 | tf_op jit(solution)/shard_map/ppermute | solution.py:310
  158.9 25.6 %collective-permute-start.4 = (bf16[384,1408]{1,0:T(8,128)(2,1)S(1)}, bf16[384,1408]{1,0:T(8,128)(2,1)S(1)}, u32[]{:S(2)}, u32[]{:S(2)}) collective-permute-start(bf16[384,1408]{1,0:T(8,128)(2,1)S(1)} %slice_bitcast_fusion.2), channel_id=1, source_target_pairs={{0,16},{1,24},{2,18},{3,26},{4,20},{5,28},{6,22},{7,30},{8,17},{9,... | collective-permute-start | bytes 3244040 | tf_op jit(solution)/shard_map/ppermute | solution.py:310
  160.3 31.7 %collective-permute-start.3 = (bf16[256,1408]{1,0:T(8,128)(2,1)S(1)}, bf16[256,1408]{1,0:T(8,128)(2,1)S(1)}, u32[]{:S(2)}, u32[]{:S(2)}) collective-permute-start(bf16[256,1408]{1,0:T(8,128)(2,1)S(1)} %slice_bitcast_fusion.3), channel_id=1, source_target_pairs={{0,16},{1,24},{2,18},{3,26},{4,20},{5,28},{6,22},{7,30},{8,17},{9,... | collective-permute-start | bytes 2162696 | tf_op jit(solution)/shard_map/ppermute | solution.py:310
  172.9 28.0 %copy-start.5 = (bf16[448,1408]{1,0:T(8,128)(2,1)}, bf16[448,1408]{1,0:T(8,128)(2,1)S(1)}, u32[]{:S(2)}) copy-start(bf16[448,1408]{1,0:T(8,128)(2,1)S(1)} %collective-permute-done.5.refs_5_) | copy-start | bytes 3784708
  172.9 21.3 %collective-permute-start.9 = (bf16[448,1408]{1,0:T(8,128)(2,1)S(1)}, bf16[448,1408]{1,0:T(8,128)(2,1)S(1)}, u32[]{:S(2)}, u32[]{:S(2)}) collective-permute-start(bf16[448,1408]{1,0:T(8,128)(2,1)S(1)} %collective-permute-done.5.refs_5_), channel_id=1, source_target_pairs={{0,8},{1,9},{2,10},{3,11},{4,12},{5,13},{6,14},{7,15},{8,0},{9,1},... | collective-permute-start | bytes 3784712 | tf_op jit(solution)/shard_map/ppermute | solution.py:311
  184.4 9.7 %copy-start.7 = (bf16[384,1408]{1,0:T(8,128)(2,1)}, bf16[384,1408]{1,0:T(8,128)(2,1)S(1)}, u32[]{:S(2)}) copy-start(bf16[384,1408]{1,0:T(8,128)(2,1)S(1)} %collective-permute-done.4.refs_4_) | copy-start | bytes 3244036
  184.4 9.7 %collective-permute-start.8 = (bf16[384,1408]{1,0:T(8,128)(2,1)S(1)}, bf16[384,1408]{1,0:T(8,128)(2,1)S(1)}, u32[]{:S(2)}, u32[]{:S(2)}) collective-permute-start(bf16[384,1408]{1,0:T(8,128)(2,1)S(1)} %collective-permute-done.4.refs_4_), channel_id=1, source_target_pairs={{0,8},{1,9},{2,10},{3,11},{4,12},{5,13},{6,14},{7,15},{8,0},{9,1},... | collective-permute-start | bytes 3244040 | tf_op jit(solution)/shard_map/ppermute | solution.py:311
  192.0 2.2 collective-permute-start.7
  194.2 1.0 copy-start.8
  195.2 1.0 copy-start.6
  227.3 58.6 %copy-start.1 = (bf16[1024,128]{1,0:T(8,128)(2,1)S(1)}, bf16[1024,128]{1,0:T(8,128)(2,1)}, u32[]{:S(2)}) copy-start(bf16[1024,128]{1,0:T(8,128)(2,1)} %get-tuple-element.17.weight_ref) | copy-start | bytes 786436

commit v5 on v4

--- a/solution.py
+++ b/solution.py
@@ -20,7 +20,7 @@
 SEG_ROWS = 16
 PACK_ROWS = 3 * ROWS + SEG_ROWS
 Q_BLOCK = 256
-X_BLOCK = 512
+X_BLOCK = 256
 PIECES = (256, 384, 448, 960)
 SPOTS = 16
 Y_SIZE = 4
@@ -209,49 +209,37 @@
     return (unit - SPOTS) // 3, (3, 1, 2)[(unit - SPOTS) % 3]
 
 
-def expert_kernel(*refs):
+def inner_kernel(own_ref, rest_ref, *refs):
     pieces = len(PIECES)
-    y_ref, own_any, x_any, refs = refs[0], refs[1], refs[2], refs[3:]
-    first, second = refs[:pieces], refs[pieces : 2 * pieces]
-    down_a, down_b, out_any, x, w_in, w_down, act, out, sems, out_sems = refs[2 * pieces :]
-    y = y_ref[0]
-    blocks = x.shape[0] // X_BLOCK
-    own_rows = SPOTS * SLOTS
-    loads = [
-        pltpu.make_async_copy(own_any, x.at[pl.ds(0, own_rows)], sems.at[2, 0]),
-        pltpu.make_async_copy(x_any, x.at[pl.ds(own_rows, 3 * own_rows)], sems.at[2, 3]),
-    ]
-    for load in loads:
-        load.start()
-    copies = []
-    for half, parts in enumerate((first, second)):
-        start = 0
-        for number, (part, count) in enumerate(zip(parts, PIECES)):
-            goal = w_in.at[half, pl.ds(start, count)]
-            copies.append(pltpu.make_async_copy(part, goal, sems.at[half, number]))
-            start += count
-    for half, down in enumerate((down_a, down_b)):
-        copies.append(pltpu.make_async_copy(down, w_down.at[half], sems.at[2, 1 + half]))
+    parts, (act, w_in, sems) = refs[:pieces], refs[pieces:]
+    copies, start = [], 0
+    for number, (part, count) in enumerate(zip(parts, PIECES)):
+        goal = w_in.at[pl.ds(start, count)]
+        copies.append(pltpu.make_async_copy(part, goal, sems.at[number]))
+        start += count
     for copy in copies:
         copy.start()
-    for load in loads:
-        load.wait()
-    for half in range(2):
-        for number in range(pieces):
-            copies[half * pieces + number].wait()
-        for block in range(blocks):
-            rows = x[block * X_BLOCK : (block + 1) * X_BLOCK, :]
-            inner = jnp.dot(rows, w_in[half], preferred_element_type=f32)
-            gate = inner[:, :HALF]
-            up = pltpu.roll(inner, HALF, axis=1)[:, :HALF]
-            act[half, block] = (gate / (1.0 + jnp.exp(-gate)) * up).astype(bf16)
-    copies[2 * pieces].wait()
-    copies[2 * pieces + 1].wait()
+    for copy in copies:
+        copy.wait()
+    for block in range(EXPERTS * SLOTS // X_BLOCK):
+        first = (block - 1) * X_BLOCK
+        rows = own_ref[...] if block == 0 else rest_ref[first : first + X_BLOCK, :]
+        inner = jnp.dot(rows, w_in[...], preferred_element_type=f32)
+        gate = inner[:, :HALF]
+        up = pltpu.roll(inner, HALF, axis=1)[:, :HALF]
+        act[block * X_BLOCK : (block + 1) * X_BLOCK, :] = (
+            gate / (1.0 + jnp.exp(-gate)) * up
+        ).astype(bf16)
+
+
+def down_kernel(y_ref, act_a, act_b, down_a, down_b, out_any, out, out_sems):
+    y = y_ref[0]
     sends = []
     units = X_BLOCK // SLOTS
-    for block in range(blocks):
-        total = jnp.dot(act[0, block], w_down[0], preferred_element_type=f32)
-        total = total + jnp.dot(act[1, block], w_down[1], preferred_element_type=f32)
+    for block in range(EXPERTS * SLOTS // X_BLOCK):
+        span = slice(block * X_BLOCK, (block + 1) * X_BLOCK)
+        total = jnp.dot(act_a[span, :], down_a[...], preferred_element_type=f32)
+        total = total + jnp.dot(act_b[span, :], down_b[...], preferred_element_type=f32)
         out[block] = total.astype(bf16).reshape(units, SLOTS, D)
         for near in range(units):
             unit = block * units + near
@@ -393,31 +381,38 @@
     )
     blocks = EXPERTS * SLOTS // X_BLOCK
     anywhere = pl.BlockSpec(memory_space=pl.ANY)
+
+    def inner(parts):
+        return pl.pallas_call(
+            inner_kernel,
+            out_shape=shape((EXPERTS * SLOTS, HALF), bf16),
+            in_specs=[VMEM, VMEM] + [anywhere] * len(PIECES),
+            out_specs=VMEM,
+            scratch_shapes=[
+                pltpu.VMEM((D, 2 * HALF), bf16),
+                pltpu.SemaphoreType.DMA((len(PIECES),)),
+            ],
+            compiler_params=params(32),
+        )(
+            arrived_own.reshape(SPOTS * SLOTS, D),
+            arrived.reshape(3 * SPOTS * SLOTS, D),
+            *parts,
+        )
+
+    act_a = inner(moved)
+    act_b = inner(other)
     results = pl.pallas_call(
-        expert_kernel,
+        down_kernel,
         out_shape=shape((4, 2, 4, 2, SLOTS, D), bf16),
-        in_specs=[SMEM] + [anywhere] * (4 + 2 * len(PIECES)),
+        in_specs=[SMEM] + [VMEM] * 4,
         out_specs=anywhere,
         scratch_shapes=[
-            pltpu.VMEM((EXPERTS * SLOTS, D), bf16),
-            pltpu.VMEM((2, D, 2 * HALF), bf16),
-            pltpu.VMEM((2, HALF, D), bf16),
-            pltpu.VMEM((2, blocks, X_BLOCK, HALF), bf16),
             pltpu.VMEM((blocks, X_BLOCK // SLOTS, SLOTS, D), bf16),
-            pltpu.SemaphoreType.DMA((3, len(PIECES))),
             pltpu.SemaphoreType.DMA((EXPERTS,)),
         ],
-        compiler_params=params(52),
-        name="experts",
-    )(
-        y,
-        arrived_own.reshape(SPOTS * SLOTS, D),
-        arrived.reshape(3 * SPOTS * SLOTS, D),
-        *moved,
-        *other,
-        moved_down,
-        other_down,
-    )
+        compiler_params=params(32),
+        name="down",
+    )(y, act_a, act_b, moved_down, other_down)
     returned = lax.all_to_all(
         results.reshape(EXPERTS, SLOTS, D), PLACES, split_axis=0, concat_axis=0, tiled=True
     )

time: 290 us -> 301 us (1.038)
  Pallas kernels: 49.1 us -> 58.1 us
    pallas_call x1 -> x3, Pallas kernels: 26.4 us -> 35.3 us  [the longest x2 19.1 us: inner(): pl.pallas_call(inner_kernel, out_shape=shape((EXPERTS * SLOTS, HALF), bf1...]
    all_to_all x1, waiting for transfers between devices: 4.65 us -> 8.88 us  [local(): lax.all_to_all(send.reshape(SPOTS, 3 * SLOTS, D), ('z', 'x'), split_axis=...]
  transfers between devices with their start and end apart: 17 -> 17, of which waited for: 9 -> 8; matrix products, arithmetic and copies ran while one was open for 3% -> 3% of each run, Pallas kernels for 6% -> 12%
where the time goes in v5:
time: 301 us; the launch traced here: 299 us
  waiting for transfers between devices  131 us (44%)
  blocking collectives  58.4 us (19%)
  Pallas kernels  58.1 us (19%)
  starting transfers between devices  39.4 us (13%)
  local copies, waits for them, and re-layouts  12.8 us (4%)
    all_to_all x1, blocking collectives, local(): lax.all_to_all(results.reshape(EXPERTS, SLOTS, D), PLACES, split_axis=0,...  58.4 us
    all_to_all x1, waiting for transfers between devices, local(): lax.all_to_all(attended, POSITIONS, split_axis=0, concat_axis=0, tiled=True)  53.5 us
    ppermute x4, waiting for transfers between devices, local(): moved.append(lax.ppermute(piece, AXES, moves(weight_target)))  28.8 us
    ppermute x3, waiting for transfers between devices, local(): arriving.append(lax.ppermute(share, AXES, moves(along_y(distance))))  24.1 us
    pallas_call x2, Pallas kernels, inner(): pl.pallas_call(inner_kernel, out_shape=shape((EXPERTS * SLOTS, HALF), bf1...  19.1 us
    pallas_call x1, Pallas kernels, local(): pl.pallas_call(down_kernel, out_shape=shape((4, 2, 4, 2, SLOTS, D), bf16)...  16.2 us
    all_to_all x1, waiting for transfers between devices, local(): lax.all_to_all(packed, POSITIONS, split_axis=0, concat_axis=0, tiled=True)  15.4 us
    all_to_all x1, waiting for transfers between devices, local(): lax.all_to_all(send.reshape(SPOTS, 3 * SLOTS, D), ('z', 'x'), split_axis=...  8.88 us
  transfers between devices with their start and end apart: 17, of which 8 were waited for; matrix products, arithmetic and copies ran while one was open for 3% of the time, Pallas kernels for 12%

profile of v5, /device:TPU:1, one launch (start us, length us, event | category | flops | bytes accessed | tf_op | source)
XLA Modules:
  0.0 299.4 jit_solution(4365059975703720134)
XLA Ops:
  0.0 2.9 pack.1
  2.9 7.8 %all-to-all-start = ((bf16[16,400,128]{2,1,0:T(8,128)(2,1)}), bf16[16,400,128]{2,1,0:T(8,128)(2,1)S(1)}, u32[]{:S(2)}, u32[]{:S(2)}) async-start(bf16[16,400,128]{2,1,0:T(8,128)(2,1)} %pack.1), calls=%async_computation | async-start | bytes 3276800 | tf_op jit(solution)/shard_map/all_to_all | solution.py:311
  10.7 3.1 %collective-permute-start.11 = (bf16[704,2048]{1,0:T(8,128)(2,1)}, bf16[704,2048]{1,0:T(8,128)(2,1)}, u32[]{:S(2)}, u32[]{:S(2)}) collective-permute-start(bf16[704,2048]{1,0:T(8,128)(2,1)} %bitcast.41), channel_id=1, source_target_pairs={{0,16},{1,24},{2,18},{3,26},{4,20},{5,28},{6,22},{7,30},{8,17},{9,... | collective-permute-start | bytes 8650760 | tf_op jit(solution)/shard_map/ppermute | solution.py:301
  13.8 3.5 %slice_bitcast_fusion = bf16[960,1408]{1,0:T(8,128)(2,1)} fusion(bf16[1,2048,1408]{2,1,0:T(8,128)(2,1)} %param.20), kind=kLoop, calls=%fused_computation | loop fusion | bytes 5406720 | tf_op jit(solution)/shard_map/slice | solution.py:297
  17.3 15.4 %all-to-all-done.x_ref = bf16[16,400,128]{2,1,0:T(8,128)(2,1)S(1)} async-done(((bf16[16,400,128]{2,1,0:T(8,128)(2,1)}), bf16[16,400,128]{2,1,0:T(8,128)(2,1)S(1)}, u32[]{:S(2)}, u32[]{:S(2)}) %all-to-all-start) | async-done | bytes 1638432 | tf_op jit(solution)/shard_map/all_to_all | solution.py:311
  32.8 5.2 %attend.1 = bf16[16,128,128]{2,1,0:T(8,128)(2,1)} custom-call(bf16[16,400,128]{2,1,0:T(8,128)(2,1)S(1)} %all-to-all-done.x_ref), custom_call_target="tpu_custom_call" | custom-call | tf_op jit(solution)/shard_map/attend/pallas_call | solution.py:312
  38.0 4.3 %all-to-all-start.1 = ((bf16[16,128,128]{2,1,0:T(8,128)(2,1)}), bf16[16,128,128]{2,1,0:T(8,128)(2,1)S(1)}, u32[]{:S(2)}, u32[]{:S(2)}) async-start(bf16[16,128,128]{2,1,0:T(8,128)(2,1)} %attend.1), calls=%async_computation.1 | async-start | bytes 1048576 | tf_op jit(solution)/shard_map/all_to_all | solution.py:320
  42.9 2.0 route.1
  44.9 53.5 %all-to-all-done.1.heads_ref = bf16[16,128,128]{2,1,0:T(8,128)(2,1)S(1)} async-done(((bf16[16,128,128]{2,1,0:T(8,128)(2,1)}), bf16[16,128,128]{2,1,0:T(8,128)(2,1)S(1)}, u32[]{:S(2)}, u32[]{:S(2)}) %all-to-all-start.1) | async-done | bytes 524320 | tf_op jit(solution)/shard_map/all_to_all | solution.py:320
  100.1 7.8 %project.1 = (bf16[128,2048]{1,0:T(8,128)(2,1)S(1)}, bf16[144,2048]{1,0:T(8,128)(2,1)}, bf16[144,2048]{1,0:T(8,128)(2,1)}, bf16[144,2048]{1,0:T(8,128)(2,1)}, bf16[16,16,2048]{2,1,0:T(8,128)(2,1)}) custom-call(bf16[16,128,128]{2,1,0:T(8,128)(2,1)} %copy-done.7, bf16[2048,2048]{1,0:T(8,128)(2,1)} %weight_ref.1, bf16[128,2048]{1,0:T(8,128)(2,1)} %bitcast.37, ...), custom_call_target="tpu_custom_call" | custom-call | tf_op jit(solution)/shard_map/project/pallas_call | solution.py:334
  108.7 4.8 %all-to-all-start.2 = ((bf16[16,16,2048]{2,1,0:T(8,128)(2,1)}), bf16[16,16,2048]{2,1,0:T(8,128)(2,1)S(1)}, u32[]{:S(2)}, u32[]{:S(2)}) async-start(bf16[16,16,2048]{2,1,0:T(8,128)(2,1)} %get-tuple-element.13), calls=%async_computation.2 | async-start | bytes 2097152 | tf_op jit(solution)/shard_map/all_to_all | solution.py:365
  114.1 2.9 collective-permute-start.1
  117.0 1.5 collective-permute-start.2
  118.5 10.2 %collective-permute-done.near_ref = bf16[144,2048]{1,0:T(8,128)(2,1)S(1)} collective-permute-done((bf16[144,2048]{1,0:T(8,128)(2,1)}, bf16[144,2048]{1,0:T(8,128)(2,1)S(1)}, u32[]{:S(2)}, u32[]{:S(2)}) %collective-permute-start) | collective-permute-done | bytes 589856 | tf_op jit(solution)/shard_map/ppermute | solution.py:364
  128.7 13.9 %collective-permute-done.1.far_ref = bf16[144,2048]{1,0:T(8,128)(2,1)S(1)} collective-permute-done((bf16[144,2048]{1,0:T(8,128)(2,1)}, bf16[144,2048]{1,0:T(8,128)(2,1)S(1)}, u32[]{:S(2)}, u32[]{:S(2)}) %collective-permute-start.1) | collective-permute-done | bytes 589856 | tf_op jit(solution)/shard_map/ppermute | solution.py:364
  142.6 2.1 fill.1
  144.7 1.6 collective-permute-start.10
  147.5 6.6 %all-to-all-start.3 = ((bf16[16,48,2048]{2,1,0:T(8,128)(2,1)}), bf16[16,48,2048]{2,1,0:T(8,128)(2,1)S(1)}, u32[]{:S(2)}, u32[]{:S(2)}) async-start(bf16[16,48,2048]{2,1,0:T(8,128)(2,1)} %bitcast.36), calls=%async_computation.3 | async-start | bytes 6291456 | tf_op jit(solution)/shard_map/all_to_all | solution.py:379
  154.1 1.4 slice_bitcast_fusion.1
  155.5 2.9 collective-permute-start.5
  158.3 1.3 slice_bitcast_fusion.2
  161.1 2.9 collective-permute-start.3
  163.9 9.6 %collective-permute-done.5.refs_2_ = bf16[448,1408]{1,0:T(8,128)(2,1)} collective-permute-done((bf16[448,1408]{1,0:T(8,128)(2,1)S(1)}, bf16[448,1408]{1,0:T(8,128)(2,1)}, u32[]{:S(2)}, u32[]{:S(2)}) %collective-permute-start.5) | collective-permute-done | bytes 1261600 | tf_op jit(solution)/shard_map/ppermute | solution.py:298
  173.5 11.6 %collective-permute-done.4.refs_1_ = bf16[384,1408]{1,0:T(8,128)(2,1)} collective-permute-done((bf16[384,1408]{1,0:T(8,128)(2,1)S(1)}, bf16[384,1408]{1,0:T(8,128)(2,1)}, u32[]{:S(2)}, u32[]{:S(2)}) %collective-permute-start.4) | collective-permute-done | bytes 1081376 | tf_op jit(solution)/shard_map/ppermute | solution.py:298
  185.1 7.6 %collective-permute-done.3.refs_0_ = bf16[256,1408]{1,0:T(8,128)(2,1)} collective-permute-done((bf16[256,1408]{1,0:T(8,128)(2,1)S(1)}, bf16[256,1408]{1,0:T(8,128)(2,1)}, u32[]{:S(2)}, u32[]{:S(2)}) %collective-permute-start.3) | collective-permute-done | bytes 720928 | tf_op jit(solution)/shard_map/ppermute | solution.py:298
  192.7 8.9 %all-to-all-done.3 = bf16[16,48,2048]{2,1,0:T(8,128)(2,1)S(1)} async-done(((bf16[16,48,2048]{2,1,0:T(8,128)(2,1)}), bf16[16,48,2048]{2,1,0:T(8,128)(2,1)S(1)}, u32[]{:S(2)}, u32[]{:S(2)}) %all-to-all-start.3) | async-done | bytes 3145760 | tf_op jit(solution)/shard_map/all_to_all | solution.py:379
  201.6 1.2 copy-done.1
  202.8 9.5 %shard_map.109.act_a = bf16[1024,704]{1,0:T(8,128)(2,1)S(1)} custom-call(bf16[256,2048]{1,0:T(8,128)(2,1)S(1)} %bitcast.33, bf16[768,2048]{1,0:T(8,128)(2,1)S(1)} %bitcast.29, bf16[256,1408]{1,0:T(8,128)(2,1)} %collective-permute-done.3.refs_0_, bf16[384,1408]{1,0:T(8,128)(2,1)} %collective-permute-done.4.refs_1_, ...), custom_call_target="tpu_custom_call" | custom-call | tf_op jit(solution)/shard_map/pallas_call | solution.py:386
  212.4 9.6 %shard_map.110.act_b = bf16[1024,704]{1,0:T(8,128)(2,1)S(1)} custom-call(bf16[256,2048]{1,0:T(8,128)(2,1)S(1)} %bitcast.34, bf16[768,2048]{1,0:T(8,128)(2,1)S(1)} %bitcast.30, bf16[256,1408]{1,0:T(8,128)(2,1)} %collective-permute-done.7.refs_0_, bf16[384,1408]{1,0:T(8,128)(2,1)} %collective-permute-done.8.refs_1_, ...), custom_call_target="tpu_custom_call" | custom-call | tf_op jit(solution)/shard_map/pallas_call | solution.py:386
  222.0 16.2 %down.1 = bf16[4,2,4,2,16,2048]{5,4,3,2,1,0:T(8,128)(2,1)S(1)} custom-call(s32[1]{0:T(128)} %bitcast.y_ref, bf16[1024,704]{1,0:T(8,128)(2,1)S(1)} %shard_map.109.act_a, bf16[1024,704]{1,0:T(8,128)(2,1)S(1)} %shard_map.110.act_b, bf16[704,2048]{1,0:T(8,128)(2,1)} %collective-permute-done.11.down_a, bf16[704,2048]{1,0:T(8,128)(2,1)} %collective-permute-done.12.down_b), custom_call_target="tpu_custom_call" | custom-call | tf_op jit(solution)/shard_map/down/pallas_call | solution.py:404
  238.2 58.4 %all_to_all.25 = bf16[64,16,2048]{2,1,0:T(8,128)(2,1)S(1)} all-to-all(bf16[64,16,2048]{2,1,0:T(8,128)(2,1)S(1)} %bitcast.31), channel_id=1, replica_groups=mesh['z'=4,'yl'=2,'c'=2,'x'=4,'yh'=2] {'z','yl','x','yh'}, dimensions={0} | all-to-all | bytes 8388608 | tf_op jit(solution)/shard_map/all_to_all | solution.py:416
  296.6 2.8 combine.1
  (37 shorter events, 6.3 us)
Async XLA Ops:
  2.9 29.9 %all-to-all-start = ((bf16[16,400,128]{2,1,0:T(8,128)(2,1)}), bf16[16,400,128]{2,1,0:T(8,128)(2,1)S(1)}, u32[]{:S(2)}, u32[]{:S(2)}) async-start(bf16[16,400,128]{2,1,0:T(8,128)(2,1)} %pack.1), calls=%async_computation | async-start | bytes 3276800 | tf_op jit(solution)/shard_map/all_to_all | solution.py:311
  10.7 135.6 %collective-permute-start.11 = (bf16[704,2048]{1,0:T(8,128)(2,1)}, bf16[704,2048]{1,0:T(8,128)(2,1)}, u32[]{:S(2)}, u32[]{:S(2)}) collective-permute-start(bf16[704,2048]{1,0:T(8,128)(2,1)} %bitcast.41), channel_id=1, source_target_pairs={{0,16},{1,24},{2,18},{3,26},{4,20},{5,28},{6,22},{7,30},{8,17},{9,... | collective-permute-start | bytes 8650760 | tf_op jit(solution)/shard_map/ppermute | solution.py:301
  17.3 25.0 %copy-start.8 = (s32[1,128,6]{1,0,2:T(1,128)S(1)}, s32[1,128,6]{1,0,2:T(1,128)}, u32[]{:S(2)}) copy-start(s32[1,128,6]{1,0,2:T(1,128)} %param.19) | copy-start | bytes 9220
  17.3 25.0 %copy-start.9 = (s32[1,128,6]{1,0,2:T(1,128)S(1)}, s32[1,128,6]{1,0,2:T(1,128)}, u32[]{:S(2)}) copy-start(s32[1,128,6]{1,0,2:T(1,128)} %param.18) | copy-start | bytes 9220
  17.3 81.9 %copy-start.6 = (f32[2048]{0:T(1024)S(1)}, f32[2048]{0:T(1024)}, u32[]{:S(2)}) copy-start(f32[2048]{0:T(1024)} %param.17) | copy-start | bytes 24580
  17.3 127.4 %collective-permute-start.6 = (bf16[960,1408]{1,0:T(8,128)(2,1)}, bf16[960,1408]{1,0:T(8,128)(2,1)}, u32[]{:S(2)}, u32[]{:S(2)}) collective-permute-start(bf16[960,1408]{1,0:T(8,128)(2,1)} %slice_bitcast_fusion), channel_id=1, source_target_pairs={{0,16},{1,24},{2,18},{3,26},{4,20},{5,28},{6,22},{7,30},{8,17},{9,... | collective-permute-start | bytes 8110088 | tf_op jit(solution)/shard_map/ppermute | solution.py:298
  38.0 60.4 %all-to-all-start.1 = ((bf16[16,128,128]{2,1,0:T(8,128)(2,1)}), bf16[16,128,128]{2,1,0:T(8,128)(2,1)S(1)}, u32[]{:S(2)}, u32[]{:S(2)}) async-start(bf16[16,128,128]{2,1,0:T(8,128)(2,1)} %attend.1), calls=%async_computation.1 | async-start | bytes 1048576 | tf_op jit(solution)/shard_map/all_to_all | solution.py:320
  98.4 0.8 copy-start.7
  99.2 1.0 copy-start.4
  107.9 0.8 copy-start.2
  108.7 37.7 %all-to-all-start.2 = ((bf16[16,16,2048]{2,1,0:T(8,128)(2,1)}), bf16[16,16,2048]{2,1,0:T(8,128)(2,1)S(1)}, u32[]{:S(2)}, u32[]{:S(2)}) async-start(bf16[16,16,2048]{2,1,0:T(8,128)(2,1)} %get-tuple-element.13), calls=%async_computation.2 | async-start | bytes 2097152 | tf_op jit(solution)/shard_map/all_to_all | solution.py:365
  113.5 15.2 %collective-permute-start = (bf16[144,2048]{1,0:T(8,128)(2,1)}, bf16[144,2048]{1,0:T(8,128)(2,1)S(1)}, u32[]{:S(2)}, u32[]{:S(2)}) collective-permute-start(bf16[144,2048]{1,0:T(8,128)(2,1)} %get-tuple-element.14), channel_id=1, source_target_pairs={{0,16},{1,17},{2,18},{3,19},{4,20},{5,21},{6,22},{7,23},{8,24},{9,... | collective-permute-start | bytes 1769480 | tf_op jit(solution)/shard_map/ppermute | solution.py:364
  114.1 28.5 %collective-permute-start.1 = (bf16[144,2048]{1,0:T(8,128)(2,1)}, bf16[144,2048]{1,0:T(8,128)(2,1)S(1)}, u32[]{:S(2)}, u32[]{:S(2)}) collective-permute-start(bf16[144,2048]{1,0:T(8,128)(2,1)} %get-tuple-element.15), channel_id=1, source_target_pairs={{0,1},{1,0},{2,3},{3,2},{4,5},{5,4},{6,7},{7,6},{8,9},{9,8},{10,11... | collective-permute-start | bytes 1769480 | tf_op jit(solution)/shard_map/ppermute | solution.py:364
  117.0 25.6 %collective-permute-start.2 = (bf16[144,2048]{1,0:T(8,128)(2,1)}, bf16[144,2048]{1,0:T(8,128)(2,1)S(1)}, u32[]{:S(2)}, u32[]{:S(2)}) collective-permute-start(bf16[144,2048]{1,0:T(8,128)(2,1)} %get-tuple-element.16), channel_id=1, source_target_pairs={{0,17},{1,16},{2,19},{3,18},{4,21},{5,20},{6,23},{7,22},{8,25},{9,... | collective-permute-start | bytes 1769480 | tf_op jit(solution)/shard_map/ppermute | solution.py:364
  144.7 67.7 %collective-permute-start.10 = (bf16[960,1408]{1,0:T(8,128)(2,1)}, bf16[960,1408]{1,0:T(8,128)(2,1)}, u32[]{:S(2)}, u32[]{:S(2)}) collective-permute-start(bf16[960,1408]{1,0:T(8,128)(2,1)} %collective-permute-done.6.refs_3_), channel_id=1, source_target_pairs={{0,8},{1,9},{2,10},{3,11},{4,12},{5,13},{6,14},{7,15},{8,0},{9,1},... | collective-permute-start | bytes 8110088 | tf_op jit(solution)/shard_map/ppermute | solution.py:299
  146.4 75.6 %collective-permute-start.12 = (bf16[704,2048]{1,0:T(8,128)(2,1)}, bf16[704,2048]{1,0:T(8,128)(2,1)}, u32[]{:S(2)}, u32[]{:S(2)}) collective-permute-start(bf16[704,2048]{1,0:T(8,128)(2,1)} %collective-permute-done.11.down_a), channel_id=1, source_target_pairs={{0,8},{1,9},{2,10},{3,11},{4,12},{5,13},{6,14},{7,15},{8,0},{9,1},... | collective-permute-start | bytes 8650760 | tf_op jit(solution)/shard_map/ppermute | solution.py:302
  146.5 1.0 copy-start
  147.5 54.1 %all-to-all-start.3 = ((bf16[16,48,2048]{2,1,0:T(8,128)(2,1)}), bf16[16,48,2048]{2,1,0:T(8,128)(2,1)S(1)}, u32[]{:S(2)}, u32[]{:S(2)}) async-start(bf16[16,48,2048]{2,1,0:T(8,128)(2,1)} %bitcast.36), calls=%async_computation.3 | async-start | bytes 6291456 | tf_op jit(solution)/shard_map/all_to_all | solution.py:379
  155.5 18.1 %collective-permute-start.5 = (bf16[448,1408]{1,0:T(8,128)(2,1)S(1)}, bf16[448,1408]{1,0:T(8,128)(2,1)}, u32[]{:S(2)}, u32[]{:S(2)}) collective-permute-start(bf16[448,1408]{1,0:T(8,128)(2,1)S(1)} %slice_bitcast_fusion.1), channel_id=1, source_target_pairs={{0,16},{1,24},{2,18},{3,26},{4,20},{5,28},{6,22},{7,30},{8,17},{9,... | collective-permute-start | bytes 3784712 | tf_op jit(solution)/shard_map/ppermute | solution.py:298
  159.6 25.5 %collective-permute-start.4 = (bf16[384,1408]{1,0:T(8,128)(2,1)S(1)}, bf16[384,1408]{1,0:T(8,128)(2,1)}, u32[]{:S(2)}, u32[]{:S(2)}) collective-permute-start(bf16[384,1408]{1,0:T(8,128)(2,1)S(1)} %slice_bitcast_fusion.2), channel_id=1, source_target_pairs={{0,16},{1,24},{2,18},{3,26},{4,20},{5,28},{6,22},{7,30},{8,17},{9,... | collective-permute-start | bytes 3244040 | tf_op jit(solution)/shard_map/ppermute | solution.py:298
  161.1 31.6 %collective-permute-start.3 = (bf16[256,1408]{1,0:T(8,128)(2,1)S(1)}, bf16[256,1408]{1,0:T(8,128)(2,1)}, u32[]{:S(2)}, u32[]{:S(2)}) collective-permute-start(bf16[256,1408]{1,0:T(8,128)(2,1)S(1)} %slice_bitcast_fusion.3), channel_id=1, source_target_pairs={{0,16},{1,24},{2,18},{3,26},{4,20},{5,28},{6,22},{7,30},{8,17},{9,... | collective-permute-start | bytes 2162696 | tf_op jit(solution)/shard_map/ppermute | solution.py:298
  173.5 38.9 %collective-permute-start.9 = (bf16[448,1408]{1,0:T(8,128)(2,1)}, bf16[448,1408]{1,0:T(8,128)(2,1)}, u32[]{:S(2)}, u32[]{:S(2)}) collective-permute-start(bf16[448,1408]{1,0:T(8,128)(2,1)} %collective-permute-done.5.refs_2_), channel_id=1, source_target_pairs={{0,8},{1,9},{2,10},{3,11},{4,12},{5,13},{6,14},{7,15},{8,0},{9,1},... | collective-permute-start | bytes 3784712 | tf_op jit(solution)/shard_map/ppermute | solution.py:299
  185.1 27.3 %collective-permute-start.8 = (bf16[384,1408]{1,0:T(8,128)(2,1)}, bf16[384,1408]{1,0:T(8,128)(2,1)}, u32[]{:S(2)}, u32[]{:S(2)}) collective-permute-start(bf16[384,1408]{1,0:T(8,128)(2,1)} %collective-permute-done.4.refs_1_), channel_id=1, source_target_pairs={{0,8},{1,9},{2,10},{3,11},{4,12},{5,13},{6,14},{7,15},{8,0},{9,1},... | collective-permute-start | bytes 3244040 | tf_op jit(solution)/shard_map/ppermute | solution.py:299
  192.7 19.7 %collective-permute-start.7 = (bf16[256,1408]{1,0:T(8,128)(2,1)}, bf16[256,1408]{1,0:T(8,128)(2,1)}, u32[]{:S(2)}, u32[]{:S(2)}) collective-permute-start(bf16[256,1408]{1,0:T(8,128)(2,1)} %collective-permute-done.3.refs_0_), channel_id=1, source_target_pairs={{0,8},{1,9},{2,10},{3,11},{4,12},{5,13},{6,14},{7,15},{8,0},{9,1},... | collective-permute-start | bytes 2162696 | tf_op jit(solution)/shard_map/ppermute | solution.py:299
  201.6 1.2 copy-start.1
  238.2 58.4 %copy-start.3 = (bf16[128,2048]{1,0:T(8,128)(2,1)S(1)}, bf16[128,2048]{1,0:T(8,128)(2,1)}, u32[]{:S(2)}) copy-start(bf16[128,2048]{1,0:T(8,128)(2,1)} %copy-done.2) | copy-start | bytes 1572868
  238.2 58.4 %copy-start.5 = (bf16[1024,128]{1,0:T(8,128)(2,1)S(1)}, bf16[1024,128]{1,0:T(8,128)(2,1)}, u32[]{:S(2)}) copy-start(bf16[1024,128]{1,0:T(8,128)(2,1)} %get-tuple-element.17.weight_ref) | copy-start | bytes 786436

commit v6 on v5

--- a/solution.py
+++ b/solution.py
@@ -209,7 +209,7 @@
     return (unit - SPOTS) // 3, (3, 1, 2)[(unit - SPOTS) % 3]
 
 
-def inner_kernel(own_ref, rest_ref, *refs):
+def inner_kernel(rows_ref, *refs):
     pieces = len(PIECES)
     parts, (act, w_in, sems) = refs[:pieces], refs[pieces:]
     copies, start = [], 0
@@ -221,36 +221,28 @@
         copy.start()
     for copy in copies:
         copy.wait()
-    for block in range(EXPERTS * SLOTS // X_BLOCK):
-        first = (block - 1) * X_BLOCK
-        rows = own_ref[...] if block == 0 else rest_ref[first : first + X_BLOCK, :]
-        inner = jnp.dot(rows, w_in[...], preferred_element_type=f32)
+    for block in range(rows_ref.shape[0] // X_BLOCK):
+        span = slice(block * X_BLOCK, (block + 1) * X_BLOCK)
+        inner = jnp.dot(rows_ref[span, :], w_in[...], preferred_element_type=f32)
         gate = inner[:, :HALF]
         up = pltpu.roll(inner, HALF, axis=1)[:, :HALF]
-        act[block * X_BLOCK : (block + 1) * X_BLOCK, :] = (
-            gate / (1.0 + jnp.exp(-gate)) * up
-        ).astype(bf16)
-
-
-def down_kernel(y_ref, act_a, act_b, down_a, down_b, out_any, out, out_sems):
+        act[span, :] = (gate / (1.0 + jnp.exp(-gate)) * up).astype(bf16)
+
+
+def down_kernel(y_ref, own_a, own_b, rest_a, rest_b, down_a, down_b, out_ref):
     y = y_ref[0]
-    sends = []
     units = X_BLOCK // SLOTS
     for block in range(EXPERTS * SLOTS // X_BLOCK):
-        span = slice(block * X_BLOCK, (block + 1) * X_BLOCK)
+        act_a, act_b, first = (own_a, own_b, 0) if block == 0 else (rest_a, rest_b, block - 1)
+        span = slice(first * X_BLOCK, (first + 1) * X_BLOCK)
         total = jnp.dot(act_a[span, :], down_a[...], preferred_element_type=f32)
         total = total + jnp.dot(act_b[span, :], down_b[...], preferred_element_type=f32)
-        out[block] = total.astype(bf16).reshape(units, SLOTS, D)
+        total = total.astype(bf16)
         for near in range(units):
-            unit = block * units + near
-            spot, ahead = origin(unit)
+            spot, ahead = origin(block * units + near)
             from_y = (y + ahead) & 3
-            goal = out_any.at[spot // 4, from_y & 1, spot % 4, from_y >> 1]
-            send = pltpu.make_async_copy(out.at[block, near], goal, out_sems.at[unit])
-            send.start()
-            sends.append(send)
-    for send in sends:
-        send.wait()
+            rows = total[near * SLOTS : (near + 1) * SLOTS, :]
+            out_ref[spot // 4, from_y & 1, spot % 4, from_y >> 1] = rows
 
 
 def combine_kernel(rows_ref, weight_ref, mixed_ref, out_ref, acc, total):
@@ -379,40 +371,34 @@
     arrived = lax.all_to_all(
         send.reshape(SPOTS, 3 * SLOTS, D), ("z", "x"), split_axis=0, concat_axis=0, tiled=True
     )
-    blocks = EXPERTS * SLOTS // X_BLOCK
     anywhere = pl.BlockSpec(memory_space=pl.ANY)
 
-    def inner(parts):
+    def inner(rows, parts):
+        rows = rows.reshape(-1, D)
         return pl.pallas_call(
             inner_kernel,
-            out_shape=shape((EXPERTS * SLOTS, HALF), bf16),
-            in_specs=[VMEM, VMEM] + [anywhere] * len(PIECES),
+            out_shape=shape((rows.shape[0], HALF), bf16),
+            in_specs=[VMEM] + [anywhere] * len(PIECES),
             out_specs=VMEM,
             scratch_shapes=[
                 pltpu.VMEM((D, 2 * HALF), bf16),
                 pltpu.SemaphoreType.DMA((len(PIECES),)),
             ],
             compiler_params=params(32),
-        )(
-            arrived_own.reshape(SPOTS * SLOTS, D),
-            arrived.reshape(3 * SPOTS * SLOTS, D),
-            *parts,
-        )
-
-    act_a = inner(moved)
-    act_b = inner(other)
+        )(rows, *parts)
+
+    own_a = inner(arrived_own, moved)
+    own_b = inner(arrived_own, other)
+    rest_a = inner(arrived, moved)
+    rest_b = inner(arrived, other)
     results = pl.pallas_call(
         down_kernel,
         out_shape=shape((4, 2, 4, 2, SLOTS, D), bf16),
-        in_specs=[SMEM] + [VMEM] * 4,
-        out_specs=anywhere,
-        scratch_shapes=[
-            pltpu.VMEM((blocks, X_BLOCK // SLOTS, SLOTS, D), bf16),
-            pltpu.SemaphoreType.DMA((EXPERTS,)),
-        ],
+        in_specs=[SMEM] + [VMEM] * 6,
+        out_specs=VMEM,
         compiler_params=params(32),
         name="down",
-    )(y, act_a, act_b, moved_down, other_down)
+    )(y, own_a, own_b, rest_a, rest_b, moved_down, other_down)
     returned = lax.all_to_all(
         results.reshape(EXPERTS, SLOTS, D), PLACES, split_axis=0, concat_axis=0, tiled=True
     )

time: 301 us -> 300 us (level)
  waiting for transfers between devices: 131 us -> 122 us
  local copies, waits for them, and re-layouts: 12.8 us -> 18.9 us
  blocking collectives: 58.4 us -> 62.3 us
    all_to_all x1, waiting for transfers between devices: 8.88 us -> 0.01 us  [local(): lax.all_to_all(send.reshape(SPOTS, 3 * SLOTS, D), ('z', 'x'), split_axis=...]
    pallas_call x1, Pallas kernels: 16.2 us -> 9.34 us  [local(): pl.pallas_call(down_kernel, out_shape=shape((4, 2, 4, 2, SLOTS, D), bf16)...]
    unnamed x20 -> x48, local copies, waits for them, and re-layouts: 4.77 us -> 10.8 us
    pallas_call x2 -> x4, Pallas kernels: 19.1 us -> 24.7 us  [inner(): pl.pallas_call(inner_kernel, out_shape=shape((rows.shape[0], HALF), bf16)...]
    all_to_all x1, blocking collectives: 58.4 us -> 62.3 us  [local(): lax.all_to_all(results.reshape(EXPERTS, SLOTS, D), PLACES, split_axis=0,...]
  transfers between devices with their start and end apart: 17 -> 17, of which waited for: 8 -> 7; matrix products, arithmetic and copies ran while one was open for 3% -> 3% of each run, Pallas kernels for 12% -> 14%
where the time goes in v6:
time: 300 us; the launch traced here: 299 us
  waiting for transfers between devices  122 us (41%)
  blocking collectives  62.3 us (21%)
  Pallas kernels  56.8 us (19%)
  starting transfers between devices  39.4 us (13%)
  local copies, waits for them, and re-layouts  18.9 us (6%)
    all_to_all x1, blocking collectives, local(): lax.all_to_all(results.reshape(EXPERTS, SLOTS, D), PLACES, split_axis=0,...  62.3 us
    all_to_all x1, waiting for transfers between devices, local(): lax.all_to_all(attended, POSITIONS, split_axis=0, concat_axis=0, tiled=True)  53.5 us
    ppermute x4, waiting for transfers between devices, local(): moved.append(lax.ppermute(piece, AXES, moves(weight_target)))  28.7 us
    pallas_call x4, Pallas kernels, inner(): pl.pallas_call(inner_kernel, out_shape=shape((rows.shape[0], HALF), bf16)...  24.7 us
    ppermute x3, waiting for transfers between devices, local(): arriving.append(lax.ppermute(share, AXES, moves(along_y(distance))))  24.1 us
    all_to_all x1, waiting for transfers between devices, local(): lax.all_to_all(packed, POSITIONS, split_axis=0, concat_axis=0, tiled=True)  15.4 us
    unnamed x48, local copies, waits for them, and re-layouts  10.8 us
    pallas_call x1, Pallas kernels, local(): pl.pallas_call(down_kernel, out_shape=shape((4, 2, 4, 2, SLOTS, D), bf16)...  9.34 us
  transfers between devices with their start and end apart: 17, of which 7 were waited for; matrix products, arithmetic and copies ran while one was open for 3% of the time, Pallas kernels for 14%

profile of v6, /device:TPU:1, one launch (start us, length us, event | category | flops | bytes accessed | tf_op | source)
XLA Modules:
  0.0 299.3 jit_solution(16420667098792356304)
XLA Ops:
  0.0 2.9 pack.1
  2.9 7.8 %all-to-all-start = ((bf16[16,400,128]{2,1,0:T(8,128)(2,1)}), bf16[16,400,128]{2,1,0:T(8,128)(2,1)S(1)}, u32[]{:S(2)}, u32[]{:S(2)}) async-start(bf16[16,400,128]{2,1,0:T(8,128)(2,1)} %pack.1), calls=%async_computation | async-start | bytes 3276800 | tf_op jit(solution)/shard_map/all_to_all | solution.py:303
  10.7 3.1 %collective-permute-start.11 = (bf16[704,2048]{1,0:T(8,128)(2,1)}, bf16[704,2048]{1,0:T(8,128)(2,1)}, u32[]{:S(2)}, u32[]{:S(2)}) collective-permute-start(bf16[704,2048]{1,0:T(8,128)(2,1)} %bitcast.41), channel_id=1, source_target_pairs={{0,16},{1,24},{2,18},{3,26},{4,20},{5,28},{6,22},{7,30},{8,17},{9,... | collective-permute-start | bytes 8650760 | tf_op jit(solution)/shard_map/ppermute | solution.py:293
  13.8 3.5 %slice_bitcast_fusion = bf16[960,1408]{1,0:T(8,128)(2,1)} fusion(bf16[1,2048,1408]{2,1,0:T(8,128)(2,1)} %param.20), kind=kLoop, calls=%fused_computation | loop fusion | bytes 5406720 | tf_op jit(solution)/shard_map/slice | solution.py:289
  17.3 15.4 %all-to-all-done.x_ref = bf16[16,400,128]{2,1,0:T(8,128)(2,1)S(1)} async-done(((bf16[16,400,128]{2,1,0:T(8,128)(2,1)}), bf16[16,400,128]{2,1,0:T(8,128)(2,1)S(1)}, u32[]{:S(2)}, u32[]{:S(2)}) %all-to-all-start) | async-done | bytes 1638432 | tf_op jit(solution)/shard_map/all_to_all | solution.py:303
  32.7 5.2 %attend.1 = bf16[16,128,128]{2,1,0:T(8,128)(2,1)} custom-call(bf16[16,400,128]{2,1,0:T(8,128)(2,1)S(1)} %all-to-all-done.x_ref), custom_call_target="tpu_custom_call" | custom-call | tf_op jit(solution)/shard_map/attend/pallas_call | solution.py:304
  38.0 4.3 %all-to-all-start.1 = ((bf16[16,128,128]{2,1,0:T(8,128)(2,1)}), bf16[16,128,128]{2,1,0:T(8,128)(2,1)S(1)}, u32[]{:S(2)}, u32[]{:S(2)}) async-start(bf16[16,128,128]{2,1,0:T(8,128)(2,1)} %attend.1), calls=%async_computation.1 | async-start | bytes 1048576 | tf_op jit(solution)/shard_map/all_to_all | solution.py:312
  42.9 2.0 route.1
  44.9 53.5 %all-to-all-done.1.heads_ref = bf16[16,128,128]{2,1,0:T(8,128)(2,1)S(1)} async-done(((bf16[16,128,128]{2,1,0:T(8,128)(2,1)}), bf16[16,128,128]{2,1,0:T(8,128)(2,1)S(1)}, u32[]{:S(2)}, u32[]{:S(2)}) %all-to-all-start.1) | async-done | bytes 524320 | tf_op jit(solution)/shard_map/all_to_all | solution.py:312
  100.1 7.7 %project.1 = (bf16[128,2048]{1,0:T(8,128)(2,1)S(1)}, bf16[144,2048]{1,0:T(8,128)(2,1)}, bf16[144,2048]{1,0:T(8,128)(2,1)}, bf16[144,2048]{1,0:T(8,128)(2,1)}, bf16[16,16,2048]{2,1,0:T(8,128)(2,1)}) custom-call(bf16[16,128,128]{2,1,0:T(8,128)(2,1)} %copy-done.21, bf16[2048,2048]{1,0:T(8,128)(2,1)} %weight_ref.1, bf16[128,2048]{1,0:T(8,128)(2,1)} %bitcast.37, ...), custom_call_target="tpu_custom_call" | custom-call | tf_op jit(solution)/shard_map/project/pallas_call | solution.py:326
  108.7 4.8 %all-to-all-start.2 = ((bf16[16,16,2048]{2,1,0:T(8,128)(2,1)}), bf16[16,16,2048]{2,1,0:T(8,128)(2,1)S(1)}, u32[]{:S(2)}, u32[]{:S(2)}) async-start(bf16[16,16,2048]{2,1,0:T(8,128)(2,1)} %get-tuple-element.13), calls=%async_computation.2 | async-start | bytes 2097152 | tf_op jit(solution)/shard_map/all_to_all | solution.py:357
  114.1 2.9 collective-permute-start.9
  117.0 1.5 collective-permute-start.10
  118.5 10.2 %collective-permute-done.8.near_ref = bf16[144,2048]{1,0:T(8,128)(2,1)S(1)} collective-permute-done((bf16[144,2048]{1,0:T(8,128)(2,1)}, bf16[144,2048]{1,0:T(8,128)(2,1)S(1)}, u32[]{:S(2)}, u32[]{:S(2)}) %collective-permute-start.8) | collective-permute-done | bytes 589856 | tf_op jit(solution)/shard_map/ppermute | solution.py:356
  128.7 13.9 %collective-permute-done.9.far_ref = bf16[144,2048]{1,0:T(8,128)(2,1)S(1)} collective-permute-done((bf16[144,2048]{1,0:T(8,128)(2,1)}, bf16[144,2048]{1,0:T(8,128)(2,1)S(1)}, u32[]{:S(2)}, u32[]{:S(2)}) %collective-permute-start.9) | collective-permute-done | bytes 589856 | tf_op jit(solution)/shard_map/ppermute | solution.py:356
  142.6 2.1 fill.1
  144.7 1.6 collective-permute-start.7
  147.4 6.6 %all-to-all-start.3 = ((bf16[16,48,2048]{2,1,0:T(8,128)(2,1)}), bf16[16,48,2048]{2,1,0:T(8,128)(2,1)S(1)}, u32[]{:S(2)}, u32[]{:S(2)}) async-start(bf16[16,48,2048]{2,1,0:T(8,128)(2,1)} %bitcast.36), calls=%async_computation.3 | async-start | bytes 6291456 | tf_op jit(solution)/shard_map/all_to_all | solution.py:371
  154.0 1.5 slice_bitcast_fusion.1
  155.4 2.9 collective-permute-start.2
  158.3 1.3 slice_bitcast_fusion.2
  161.1 2.9 collective-permute-start
  163.9 9.6 %collective-permute-done.2.refs_2_ = bf16[448,1408]{1,0:T(8,128)(2,1)S(1)} collective-permute-done((bf16[448,1408]{1,0:T(8,128)(2,1)S(1)}, bf16[448,1408]{1,0:T(8,128)(2,1)S(1)}, u32[]{:S(2)}, u32[]{:S(2)}) %collective-permute-start.2) | collective-permute-done | bytes 1261600 | tf_op jit(solution)/shard_map/ppermute | solution.py:290
  173.5 11.6 %collective-permute-done.1.refs_1_ = bf16[384,1408]{1,0:T(8,128)(2,1)S(1)} collective-permute-done((bf16[384,1408]{1,0:T(8,128)(2,1)S(1)}, bf16[384,1408]{1,0:T(8,128)(2,1)S(1)}, u32[]{:S(2)}, u32[]{:S(2)}) %collective-permute-start.1) | collective-permute-done | bytes 1081376 | tf_op jit(solution)/shard_map/ppermute | solution.py:290
  185.1 7.5 %collective-permute-done.refs_0_ = bf16[256,1408]{1,0:T(8,128)(2,1)S(1)} collective-permute-done((bf16[256,1408]{1,0:T(8,128)(2,1)S(1)}, bf16[256,1408]{1,0:T(8,128)(2,1)S(1)}, u32[]{:S(2)}, u32[]{:S(2)}) %collective-permute-start) | collective-permute-done | bytes 720928 | tf_op jit(solution)/shard_map/ppermute | solution.py:290
  192.6 4.4 %shard_map.109.own_a = bf16[256,704]{1,0:T(8,128)(2,1)S(1)} custom-call(bf16[256,2048]{1,0:T(8,128)(2,1)S(1)} %bitcast.33, bf16[256,1408]{1,0:T(8,128)(2,1)S(1)} %collective-permute-done.refs_0_, bf16[384,1408]{1,0:T(8,128)(2,1)S(1)} %collective-permute-done.1.refs_1_, bf16[448,1408]{1,0:T(8,128)(2,1)S(1)} %collective-permute-done.2.refs_2_, ...), custom_call_target="tpu_custom_call" | custom-call | tf_op jit(solution)/shard_map/pallas_call | solution.py:378
  197.1 4.4 %shard_map.110.own_b = bf16[256,704]{1,0:T(8,128)(2,1)S(1)} custom-call(bf16[256,2048]{1,0:T(8,128)(2,1)S(1)} %bitcast.34, bf16[256,1408]{1,0:T(8,128)(2,1)S(1)} %collective-permute-done.4.refs_0_, bf16[384,1408]{1,0:T(8,128)(2,1)S(1)} %collective-permute-done.5.refs_1_, bf16[448,1408]{1,0:T(8,128)(2,1)S(1)} %collective-permute-done.6.refs_2_, ...), custom_call_target="tpu_custom_call" | custom-call | tf_op jit(solution)/shard_map/pallas_call | solution.py:378
  208.9 7.9 %shard_map.111.rest_a = bf16[768,704]{1,0:T(8,128)(2,1)S(1)} custom-call(bf16[768,2048]{1,0:T(8,128)(2,1)S(1)} %bitcast.29, bf16[256,1408]{1,0:T(8,128)(2,1)S(1)} %copy-done.11, bf16[384,1408]{1,0:T(8,128)(2,1)S(1)} %copy-done.7, bf16[448,1408]{1,0:T(8,128)(2,1)S(1)} %copy-done.3, bf16[960,1408]{1,0:T(8,128)(2,1)} %collective-permute-done.3.refs_3_), custom_call_target="tpu_custom_call" | custom-call | tf_op jit(solution)/shard_map/pallas_call | solution.py:378
  216.8 7.9 %shard_map.112.rest_b = bf16[768,704]{1,0:T(8,128)(2,1)S(1)} custom-call(bf16[768,2048]{1,0:T(8,128)(2,1)S(1)} %bitcast.30, bf16[256,1408]{1,0:T(8,128)(2,1)S(1)} %copy-done.13, bf16[384,1408]{1,0:T(8,128)(2,1)S(1)} %copy-done.9, bf16[448,1408]{1,0:T(8,128)(2,1)S(1)} %copy-done.5, bf16[960,1408]{1,0:T(8,128)(2,1)} %collective-permute-done.7.refs_3_), custom_call_target="tpu_custom_call" | custom-call | tf_op jit(solution)/shard_map/pallas_call | solution.py:378
  224.8 9.3 %down.1 = bf16[4,2,4,2,16,2048]{5,4,3,2,1,0:T(8,128)(2,1)S(1)} custom-call(s32[1]{0:T(128)} %bitcast.y_ref, bf16[256,704]{1,0:T(8,128)(2,1)S(1)} %shard_map.109.own_a, bf16[256,704]{1,0:T(8,128)(2,1)S(1)} %copy-done.15, bf16[768,704]{1,0:T(8,128)(2,1)S(1)} %shard_map.111.rest_a, bf16[768,704]{1,0:T(8,128)(2,1)S(1)} %shard_map.112.rest_b, ...), custom_call_target="tpu_custom_call" | custom-call | tf_op jit(solution)/shard_map/down/pallas_call | solution.py:394
  234.2 62.3 %all_to_all.25 = bf16[64,16,2048]{2,1,0:T(8,128)(2,1)S(1)} all-to-all(bf16[64,16,2048]{2,1,0:T(8,128)(2,1)S(1)} %bitcast.31), channel_id=1, replica_groups=mesh['z'=4,'yl'=2,'c'=2,'x'=4,'yh'=2] {'z','yl','x','yh'}, dimensions={0} | all-to-all | bytes 8388608 | tf_op jit(solution)/shard_map/all_to_all | solution.py:402
  296.5 2.8 combine.1
  (67 shorter events, 13.6 us)
Async XLA Ops:
  2.9 29.9 %all-to-all-start = ((bf16[16,400,128]{2,1,0:T(8,128)(2,1)}), bf16[16,400,128]{2,1,0:T(8,128)(2,1)S(1)}, u32[]{:S(2)}, u32[]{:S(2)}) async-start(bf16[16,400,128]{2,1,0:T(8,128)(2,1)} %pack.1), calls=%async_computation | async-start | bytes 3276800 | tf_op jit(solution)/shard_map/all_to_all | solution.py:303
  10.7 135.6 %collective-permute-start.11 = (bf16[704,2048]{1,0:T(8,128)(2,1)}, bf16[704,2048]{1,0:T(8,128)(2,1)}, u32[]{:S(2)}, u32[]{:S(2)}) collective-permute-start(bf16[704,2048]{1,0:T(8,128)(2,1)} %bitcast.41), channel_id=1, source_target_pairs={{0,16},{1,24},{2,18},{3,26},{4,20},{5,28},{6,22},{7,30},{8,17},{9,... | collective-permute-start | bytes 8650760 | tf_op jit(solution)/shard_map/ppermute | solution.py:293
  17.3 25.0 %copy-start.22 = (s32[1,128,6]{1,0,2:T(1,128)S(1)}, s32[1,128,6]{1,0,2:T(1,128)}, u32[]{:S(2)}) copy-start(s32[1,128,6]{1,0,2:T(1,128)} %param.19) | copy-start | bytes 9220
  17.3 25.0 %copy-start.23 = (s32[1,128,6]{1,0,2:T(1,128)S(1)}, s32[1,128,6]{1,0,2:T(1,128)}, u32[]{:S(2)}) copy-start(s32[1,128,6]{1,0,2:T(1,128)} %param.18) | copy-start | bytes 9220
  17.3 81.9 %copy-start.20 = (f32[2048]{0:T(1024)S(1)}, f32[2048]{0:T(1024)}, u32[]{:S(2)}) copy-start(f32[2048]{0:T(1024)} %param.17) | copy-start | bytes 24580
  17.3 127.3 %collective-permute-start.3 = (bf16[960,1408]{1,0:T(8,128)(2,1)}, bf16[960,1408]{1,0:T(8,128)(2,1)}, u32[]{:S(2)}, u32[]{:S(2)}) collective-permute-start(bf16[960,1408]{1,0:T(8,128)(2,1)} %slice_bitcast_fusion), channel_id=1, source_target_pairs={{0,16},{1,24},{2,18},{3,26},{4,20},{5,28},{6,22},{7,30},{8,17},{9,... | collective-permute-start | bytes 8110088 | tf_op jit(solution)/shard_map/ppermute | solution.py:290
  38.0 60.4 %all-to-all-start.1 = ((bf16[16,128,128]{2,1,0:T(8,128)(2,1)}), bf16[16,128,128]{2,1,0:T(8,128)(2,1)S(1)}, u32[]{:S(2)}, u32[]{:S(2)}) async-start(bf16[16,128,128]{2,1,0:T(8,128)(2,1)} %attend.1), calls=%async_computation.1 | async-start | bytes 1048576 | tf_op jit(solution)/shard_map/all_to_all | solution.py:312
  108.7 37.7 %all-to-all-start.2 = ((bf16[16,16,2048]{2,1,0:T(8,128)(2,1)}), bf16[16,16,2048]{2,1,0:T(8,128)(2,1)S(1)}, u32[]{:S(2)}, u32[]{:S(2)}) async-start(bf16[16,16,2048]{2,1,0:T(8,128)(2,1)} %get-tuple-element.13), calls=%async_computation.2 | async-start | bytes 2097152 | tf_op jit(solution)/shard_map/all_to_all | solution.py:357
  113.5 15.2 %collective-permute-start.8 = (bf16[144,2048]{1,0:T(8,128)(2,1)}, bf16[144,2048]{1,0:T(8,128)(2,1)S(1)}, u32[]{:S(2)}, u32[]{:S(2)}) collective-permute-start(bf16[144,2048]{1,0:T(8,128)(2,1)} %get-tuple-element.14), channel_id=1, source_target_pairs={{0,16},{1,17},{2,18},{3,19},{4,20},{5,21},{6,22},{7,23},{8,24},{9,... | collective-permute-start | bytes 1769480 | tf_op jit(solution)/shard_map/ppermute | solution.py:356
  114.1 28.5 %collective-permute-start.9 = (bf16[144,2048]{1,0:T(8,128)(2,1)}, bf16[144,2048]{1,0:T(8,128)(2,1)S(1)}, u32[]{:S(2)}, u32[]{:S(2)}) collective-permute-start(bf16[144,2048]{1,0:T(8,128)(2,1)} %get-tuple-element.15), channel_id=1, source_target_pairs={{0,1},{1,0},{2,3},{3,2},{4,5},{5,4},{6,7},{7,6},{8,9},{9,8},{10,11... | collective-permute-start | bytes 1769480 | tf_op jit(solution)/shard_map/ppermute | solution.py:356
  117.0 25.6 %collective-permute-start.10 = (bf16[144,2048]{1,0:T(8,128)(2,1)}, bf16[144,2048]{1,0:T(8,128)(2,1)S(1)}, u32[]{:S(2)}, u32[]{:S(2)}) collective-permute-start(bf16[144,2048]{1,0:T(8,128)(2,1)} %get-tuple-element.16), channel_id=1, source_target_pairs={{0,17},{1,16},{2,19},{3,18},{4,21},{5,20},{6,23},{7,22},{8,25},{9,... | collective-permute-start | bytes 1769480 | tf_op jit(solution)/shard_map/ppermute | solution.py:356
  144.7 52.5 %collective-permute-start.7 = (bf16[960,1408]{1,0:T(8,128)(2,1)}, bf16[960,1408]{1,0:T(8,128)(2,1)}, u32[]{:S(2)}, u32[]{:S(2)}) collective-permute-start(bf16[960,1408]{1,0:T(8,128)(2,1)} %collective-permute-done.3.refs_3_), channel_id=1, source_target_pairs={{0,8},{1,9},{2,10},{3,11},{4,12},{5,13},{6,14},{7,15},{8,0},{9,1},... | collective-permute-start | bytes 8110088 | tf_op jit(solution)/shard_map/ppermute | solution.py:291
  146.3 78.5 %collective-permute-start.12 = (bf16[704,2048]{1,0:T(8,128)(2,1)}, bf16[704,2048]{1,0:T(8,128)(2,1)}, u32[]{:S(2)}, u32[]{:S(2)}) collective-permute-start(bf16[704,2048]{1,0:T(8,128)(2,1)} %collective-permute-done.11.down_a), channel_id=1, source_target_pairs={{0,8},{1,9},{2,10},{3,11},{4,12},{5,13},{6,14},{7,15},{8,0},{9,1},... | collective-permute-start | bytes 8650760 | tf_op jit(solution)/shard_map/ppermute | solution.py:294
  147.4 57.9 %all-to-all-start.3 = ((bf16[16,48,2048]{2,1,0:T(8,128)(2,1)}), bf16[16,48,2048]{2,1,0:T(8,128)(2,1)S(1)}, u32[]{:S(2)}, u32[]{:S(2)}) async-start(bf16[16,48,2048]{2,1,0:T(8,128)(2,1)} %bitcast.36), calls=%async_computation.3 | async-start | bytes 6291456 | tf_op jit(solution)/shard_map/all_to_all | solution.py:371
  154.0 38.7 %copy-start.1 = (bf16[16,16,2048]{2,1,0:T(8,128)(2,1)S(1)}, bf16[16,16,2048]{2,1,0:T(8,128)(2,1)}, u32[]{:S(2)}) copy-start(bf16[16,16,2048]{2,1,0:T(8,128)(2,1)} %copy-done) | copy-start | bytes 3145732
  155.4 18.1 %collective-permute-start.2 = (bf16[448,1408]{1,0:T(8,128)(2,1)S(1)}, bf16[448,1408]{1,0:T(8,128)(2,1)S(1)}, u32[]{:S(2)}, u32[]{:S(2)}) collective-permute-start(bf16[448,1408]{1,0:T(8,128)(2,1)S(1)} %slice_bitcast_fusion.1), channel_id=1, source_target_pairs={{0,16},{1,24},{2,18},{3,26},{4,20},{5,28},{6,22},{7,30},{8,17},{9,... | collective-permute-start | bytes 3784712 | tf_op jit(solution)/shard_map/ppermute | solution.py:290
  159.6 25.5 %collective-permute-start.1 = (bf16[384,1408]{1,0:T(8,128)(2,1)S(1)}, bf16[384,1408]{1,0:T(8,128)(2,1)S(1)}, u32[]{:S(2)}, u32[]{:S(2)}) collective-permute-start(bf16[384,1408]{1,0:T(8,128)(2,1)S(1)} %slice_bitcast_fusion.2), channel_id=1, source_target_pairs={{0,16},{1,24},{2,18},{3,26},{4,20},{5,28},{6,22},{7,30},{8,17},{9,... | collective-permute-start | bytes 3244040 | tf_op jit(solution)/shard_map/ppermute | solution.py:290
  161.1 31.6 %collective-permute-start = (bf16[256,1408]{1,0:T(8,128)(2,1)S(1)}, bf16[256,1408]{1,0:T(8,128)(2,1)S(1)}, u32[]{:S(2)}, u32[]{:S(2)}) collective-permute-start(bf16[256,1408]{1,0:T(8,128)(2,1)S(1)} %slice_bitcast_fusion.3), channel_id=1, source_target_pairs={{0,16},{1,24},{2,18},{3,26},{4,20},{5,28},{6,22},{7,30},{8,17},{9,... | collective-permute-start | bytes 2162696 | tf_op jit(solution)/shard_map/ppermute | solution.py:290
  173.5 23.5 %copy-start.2 = (bf16[448,1408]{1,0:T(8,128)(2,1)}, bf16[448,1408]{1,0:T(8,128)(2,1)S(1)}, u32[]{:S(2)}) copy-start(bf16[448,1408]{1,0:T(8,128)(2,1)S(1)} %collective-permute-done.2.refs_2_) | copy-start | bytes 3784708
  173.5 23.6 %collective-permute-start.6 = (bf16[448,1408]{1,0:T(8,128)(2,1)S(1)}, bf16[448,1408]{1,0:T(8,128)(2,1)S(1)}, u32[]{:S(2)}, u32[]{:S(2)}) collective-permute-start(bf16[448,1408]{1,0:T(8,128)(2,1)S(1)} %collective-permute-done.2.refs_2_), channel_id=1, source_target_pairs={{0,8},{1,9},{2,10},{3,11},{4,12},{5,13},{6,14},{7,15},{8,0},{9,1},... | collective-permute-start | bytes 3784712 | tf_op jit(solution)/shard_map/ppermute | solution.py:291
  185.1 12.0 %copy-start.6 = (bf16[384,1408]{1,0:T(8,128)(2,1)}, bf16[384,1408]{1,0:T(8,128)(2,1)S(1)}, u32[]{:S(2)}) copy-start(bf16[384,1408]{1,0:T(8,128)(2,1)S(1)} %collective-permute-done.1.refs_1_) | copy-start | bytes 3244036
  185.1 12.0 %collective-permute-start.5 = (bf16[384,1408]{1,0:T(8,128)(2,1)S(1)}, bf16[384,1408]{1,0:T(8,128)(2,1)S(1)}, u32[]{:S(2)}, u32[]{:S(2)}) collective-permute-start(bf16[384,1408]{1,0:T(8,128)(2,1)S(1)} %collective-permute-done.1.refs_1_), channel_id=1, source_target_pairs={{0,8},{1,9},{2,10},{3,11},{4,12},{5,13},{6,14},{7,15},{8,0},{9,1},... | collective-permute-start | bytes 3244040 | tf_op jit(solution)/shard_map/ppermute | solution.py:291
  192.6 4.5 %copy-start.10 = (bf16[256,1408]{1,0:T(8,128)(2,1)}, bf16[256,1408]{1,0:T(8,128)(2,1)S(1)}, u32[]{:S(2)}) copy-start(bf16[256,1408]{1,0:T(8,128)(2,1)S(1)} %collective-permute-done.refs_0_) | copy-start | bytes 2162692
  192.6 4.5 %collective-permute-start.4 = (bf16[256,1408]{1,0:T(8,128)(2,1)S(1)}, bf16[256,1408]{1,0:T(8,128)(2,1)S(1)}, u32[]{:S(2)}, u32[]{:S(2)}) collective-permute-start(bf16[256,1408]{1,0:T(8,128)(2,1)S(1)} %collective-permute-done.refs_0_), channel_id=1, source_target_pairs={{0,8},{1,9},{2,10},{3,11},{4,12},{5,13},{6,14},{7,15},{8,0},{9,1},... | collective-permute-start | bytes 2162696 | tf_op jit(solution)/shard_map/ppermute | solution.py:291
  205.2 1.3 copy-start.3
  206.5 1.2 copy-start.7
  208.9 7.9 %copy-start.5 = (bf16[448,1408]{1,0:T(8,128)(2,1)S(1)}, bf16[448,1408]{1,0:T(8,128)(2,1)}, u32[]{:S(2)}) copy-start(bf16[448,1408]{1,0:T(8,128)(2,1)} %copy-done.4) | copy-start | bytes 3784708
  208.9 7.9 %copy-start.9 = (bf16[384,1408]{1,0:T(8,128)(2,1)S(1)}, bf16[384,1408]{1,0:T(8,128)(2,1)}, u32[]{:S(2)}) copy-start(bf16[384,1408]{1,0:T(8,128)(2,1)} %copy-done.8) | copy-start | bytes 3244036
  208.9 7.9 %copy-start.13 = (bf16[256,1408]{1,0:T(8,128)(2,1)S(1)}, bf16[256,1408]{1,0:T(8,128)(2,1)}, u32[]{:S(2)}) copy-start(bf16[256,1408]{1,0:T(8,128)(2,1)} %copy-done.12) | copy-start | bytes 2162692
  216.8 8.0 %copy-start.15 = (bf16[256,704]{1,0:T(8,128)(2,1)S(1)}, bf16[256,704]{1,0:T(8,128)(2,1)}, u32[]{:S(2)}) copy-start(bf16[256,704]{1,0:T(8,128)(2,1)} %copy-done.14) | copy-start | bytes 1081348
  234.1 62.3 %copy-start.17 = (bf16[128,2048]{1,0:T(8,128)(2,1)S(1)}, bf16[128,2048]{1,0:T(8,128)(2,1)}, u32[]{:S(2)}) copy-start(bf16[128,2048]{1,0:T(8,128)(2,1)} %copy-done.16) | copy-start | bytes 1572868
  234.2 62.3 %copy-start.19 = (bf16[1024,128]{1,0:T(8,128)(2,1)S(1)}, bf16[1024,128]{1,0:T(8,128)(2,1)}, u32[]{:S(2)}) copy-start(bf16[1024,128]{1,0:T(8,128)(2,1)} %get-tuple-element.17.weight_ref) | copy-start | bytes 786436
  (9 other events, 8.3 us)

commit v7 on v6

--- a/solution.py
+++ b/solution.py
@@ -21,6 +21,7 @@
 PACK_ROWS = 3 * ROWS + SEG_ROWS
 Q_BLOCK = 256
 X_BLOCK = 256
+PACK_STEPS = 4
 PIECES = (256, 384, 448, 960)
 SPOTS = 16
 Y_SIZE = 4
@@ -75,7 +76,7 @@
 
 def pack_kernel(q_ref, k_ref, v_ref, seg_ref, out_ref):
     seg = jnp.broadcast_to(seg_ref[...].astype(f32), (SEG_ROWS, ROWS)).astype(bf16)
-    for head in range(HEADS):
+    for head in range(HEADS // PACK_STEPS):
         lanes = slice(head * HEAD_DIM, (head + 1) * HEAD_DIM)
         out_ref[head, 0:ROWS, :] = q_ref[:, lanes]
         out_ref[head, ROWS : 2 * ROWS, :] = k_ref[:, lanes]
@@ -245,28 +246,13 @@
             out_ref[spot // 4, from_y & 1, spot % 4, from_y >> 1] = rows
 
 
-def combine_kernel(rows_ref, weight_ref, mixed_ref, out_ref, acc, total):
-    step = pl.program_id(0)
+def combine_kernel(rows_ref, weight_ref, mixed_ref, out_ref):
     over = (((0,), (0,)), ((), ()))
     weight = weight_ref[...]
-    product = lax.dot_general(weight, rows_ref[...], over, preferred_element_type=f32)
+    routed = lax.dot_general(weight, rows_ref[...], over, preferred_element_type=f32)
     ones = jnp.ones((weight.shape[0], ROWS), bf16)
-    count = lax.dot_general(weight, ones, over, preferred_element_type=f32)
-
-    @pl.when(step == 0)
-    def _():
-        acc[...] = product
-        total[...] = count
-
-    @pl.when(step > 0)
-    def _():
-        acc[...] += product
-        total[...] += count
-
-    @pl.when(step == pl.num_programs(0) - 1)
-    def _():
-        routed = acc[...] / total[:, 0:1]
-        out_ref[...] = (mixed_ref[...].astype(f32) + routed).astype(bf16)
+    total = lax.dot_general(weight, ones, over, preferred_element_type=f32)
+    out_ref[...] = (mixed_ref[...].astype(f32) + routed / total[:, 0:1]).astype(bf16)
 
 
 def local(
@@ -292,11 +278,13 @@
         start += count
     moved_down = lax.ppermute(w_down[0], AXES, moves(weight_target))
     other_down = lax.ppermute(moved_down, AXES, moves(core_target))
+    wide = pl.BlockSpec((ROWS, D // PACK_STEPS), lambda i: (0, i))
     packed = pl.pallas_call(
         pack_kernel,
+        grid=(PACK_STEPS,),
         out_shape=shape((HEADS, PACK_ROWS, HEAD_DIM), bf16),
-        in_specs=[VMEM] * 4,
-        out_specs=VMEM,
+        in_specs=[wide, wide, wide, pl.BlockSpec((1, ROWS), lambda i: (0, 0))],
+        out_specs=pl.BlockSpec((HEADS // PACK_STEPS, PACK_ROWS, HEAD_DIM), lambda i: (i, 0, 0)),
         compiler_params=params(60),
         name="pack",
     )(queries[0], keys[0], values[0], segment_ids)
@@ -348,7 +336,7 @@
             pl.BlockSpec((SPOTS, SLOTS, D), lambda i: (0, 0, 0)),
         ),
         scratch_shapes=[pltpu.VMEM((ROWS, D), f32)],
-        compiler_params=params(53),
+        compiler_params=params(50),
         name="project",
     )(heads, out_weight, hidden_in[0], norm_gain[None], pick)
     arriving = []
@@ -402,19 +390,12 @@
     returned = lax.all_to_all(
         results.reshape(EXPERTS, SLOTS, D), PLACES, split_axis=0, concat_axis=0, tiled=True
     )
-    block = 256
     layer_out = pl.pallas_call(
         combine_kernel,
-        grid=(EXPERTS * SLOTS // block,),
         out_shape=shape((ROWS, D), bf16),
-        in_specs=[
-            pl.BlockSpec((block, D), lambda i: (i, 0)),
-            pl.BlockSpec((block, ROWS), lambda i: (i, 0)),
-            pl.BlockSpec((ROWS, D), lambda i: (0, 0)),
-        ],
-        out_specs=pl.BlockSpec((ROWS, D), lambda i: (0, 0)),
-        scratch_shapes=[pltpu.VMEM((ROWS, D), f32), pltpu.VMEM((ROWS, ROWS), f32)],
-        compiler_params=params(12),
+        in_specs=[VMEM] * 3,
+        out_specs=VMEM,
+        compiler_params=params(24),
         name="combine",
     )(returned.reshape(EXPERTS * SLOTS, D), weight, mixed)
     return layer_out[None]

time: 300 us -> 298 us (level)
  no operation moved by 1% of the time
where the time goes in v7:
time: 298 us; the launch traced here: 297 us
  waiting for transfers between devices  121 us (41%)
  blocking collectives  62.3 us (21%)
  Pallas kernels  55.7 us (19%)
  starting transfers between devices  39.4 us (13%)
  local copies, waits for them, and re-layouts  18.1 us (6%)
    all_to_all x1, blocking collectives, local(): lax.all_to_all(results.reshape(EXPERTS, SLOTS, D), PLACES, split_axis=0,...  62.3 us
    all_to_all x1, waiting for transfers between devices, local(): lax.all_to_all(attended, POSITIONS, split_axis=0, concat_axis=0, tiled=True)  53.5 us
    ppermute x4, waiting for transfers between devices, local(): moved.append(lax.ppermute(piece, AXES, moves(weight_target)))  28.7 us
    pallas_call x4, Pallas kernels, inner(): pl.pallas_call(inner_kernel, out_shape=shape((rows.shape[0], HALF), bf16)...  24.7 us
    ppermute x3, waiting for transfers between devices, local(): arriving.append(lax.ppermute(share, AXES, moves(along_y(distance))))  23.9 us
    all_to_all x1, waiting for transfers between devices, local(): lax.all_to_all(packed, POSITIONS, split_axis=0, concat_axis=0, tiled=True)  15.3 us
    unnamed x48, local copies, waits for them, and re-layouts  10 us
    pallas_call x1, Pallas kernels, local(): pl.pallas_call(down_kernel, out_shape=shape((4, 2, 4, 2, SLOTS, D), bf16)...  9.34 us
  transfers between devices with their start and end apart: 17, of which 7 were waited for; matrix products, arithmetic and copies ran while one was open for 3% of the time, Pallas kernels for 14%

profile of v7, /device:TPU:1, one launch (start us, length us, event | category | flops | bytes accessed | tf_op | source)
XLA Modules:
  0.0 297.2 jit_solution(784968293273235376)
XLA Ops:
  0.0 3.8 %pack.1 = bf16[16,400,128]{2,1,0:T(8,128)(2,1)} custom-call(bf16[128,2048]{1,0:T(8,128)(2,1)} %bitcast.38, bf16[128,2048]{1,0:T(8,128)(2,1)} %bitcast.39, bf16[128,2048]{1,0:T(8,128)(2,1)} %bitcast.40, s32[1,128]{1,0:T(1,128)} %seg_ref.1), custom_call_target="tpu_custom_call" | custom-call | tf_op jit(solution)/shard_map/pack/pallas_call | solution.py:282
  3.8 7.8 %all-to-all-start = ((bf16[16,400,128]{2,1,0:T(8,128)(2,1)}), bf16[16,400,128]{2,1,0:T(8,128)(2,1)S(1)}, u32[]{:S(2)}, u32[]{:S(2)}) async-start(bf16[16,400,128]{2,1,0:T(8,128)(2,1)} %pack.1), calls=%async_computation | async-start | bytes 3276800 | tf_op jit(solution)/shard_map/all_to_all | solution.py:291
  11.6 3.1 %collective-permute-start.11 = (bf16[704,2048]{1,0:T(8,128)(2,1)}, bf16[704,2048]{1,0:T(8,128)(2,1)}, u32[]{:S(2)}, u32[]{:S(2)}) collective-permute-start(bf16[704,2048]{1,0:T(8,128)(2,1)} %bitcast.41), channel_id=1, source_target_pairs={{0,16},{1,24},{2,18},{3,26},{4,20},{5,28},{6,22},{7,30},{8,17},{9,... | collective-permute-start | bytes 8650760 | tf_op jit(solution)/shard_map/ppermute | solution.py:279
  14.7 3.5 %slice_bitcast_fusion = bf16[960,1408]{1,0:T(8,128)(2,1)} fusion(bf16[1,2048,1408]{2,1,0:T(8,128)(2,1)} %param.20), kind=kLoop, calls=%fused_computation | loop fusion | bytes 5406720 | tf_op jit(solution)/shard_map/slice | solution.py:275
  18.3 15.3 %all-to-all-done.x_ref = bf16[16,400,128]{2,1,0:T(8,128)(2,1)S(1)} async-done(((bf16[16,400,128]{2,1,0:T(8,128)(2,1)}), bf16[16,400,128]{2,1,0:T(8,128)(2,1)S(1)}, u32[]{:S(2)}, u32[]{:S(2)}) %all-to-all-start) | async-done | bytes 1638432 | tf_op jit(solution)/shard_map/all_to_all | solution.py:291
  33.6 5.2 %attend.1 = bf16[16,128,128]{2,1,0:T(8,128)(2,1)} custom-call(bf16[16,400,128]{2,1,0:T(8,128)(2,1)S(1)} %all-to-all-done.x_ref), custom_call_target="tpu_custom_call" | custom-call | tf_op jit(solution)/shard_map/attend/pallas_call | solution.py:292
  38.8 4.3 %all-to-all-start.1 = ((bf16[16,128,128]{2,1,0:T(8,128)(2,1)}), bf16[16,128,128]{2,1,0:T(8,128)(2,1)S(1)}, u32[]{:S(2)}, u32[]{:S(2)}) async-start(bf16[16,128,128]{2,1,0:T(8,128)(2,1)} %attend.1), calls=%async_computation.1 | async-start | bytes 1048576 | tf_op jit(solution)/shard_map/all_to_all | solution.py:300
  43.8 2.0 route.1
  45.8 53.5 %all-to-all-done.1.heads_ref = bf16[16,128,128]{2,1,0:T(8,128)(2,1)S(1)} async-done(((bf16[16,128,128]{2,1,0:T(8,128)(2,1)}), bf16[16,128,128]{2,1,0:T(8,128)(2,1)S(1)}, u32[]{:S(2)}, u32[]{:S(2)}) %all-to-all-start.1) | async-done | bytes 524320 | tf_op jit(solution)/shard_map/all_to_all | solution.py:300
  100.2 6.8 %project.1 = (bf16[128,2048]{1,0:T(8,128)(2,1)S(1)}, bf16[144,2048]{1,0:T(8,128)(2,1)S(1)}, bf16[144,2048]{1,0:T(8,128)(2,1)S(1)}, bf16[144,2048]{1,0:T(8,128)(2,1)S(1)}, bf16[16,16,2048]{2,1,0:T(8,128)(2,1)}) custom-call(bf16[16,128,128]{2,1,0:T(8,128)(2,1)S(1)} %all-to-all-done.1.heads_ref, bf16[2048,2048]{1,0:T(8,128)(2,1)} %weight_ref.1, ...), custom_call_target="tpu_custom_call" | custom-call | tf_op jit(solution)/shard_map/project/pallas_call | solution.py:314
  107.8 4.8 %all-to-all-start.2 = ((bf16[16,16,2048]{2,1,0:T(8,128)(2,1)}), bf16[16,16,2048]{2,1,0:T(8,128)(2,1)S(1)}, u32[]{:S(2)}, u32[]{:S(2)}) async-start(bf16[16,16,2048]{2,1,0:T(8,128)(2,1)} %get-tuple-element.13), calls=%async_computation.2 | async-start | bytes 2097152 | tf_op jit(solution)/shard_map/all_to_all | solution.py:345
  113.2 2.9 collective-permute-start.9
  116.1 1.5 collective-permute-start.10
  117.6 10.0 %collective-permute-done.8.near_ref = bf16[144,2048]{1,0:T(8,128)(2,1)S(1)} collective-permute-done((bf16[144,2048]{1,0:T(8,128)(2,1)S(1)}, bf16[144,2048]{1,0:T(8,128)(2,1)S(1)}, u32[]{:S(2)}, u32[]{:S(2)}) %collective-permute-start.8) | collective-permute-done | bytes 589856 | tf_op jit(solution)/shard_map/ppermute | solution.py:344
  127.6 13.9 %collective-permute-done.9.far_ref = bf16[144,2048]{1,0:T(8,128)(2,1)S(1)} collective-permute-done((bf16[144,2048]{1,0:T(8,128)(2,1)S(1)}, bf16[144,2048]{1,0:T(8,128)(2,1)S(1)}, u32[]{:S(2)}, u32[]{:S(2)}) %collective-permute-start.9) | collective-permute-done | bytes 589856 | tf_op jit(solution)/shard_map/ppermute | solution.py:344
  141.5 2.1 fill.1
  143.6 1.6 collective-permute-start.7
  146.3 6.6 %all-to-all-start.3 = ((bf16[16,48,2048]{2,1,0:T(8,128)(2,1)}), bf16[16,48,2048]{2,1,0:T(8,128)(2,1)S(1)}, u32[]{:S(2)}, u32[]{:S(2)}) async-start(bf16[16,48,2048]{2,1,0:T(8,128)(2,1)} %bitcast.37), calls=%async_computation.3 | async-start | bytes 6291456 | tf_op jit(solution)/shard_map/all_to_all | solution.py:359
  152.9 1.5 slice_bitcast_fusion.1
  154.4 2.9 collective-permute-start.2
  157.3 1.3 slice_bitcast_fusion.2
  160.0 2.9 collective-permute-start
  162.9 9.6 %collective-permute-done.2.refs_2_ = bf16[448,1408]{1,0:T(8,128)(2,1)S(1)} collective-permute-done((bf16[448,1408]{1,0:T(8,128)(2,1)S(1)}, bf16[448,1408]{1,0:T(8,128)(2,1)S(1)}, u32[]{:S(2)}, u32[]{:S(2)}) %collective-permute-start.2) | collective-permute-done | bytes 1261600 | tf_op jit(solution)/shard_map/ppermute | solution.py:276
  172.5 11.6 %collective-permute-done.1.refs_1_ = bf16[384,1408]{1,0:T(8,128)(2,1)S(1)} collective-permute-done((bf16[384,1408]{1,0:T(8,128)(2,1)S(1)}, bf16[384,1408]{1,0:T(8,128)(2,1)S(1)}, u32[]{:S(2)}, u32[]{:S(2)}) %collective-permute-start.1) | collective-permute-done | bytes 1081376 | tf_op jit(solution)/shard_map/ppermute | solution.py:276
  184.1 7.5 %collective-permute-done.refs_0_ = bf16[256,1408]{1,0:T(8,128)(2,1)S(1)} collective-permute-done((bf16[256,1408]{1,0:T(8,128)(2,1)S(1)}, bf16[256,1408]{1,0:T(8,128)(2,1)S(1)}, u32[]{:S(2)}, u32[]{:S(2)}) %collective-permute-start) | collective-permute-done | bytes 720928 | tf_op jit(solution)/shard_map/ppermute | solution.py:276
  191.6 4.4 %shard_map.109.own_a = bf16[256,704]{1,0:T(8,128)(2,1)S(1)} custom-call(bf16[256,2048]{1,0:T(8,128)(2,1)S(1)} %bitcast.33, bf16[256,1408]{1,0:T(8,128)(2,1)S(1)} %collective-permute-done.refs_0_, bf16[384,1408]{1,0:T(8,128)(2,1)S(1)} %collective-permute-done.1.refs_1_, bf16[448,1408]{1,0:T(8,128)(2,1)S(1)} %collective-permute-done.2.refs_2_, ...), custom_call_target="tpu_custom_call" | custom-call | tf_op jit(solution)/shard_map/pallas_call | solution.py:366
  196.1 4.4 %shard_map.110.own_b = bf16[256,704]{1,0:T(8,128)(2,1)S(1)} custom-call(bf16[256,2048]{1,0:T(8,128)(2,1)S(1)} %bitcast.34, bf16[256,1408]{1,0:T(8,128)(2,1)S(1)} %collective-permute-done.4.refs_0_, bf16[384,1408]{1,0:T(8,128)(2,1)S(1)} %collective-permute-done.5.refs_1_, bf16[448,1408]{1,0:T(8,128)(2,1)S(1)} %collective-permute-done.6.refs_2_, ...), custom_call_target="tpu_custom_call" | custom-call | tf_op jit(solution)/shard_map/pallas_call | solution.py:366
  207.9 7.9 %shard_map.111.rest_a = bf16[768,704]{1,0:T(8,128)(2,1)S(1)} custom-call(bf16[768,2048]{1,0:T(8,128)(2,1)S(1)} %bitcast.29, bf16[256,1408]{1,0:T(8,128)(2,1)S(1)} %copy-done.11, bf16[384,1408]{1,0:T(8,128)(2,1)S(1)} %copy-done.7, bf16[448,1408]{1,0:T(8,128)(2,1)S(1)} %copy-done.3, bf16[960,1408]{1,0:T(8,128)(2,1)} %collective-permute-done.3.refs_3_), custom_call_target="tpu_custom_call" | custom-call | tf_op jit(solution)/shard_map/pallas_call | solution.py:366
  215.8 7.9 %shard_map.112.rest_b = bf16[768,704]{1,0:T(8,128)(2,1)S(1)} custom-call(bf16[768,2048]{1,0:T(8,128)(2,1)S(1)} %bitcast.30, bf16[256,1408]{1,0:T(8,128)(2,1)S(1)} %copy-done.13, bf16[384,1408]{1,0:T(8,128)(2,1)S(1)} %copy-done.9, bf16[448,1408]{1,0:T(8,128)(2,1)S(1)} %copy-done.5, bf16[960,1408]{1,0:T(8,128)(2,1)} %collective-permute-done.7.refs_3_), custom_call_target="tpu_custom_call" | custom-call | tf_op jit(solution)/shard_map/pallas_call | solution.py:366
  223.7 9.3 %down.1 = bf16[4,2,4,2,16,2048]{5,4,3,2,1,0:T(8,128)(2,1)S(1)} custom-call(s32[1]{0:T(128)} %bitcast.y_ref, bf16[256,704]{1,0:T(8,128)(2,1)S(1)} %shard_map.109.own_a, bf16[256,704]{1,0:T(8,128)(2,1)S(1)} %copy-done.15, bf16[768,704]{1,0:T(8,128)(2,1)S(1)} %shard_map.111.rest_a, bf16[768,704]{1,0:T(8,128)(2,1)S(1)} %shard_map.112.rest_b, ...), custom_call_target="tpu_custom_call" | custom-call | tf_op jit(solution)/shard_map/down/pallas_call | solution.py:382
  233.1 62.3 %all_to_all.25 = bf16[64,16,2048]{2,1,0:T(8,128)(2,1)S(1)} all-to-all(bf16[64,16,2048]{2,1,0:T(8,128)(2,1)S(1)} %bitcast.31), channel_id=1, replica_groups=mesh['z'=4,'yl'=2,'c'=2,'x'=4,'yh'=2] {'z','yl','x','yh'}, dimensions={0} | all-to-all | bytes 8388608 | tf_op jit(solution)/shard_map/all_to_all | solution.py:390
  295.4 1.8 combine.1
  (67 shorter events, 12.9 us)
Async XLA Ops:
  3.8 29.9 %all-to-all-start = ((bf16[16,400,128]{2,1,0:T(8,128)(2,1)}), bf16[16,400,128]{2,1,0:T(8,128)(2,1)S(1)}, u32[]{:S(2)}, u32[]{:S(2)}) async-start(bf16[16,400,128]{2,1,0:T(8,128)(2,1)} %pack.1), calls=%async_computation | async-start | bytes 3276800 | tf_op jit(solution)/shard_map/all_to_all | solution.py:291
  11.6 133.6 %collective-permute-start.11 = (bf16[704,2048]{1,0:T(8,128)(2,1)}, bf16[704,2048]{1,0:T(8,128)(2,1)}, u32[]{:S(2)}, u32[]{:S(2)}) collective-permute-start(bf16[704,2048]{1,0:T(8,128)(2,1)} %bitcast.41), channel_id=1, source_target_pairs={{0,16},{1,24},{2,18},{3,26},{4,20},{5,28},{6,22},{7,30},{8,17},{9,... | collective-permute-start | bytes 8650760 | tf_op jit(solution)/shard_map/ppermute | solution.py:279
  18.2 25.0 %copy-start.22 = (s32[1,128,6]{1,0,2:T(1,128)S(1)}, s32[1,128,6]{1,0,2:T(1,128)}, u32[]{:S(2)}) copy-start(s32[1,128,6]{1,0,2:T(1,128)} %param.19) | copy-start | bytes 9220
  18.2 25.0 %copy-start.23 = (s32[1,128,6]{1,0,2:T(1,128)S(1)}, s32[1,128,6]{1,0,2:T(1,128)}, u32[]{:S(2)}) copy-start(s32[1,128,6]{1,0,2:T(1,128)} %param.18) | copy-start | bytes 9220
  18.2 81.1 %copy-start.16 = (bf16[1,128,2048]{2,1,0:T(8,128)(2,1)S(1)}, bf16[1,128,2048]{2,1,0:T(8,128)(2,1)}, u32[]{:S(2)}) copy-start(bf16[1,128,2048]{2,1,0:T(8,128)(2,1)} %param.15) | copy-start | bytes 1572868
  18.2 81.1 %copy-start.21 = (f32[2048]{0:T(1024)S(1)}, f32[2048]{0:T(1024)}, u32[]{:S(2)}) copy-start(f32[2048]{0:T(1024)} %param.17) | copy-start | bytes 24580
  18.2 125.4 %collective-permute-start.3 = (bf16[960,1408]{1,0:T(8,128)(2,1)}, bf16[960,1408]{1,0:T(8,128)(2,1)}, u32[]{:S(2)}, u32[]{:S(2)}) collective-permute-start(bf16[960,1408]{1,0:T(8,128)(2,1)} %slice_bitcast_fusion), channel_id=1, source_target_pairs={{0,16},{1,24},{2,18},{3,26},{4,20},{5,28},{6,22},{7,30},{8,17},{9,... | collective-permute-start | bytes 8110088 | tf_op jit(solution)/shard_map/ppermute | solution.py:276
  38.8 60.4 %all-to-all-start.1 = ((bf16[16,128,128]{2,1,0:T(8,128)(2,1)}), bf16[16,128,128]{2,1,0:T(8,128)(2,1)S(1)}, u32[]{:S(2)}, u32[]{:S(2)}) async-start(bf16[16,128,128]{2,1,0:T(8,128)(2,1)} %attend.1), calls=%async_computation.1 | async-start | bytes 1048576 | tf_op jit(solution)/shard_map/all_to_all | solution.py:300
  107.8 37.5 %all-to-all-start.2 = ((bf16[16,16,2048]{2,1,0:T(8,128)(2,1)}), bf16[16,16,2048]{2,1,0:T(8,128)(2,1)S(1)}, u32[]{:S(2)}, u32[]{:S(2)}) async-start(bf16[16,16,2048]{2,1,0:T(8,128)(2,1)} %get-tuple-element.13), calls=%async_computation.2 | async-start | bytes 2097152 | tf_op jit(solution)/shard_map/all_to_all | solution.py:345
  112.6 15.0 %collective-permute-start.8 = (bf16[144,2048]{1,0:T(8,128)(2,1)S(1)}, bf16[144,2048]{1,0:T(8,128)(2,1)S(1)}, u32[]{:S(2)}, u32[]{:S(2)}) collective-permute-start(bf16[144,2048]{1,0:T(8,128)(2,1)S(1)} %get-tuple-element.14), channel_id=1, source_target_pairs={{0,16},{1,17},{2,18},{3,19},{4,20},{5,21},{6,22},{7,23},{8,24},{9,... | collective-permute-start | bytes 1769480 | tf_op jit(solution)/shard_map/ppermute | solution.py:344
  113.2 28.3 %collective-permute-start.9 = (bf16[144,2048]{1,0:T(8,128)(2,1)S(1)}, bf16[144,2048]{1,0:T(8,128)(2,1)S(1)}, u32[]{:S(2)}, u32[]{:S(2)}) collective-permute-start(bf16[144,2048]{1,0:T(8,128)(2,1)S(1)} %get-tuple-element.15), channel_id=1, source_target_pairs={{0,1},{1,0},{2,3},{3,2},{4,5},{5,4},{6,7},{7,6},{8,9},{9,8},{10,11... | collective-permute-start | bytes 1769480 | tf_op jit(solution)/shard_map/ppermute | solution.py:344
  116.1 25.4 %collective-permute-start.10 = (bf16[144,2048]{1,0:T(8,128)(2,1)S(1)}, bf16[144,2048]{1,0:T(8,128)(2,1)S(1)}, u32[]{:S(2)}, u32[]{:S(2)}) collective-permute-start(bf16[144,2048]{1,0:T(8,128)(2,1)S(1)} %get-tuple-element.16), channel_id=1, source_target_pairs={{0,17},{1,16},{2,19},{3,18},{4,21},{5,20},{6,23},{7,22},{8,25},{9,... | collective-permute-start | bytes 1769480 | tf_op jit(solution)/shard_map/ppermute | solution.py:344
  143.6 52.5 %collective-permute-start.7 = (bf16[960,1408]{1,0:T(8,128)(2,1)}, bf16[960,1408]{1,0:T(8,128)(2,1)}, u32[]{:S(2)}, u32[]{:S(2)}) collective-permute-start(bf16[960,1408]{1,0:T(8,128)(2,1)} %collective-permute-done.3.refs_3_), channel_id=1, source_target_pairs={{0,8},{1,9},{2,10},{3,11},{4,12},{5,13},{6,14},{7,15},{8,0},{9,1},... | collective-permute-start | bytes 8110088 | tf_op jit(solution)/shard_map/ppermute | solution.py:277
  145.2 78.5 %collective-permute-start.12 = (bf16[704,2048]{1,0:T(8,128)(2,1)}, bf16[704,2048]{1,0:T(8,128)(2,1)}, u32[]{:S(2)}, u32[]{:S(2)}) collective-permute-start(bf16[704,2048]{1,0:T(8,128)(2,1)} %collective-permute-done.11.down_a), channel_id=1, source_target_pairs={{0,8},{1,9},{2,10},{3,11},{4,12},{5,13},{6,14},{7,15},{8,0},{9,1},... | collective-permute-start | bytes 8650760 | tf_op jit(solution)/shard_map/ppermute | solution.py:280
  146.3 57.9 %all-to-all-start.3 = ((bf16[16,48,2048]{2,1,0:T(8,128)(2,1)}), bf16[16,48,2048]{2,1,0:T(8,128)(2,1)S(1)}, u32[]{:S(2)}, u32[]{:S(2)}) async-start(bf16[16,48,2048]{2,1,0:T(8,128)(2,1)} %bitcast.37), calls=%async_computation.3 | async-start | bytes 6291456 | tf_op jit(solution)/shard_map/all_to_all | solution.py:359
  152.9 38.7 %copy-start.1 = (bf16[16,16,2048]{2,1,0:T(8,128)(2,1)S(1)}, bf16[16,16,2048]{2,1,0:T(8,128)(2,1)}, u32[]{:S(2)}) copy-start(bf16[16,16,2048]{2,1,0:T(8,128)(2,1)} %copy-done) | copy-start | bytes 3145732
  154.4 18.1 %collective-permute-start.2 = (bf16[448,1408]{1,0:T(8,128)(2,1)S(1)}, bf16[448,1408]{1,0:T(8,128)(2,1)S(1)}, u32[]{:S(2)}, u32[]{:S(2)}) collective-permute-start(bf16[448,1408]{1,0:T(8,128)(2,1)S(1)} %slice_bitcast_fusion.1), channel_id=1, source_target_pairs={{0,16},{1,24},{2,18},{3,26},{4,20},{5,28},{6,22},{7,30},{8,17},{9,... | collective-permute-start | bytes 3784712 | tf_op jit(solution)/shard_map/ppermute | solution.py:276
  158.6 25.5 %collective-permute-start.1 = (bf16[384,1408]{1,0:T(8,128)(2,1)S(1)}, bf16[384,1408]{1,0:T(8,128)(2,1)S(1)}, u32[]{:S(2)}, u32[]{:S(2)}) collective-permute-start(bf16[384,1408]{1,0:T(8,128)(2,1)S(1)} %slice_bitcast_fusion.2), channel_id=1, source_target_pairs={{0,16},{1,24},{2,18},{3,26},{4,20},{5,28},{6,22},{7,30},{8,17},{9,... | collective-permute-start | bytes 3244040 | tf_op jit(solution)/shard_map/ppermute | solution.py:276
  160.0 31.6 %collective-permute-start = (bf16[256,1408]{1,0:T(8,128)(2,1)S(1)}, bf16[256,1408]{1,0:T(8,128)(2,1)S(1)}, u32[]{:S(2)}, u32[]{:S(2)}) collective-permute-start(bf16[256,1408]{1,0:T(8,128)(2,1)S(1)} %slice_bitcast_fusion.3), channel_id=1, source_target_pairs={{0,16},{1,24},{2,18},{3,26},{4,20},{5,28},{6,22},{7,30},{8,17},{9,... | collective-permute-start | bytes 2162696 | tf_op jit(solution)/shard_map/ppermute | solution.py:276
  172.5 23.5 %copy-start.2 = (bf16[448,1408]{1,0:T(8,128)(2,1)}, bf16[448,1408]{1,0:T(8,128)(2,1)S(1)}, u32[]{:S(2)}) copy-start(bf16[448,1408]{1,0:T(8,128)(2,1)S(1)} %collective-permute-done.2.refs_2_) | copy-start | bytes 3784708
  172.5 23.6 %collective-permute-start.6 = (bf16[448,1408]{1,0:T(8,128)(2,1)S(1)}, bf16[448,1408]{1,0:T(8,128)(2,1)S(1)}, u32[]{:S(2)}, u32[]{:S(2)}) collective-permute-start(bf16[448,1408]{1,0:T(8,128)(2,1)S(1)} %collective-permute-done.2.refs_2_), channel_id=1, source_target_pairs={{0,8},{1,9},{2,10},{3,11},{4,12},{5,13},{6,14},{7,15},{8,0},{9,1},... | collective-permute-start | bytes 3784712 | tf_op jit(solution)/shard_map/ppermute | solution.py:277
  184.1 12.0 %copy-start.6 = (bf16[384,1408]{1,0:T(8,128)(2,1)}, bf16[384,1408]{1,0:T(8,128)(2,1)S(1)}, u32[]{:S(2)}) copy-start(bf16[384,1408]{1,0:T(8,128)(2,1)S(1)} %collective-permute-done.1.refs_1_) | copy-start | bytes 3244036
  184.1 12.0 %collective-permute-start.5 = (bf16[384,1408]{1,0:T(8,128)(2,1)S(1)}, bf16[384,1408]{1,0:T(8,128)(2,1)S(1)}, u32[]{:S(2)}, u32[]{:S(2)}) collective-permute-start(bf16[384,1408]{1,0:T(8,128)(2,1)S(1)} %collective-permute-done.1.refs_1_), channel_id=1, source_target_pairs={{0,8},{1,9},{2,10},{3,11},{4,12},{5,13},{6,14},{7,15},{8,0},{9,1},... | collective-permute-start | bytes 3244040 | tf_op jit(solution)/shard_map/ppermute | solution.py:277
  191.6 4.5 %copy-start.10 = (bf16[256,1408]{1,0:T(8,128)(2,1)}, bf16[256,1408]{1,0:T(8,128)(2,1)S(1)}, u32[]{:S(2)}) copy-start(bf16[256,1408]{1,0:T(8,128)(2,1)S(1)} %collective-permute-done.refs_0_) | copy-start | bytes 2162692
  191.6 4.5 %collective-permute-start.4 = (bf16[256,1408]{1,0:T(8,128)(2,1)S(1)}, bf16[256,1408]{1,0:T(8,128)(2,1)S(1)}, u32[]{:S(2)}, u32[]{:S(2)}) collective-permute-start(bf16[256,1408]{1,0:T(8,128)(2,1)S(1)} %collective-permute-done.refs_0_), channel_id=1, source_target_pairs={{0,8},{1,9},{2,10},{3,11},{4,12},{5,13},{6,14},{7,15},{8,0},{9,1},... | collective-permute-start | bytes 2162696 | tf_op jit(solution)/shard_map/ppermute | solution.py:277
  204.2 1.3 copy-start.3
  207.8 7.9 %copy-start.5 = (bf16[448,1408]{1,0:T(8,128)(2,1)S(1)}, bf16[448,1408]{1,0:T(8,128)(2,1)}, u32[]{:S(2)}) copy-start(bf16[448,1408]{1,0:T(8,128)(2,1)} %copy-done.4) | copy-start | bytes 3784708
  207.8 7.9 %copy-start.9 = (bf16[384,1408]{1,0:T(8,128)(2,1)S(1)}, bf16[384,1408]{1,0:T(8,128)(2,1)}, u32[]{:S(2)}) copy-start(bf16[384,1408]{1,0:T(8,128)(2,1)} %copy-done.8) | copy-start | bytes 3244036
  207.9 7.9 %copy-start.13 = (bf16[256,1408]{1,0:T(8,128)(2,1)S(1)}, bf16[256,1408]{1,0:T(8,128)(2,1)}, u32[]{:S(2)}) copy-start(bf16[256,1408]{1,0:T(8,128)(2,1)} %copy-done.12) | copy-start | bytes 2162692
  215.8 8.0 %copy-start.15 = (bf16[256,704]{1,0:T(8,128)(2,1)S(1)}, bf16[256,704]{1,0:T(8,128)(2,1)}, u32[]{:S(2)}) copy-start(bf16[256,704]{1,0:T(8,128)(2,1)} %copy-done.14) | copy-start | bytes 1081348
  233.1 62.3 %copy-start.18 = (bf16[128,2048]{1,0:T(8,128)(2,1)S(1)}, bf16[128,2048]{1,0:T(8,128)(2,1)}, u32[]{:S(2)}) copy-start(bf16[128,2048]{1,0:T(8,128)(2,1)} %copy-done.17) | copy-start | bytes 1572868
  233.1 62.3 %copy-start.20 = (bf16[1024,128]{1,0:T(8,128)(2,1)S(1)}, bf16[1024,128]{1,0:T(8,128)(2,1)}, u32[]{:S(2)}) copy-start(bf16[1024,128]{1,0:T(8,128)(2,1)} %get-tuple-element.17.weight_ref) | copy-start | bytes 786436
  (9 other events, 8.7 us)

commit v8 on v7

--- a/solution.py
+++ b/solution.py
@@ -1,3 +1,4 @@
+import functools
 import math
 
 import jax
@@ -21,7 +22,6 @@
 PACK_ROWS = 3 * ROWS + SEG_ROWS
 Q_BLOCK = 256
 X_BLOCK = 256
-PACK_STEPS = 4
 PIECES = (256, 384, 448, 960)
 SPOTS = 16
 Y_SIZE = 4
@@ -76,7 +76,7 @@
 
 def pack_kernel(q_ref, k_ref, v_ref, seg_ref, out_ref):
     seg = jnp.broadcast_to(seg_ref[...].astype(f32), (SEG_ROWS, ROWS)).astype(bf16)
-    for head in range(HEADS // PACK_STEPS):
+    for head in range(HEADS):
         lanes = slice(head * HEAD_DIM, (head + 1) * HEAD_DIM)
         out_ref[head, 0:ROWS, :] = q_ref[:, lanes]
         out_ref[head, ROWS : 2 * ROWS, :] = k_ref[:, lanes]
@@ -210,7 +210,7 @@
     return (unit - SPOTS) // 3, (3, 1, 2)[(unit - SPOTS) % 3]
 
 
-def inner_kernel(rows_ref, *refs):
+def inner_kernel(early, rows_ref, *refs):
     pieces = len(PIECES)
     parts, (act, w_in, sems) = refs[:pieces], refs[pieces:]
     copies, start = [], 0
@@ -220,24 +220,35 @@
         start += count
     for copy in copies:
         copy.start()
-    for copy in copies:
+    for copy in copies[: pieces - early]:
         copy.wait()
+    depth = D - PIECES[-1]
     for block in range(rows_ref.shape[0] // X_BLOCK):
         span = slice(block * X_BLOCK, (block + 1) * X_BLOCK)
-        inner = jnp.dot(rows_ref[span, :], w_in[...], preferred_element_type=f32)
+        if block == 0 and early:
+            inner = jnp.dot(rows_ref[span, :depth], w_in[:depth, :], preferred_element_type=f32)
+            copies[-1].wait()
+            rows = rows_ref[span, depth:]
+            inner = inner + jnp.dot(rows, w_in[depth:, :], preferred_element_type=f32)
+        else:
+            inner = jnp.dot(rows_ref[span, :], w_in[...], preferred_element_type=f32)
         gate = inner[:, :HALF]
         up = pltpu.roll(inner, HALF, axis=1)[:, :HALF]
         act[span, :] = (gate / (1.0 + jnp.exp(-gate)) * up).astype(bf16)
 
 
-def down_kernel(y_ref, own_a, own_b, rest_a, rest_b, down_a, down_b, out_ref):
+def down_kernel(y_ref, own_a, own_b, rest_a, rest_b, down_any, down_b, out_ref, down_a, sem):
     y = y_ref[0]
+    load = pltpu.make_async_copy(down_any, down_a, sem)
+    load.start()
     units = X_BLOCK // SLOTS
     for block in range(EXPERTS * SLOTS // X_BLOCK):
         act_a, act_b, first = (own_a, own_b, 0) if block == 0 else (rest_a, rest_b, block - 1)
         span = slice(first * X_BLOCK, (first + 1) * X_BLOCK)
-        total = jnp.dot(act_a[span, :], down_a[...], preferred_element_type=f32)
-        total = total + jnp.dot(act_b[span, :], down_b[...], preferred_element_type=f32)
+        total = jnp.dot(act_b[span, :], down_b[...], preferred_element_type=f32)
+        if block == 0:
+            load.wait()
+        total = total + jnp.dot(act_a[span, :], down_a[...], preferred_element_type=f32)
         total = total.astype(bf16)
         for near in range(units):
             spot, ahead = origin(block * units + near)
@@ -278,13 +289,11 @@
         start += count
     moved_down = lax.ppermute(w_down[0], AXES, moves(weight_target))
     other_down = lax.ppermute(moved_down, AXES, moves(core_target))
-    wide = pl.BlockSpec((ROWS, D // PACK_STEPS), lambda i: (0, i))
     packed = pl.pallas_call(
         pack_kernel,
-        grid=(PACK_STEPS,),
         out_shape=shape((HEADS, PACK_ROWS, HEAD_DIM), bf16),
-        in_specs=[wide, wide, wide, pl.BlockSpec((1, ROWS), lambda i: (0, 0))],
-        out_specs=pl.BlockSpec((HEADS // PACK_STEPS, PACK_ROWS, HEAD_DIM), lambda i: (i, 0, 0)),
+        in_specs=[VMEM] * 4,
+        out_specs=VMEM,
         compiler_params=params(60),
         name="pack",
     )(queries[0], keys[0], values[0], segment_ids)
@@ -361,10 +370,10 @@
     )
     anywhere = pl.BlockSpec(memory_space=pl.ANY)
 
-    def inner(rows, parts):
+    def inner(name, rows, parts):
         rows = rows.reshape(-1, D)
         return pl.pallas_call(
-            inner_kernel,
+            functools.partial(inner_kernel, name == "rest_a"),
             out_shape=shape((rows.shape[0], HALF), bf16),
             in_specs=[VMEM] + [anywhere] * len(PIECES),
             out_specs=VMEM,
@@ -375,15 +384,16 @@
             compiler_params=params(32),
         )(rows, *parts)
 
-    own_a = inner(arrived_own, moved)
-    own_b = inner(arrived_own, other)
-    rest_a = inner(arrived, moved)
-    rest_b = inner(arrived, other)
+    own_a = inner("own_a", arrived_own, moved)
+    own_b = inner("own_b", arrived_own, other)
+    rest_a = inner("rest_a", arrived, moved)
+    rest_b = inner("rest_b", arrived, other)
     results = pl.pallas_call(
         down_kernel,
         out_shape=shape((4, 2, 4, 2, SLOTS, D), bf16),
-        in_specs=[SMEM] + [VMEM] * 6,
+        in_specs=[SMEM] + [VMEM] * 4 + [anywhere, VMEM],
         out_specs=VMEM,
+        scratch_shapes=[pltpu.VMEM((HALF, D), bf16), pltpu.SemaphoreType.DMA],
         compiler_params=params(32),
         name="down",
     )(y, own_a, own_b, rest_a, rest_b, moved_down, other_down)

time: 298 us -> 299 us (level)
  no operation moved by 1% of the time
where the time goes in v8:
time: 299 us; the launch traced here: 298 us
  waiting for transfers between devices  121 us (40%)
  blocking collectives  62.3 us (21%)
  Pallas kernels  56.1 us (19%)
  starting transfers between devices  39.5 us (13%)
  local copies, waits for them, and re-layouts  18.1 us (6%)
    all_to_all x1, blocking collectives, local(): lax.all_to_all(results.reshape(EXPERTS, SLOTS, D), PLACES, split_axis=0,...  62.3 us
    all_to_all x1, waiting for transfers between devices, local(): lax.all_to_all(attended, POSITIONS, split_axis=0, concat_axis=0, tiled=True)  53.5 us
    ppermute x4, waiting for transfers between devices, local(): moved.append(lax.ppermute(piece, AXES, moves(weight_target)))  28.7 us
    pallas_call x4, Pallas kernels, inner(): pl.pallas_call(functools.partial(inner_kernel, name == 'rest_a'), out_sha...  25 us
    ppermute x3, waiting for transfers between devices, local(): arriving.append(lax.ppermute(share, AXES, moves(along_y(distance))))  23.9 us
    all_to_all x1, waiting for transfers between devices, local(): lax.all_to_all(packed, POSITIONS, split_axis=0, concat_axis=0, tiled=True)  15.3 us
    pallas_call x1, Pallas kernels, local(): pl.pallas_call(down_kernel, out_shape=shape((4, 2, 4, 2, SLOTS, D), bf16)...  10.3 us
    unnamed x48, local copies, waits for them, and re-layouts  10 us
  transfers between devices with their start and end apart: 17, of which 7 were waited for; matrix products, arithmetic and copies ran while one was open for 3% of the time, Pallas kernels for 14%

profile of v8, /device:TPU:1, one launch (start us, length us, event | category | flops | bytes accessed | tf_op | source)
XLA Modules:
  0.0 297.6 jit_solution(6759180524884635936)
XLA Ops:
  0.0 2.9 pack.1
  2.9 7.8 %all-to-all-start = ((bf16[16,400,128]{2,1,0:T(8,128)(2,1)}), bf16[16,400,128]{2,1,0:T(8,128)(2,1)S(1)}, u32[]{:S(2)}, u32[]{:S(2)}) async-start(bf16[16,400,128]{2,1,0:T(8,128)(2,1)} %pack.1), calls=%async_computation | async-start | bytes 3276800 | tf_op jit(solution)/shard_map/all_to_all | solution.py:300
  10.7 3.1 %collective-permute-start.11 = (bf16[704,2048]{1,0:T(8,128)(2,1)}, bf16[704,2048]{1,0:T(8,128)(2,1)}, u32[]{:S(2)}, u32[]{:S(2)}) collective-permute-start(bf16[704,2048]{1,0:T(8,128)(2,1)} %bitcast.41), channel_id=1, source_target_pairs={{0,16},{1,24},{2,18},{3,26},{4,20},{5,28},{6,22},{7,30},{8,17},{9,... | collective-permute-start | bytes 8650760 | tf_op jit(solution)/shard_map/ppermute | solution.py:290
  13.8 3.5 %slice_bitcast_fusion = bf16[960,1408]{1,0:T(8,128)(2,1)} fusion(bf16[1,2048,1408]{2,1,0:T(8,128)(2,1)} %param.20), kind=kLoop, calls=%fused_computation | loop fusion | bytes 5406720 | tf_op jit(solution)/shard_map/slice | solution.py:286
  17.4 15.3 %all-to-all-done.x_ref = bf16[16,400,128]{2,1,0:T(8,128)(2,1)S(1)} async-done(((bf16[16,400,128]{2,1,0:T(8,128)(2,1)}), bf16[16,400,128]{2,1,0:T(8,128)(2,1)S(1)}, u32[]{:S(2)}, u32[]{:S(2)}) %all-to-all-start) | async-done | bytes 1638432 | tf_op jit(solution)/shard_map/all_to_all | solution.py:300
  32.7 5.2 %attend.1 = bf16[16,128,128]{2,1,0:T(8,128)(2,1)} custom-call(bf16[16,400,128]{2,1,0:T(8,128)(2,1)S(1)} %all-to-all-done.x_ref), custom_call_target="tpu_custom_call" | custom-call | tf_op jit(solution)/shard_map/attend/pallas_call | solution.py:301
  38.0 4.3 %all-to-all-start.1 = ((bf16[16,128,128]{2,1,0:T(8,128)(2,1)}), bf16[16,128,128]{2,1,0:T(8,128)(2,1)S(1)}, u32[]{:S(2)}, u32[]{:S(2)}) async-start(bf16[16,128,128]{2,1,0:T(8,128)(2,1)} %attend.1), calls=%async_computation.1 | async-start | bytes 1048576 | tf_op jit(solution)/shard_map/all_to_all | solution.py:309
  42.9 2.0 route.1
  44.9 53.5 %all-to-all-done.1.heads_ref = bf16[16,128,128]{2,1,0:T(8,128)(2,1)S(1)} async-done(((bf16[16,128,128]{2,1,0:T(8,128)(2,1)}), bf16[16,128,128]{2,1,0:T(8,128)(2,1)S(1)}, u32[]{:S(2)}, u32[]{:S(2)}) %all-to-all-start.1) | async-done | bytes 524320 | tf_op jit(solution)/shard_map/all_to_all | solution.py:309
  99.3 6.8 %project.1 = (bf16[128,2048]{1,0:T(8,128)(2,1)S(1)}, bf16[144,2048]{1,0:T(8,128)(2,1)S(1)}, bf16[144,2048]{1,0:T(8,128)(2,1)S(1)}, bf16[144,2048]{1,0:T(8,128)(2,1)S(1)}, bf16[16,16,2048]{2,1,0:T(8,128)(2,1)}) custom-call(bf16[16,128,128]{2,1,0:T(8,128)(2,1)S(1)} %all-to-all-done.1.heads_ref, bf16[2048,2048]{1,0:T(8,128)(2,1)} %weight_ref.1, ...), custom_call_target="tpu_custom_call" | custom-call | tf_op jit(solution)/shard_map/project/pallas_call | solution.py:323
  107.0 4.8 %all-to-all-start.2 = ((bf16[16,16,2048]{2,1,0:T(8,128)(2,1)}), bf16[16,16,2048]{2,1,0:T(8,128)(2,1)S(1)}, u32[]{:S(2)}, u32[]{:S(2)}) async-start(bf16[16,16,2048]{2,1,0:T(8,128)(2,1)} %get-tuple-element.13), calls=%async_computation.2 | async-start | bytes 2097152 | tf_op jit(solution)/shard_map/all_to_all | solution.py:354
  112.4 2.9 collective-permute-start.9
  115.3 1.5 collective-permute-start.10
  116.8 10.0 %collective-permute-done.8.near_ref = bf16[144,2048]{1,0:T(8,128)(2,1)S(1)} collective-permute-done((bf16[144,2048]{1,0:T(8,128)(2,1)S(1)}, bf16[144,2048]{1,0:T(8,128)(2,1)S(1)}, u32[]{:S(2)}, u32[]{:S(2)}) %collective-permute-start.8) | collective-permute-done | bytes 589856 | tf_op jit(solution)/shard_map/ppermute | solution.py:353
  126.8 13.9 %collective-permute-done.9.far_ref = bf16[144,2048]{1,0:T(8,128)(2,1)S(1)} collective-permute-done((bf16[144,2048]{1,0:T(8,128)(2,1)S(1)}, bf16[144,2048]{1,0:T(8,128)(2,1)S(1)}, u32[]{:S(2)}, u32[]{:S(2)}) %collective-permute-start.9) | collective-permute-done | bytes 589856 | tf_op jit(solution)/shard_map/ppermute | solution.py:353
  140.7 2.1 fill.1
  142.7 1.6 collective-permute-start.7
  145.4 6.6 %all-to-all-start.3 = ((bf16[16,48,2048]{2,1,0:T(8,128)(2,1)}), bf16[16,48,2048]{2,1,0:T(8,128)(2,1)S(1)}, u32[]{:S(2)}, u32[]{:S(2)}) async-start(bf16[16,48,2048]{2,1,0:T(8,128)(2,1)} %bitcast.37), calls=%async_computation.3 | async-start | bytes 6291456 | tf_op jit(solution)/shard_map/all_to_all | solution.py:368
  152.1 1.5 slice_bitcast_fusion.1
  153.5 2.9 collective-permute-start.2
  156.4 1.3 slice_bitcast_fusion.2
  159.1 2.9 collective-permute-start
  162.0 9.6 %collective-permute-done.2.refs_2_ = bf16[448,1408]{1,0:T(8,128)(2,1)S(1)} collective-permute-done((bf16[448,1408]{1,0:T(8,128)(2,1)S(1)}, bf16[448,1408]{1,0:T(8,128)(2,1)S(1)}, u32[]{:S(2)}, u32[]{:S(2)}) %collective-permute-start.2) | collective-permute-done | bytes 1261600 | tf_op jit(solution)/shard_map/ppermute | solution.py:287
  171.6 11.6 %collective-permute-done.1.refs_1_ = bf16[384,1408]{1,0:T(8,128)(2,1)S(1)} collective-permute-done((bf16[384,1408]{1,0:T(8,128)(2,1)S(1)}, bf16[384,1408]{1,0:T(8,128)(2,1)S(1)}, u32[]{:S(2)}, u32[]{:S(2)}) %collective-permute-start.1) | collective-permute-done | bytes 1081376 | tf_op jit(solution)/shard_map/ppermute | solution.py:287
  183.2 7.5 %collective-permute-done.refs_0_ = bf16[256,1408]{1,0:T(8,128)(2,1)S(1)} collective-permute-done((bf16[256,1408]{1,0:T(8,128)(2,1)S(1)}, bf16[256,1408]{1,0:T(8,128)(2,1)S(1)}, u32[]{:S(2)}, u32[]{:S(2)}) %collective-permute-start) | collective-permute-done | bytes 720928 | tf_op jit(solution)/shard_map/ppermute | solution.py:287
  190.7 4.4 %shard_map.109.own_a = bf16[256,704]{1,0:T(8,128)(2,1)S(1)} custom-call(bf16[256,2048]{1,0:T(8,128)(2,1)S(1)} %bitcast.33, bf16[256,1408]{1,0:T(8,128)(2,1)S(1)} %collective-permute-done.refs_0_, bf16[384,1408]{1,0:T(8,128)(2,1)S(1)} %collective-permute-done.1.refs_1_, bf16[448,1408]{1,0:T(8,128)(2,1)S(1)} %collective-permute-done.2.refs_2_, ...), custom_call_target="tpu_custom_call" | custom-call | tf_op jit(solution)/shard_map/pallas_call | solution.py:375
  195.2 4.4 %shard_map.110.own_b = bf16[256,704]{1,0:T(8,128)(2,1)S(1)} custom-call(bf16[256,2048]{1,0:T(8,128)(2,1)S(1)} %bitcast.34, bf16[256,1408]{1,0:T(8,128)(2,1)S(1)} %collective-permute-done.4.refs_0_, bf16[384,1408]{1,0:T(8,128)(2,1)S(1)} %collective-permute-done.5.refs_1_, bf16[448,1408]{1,0:T(8,128)(2,1)S(1)} %collective-permute-done.6.refs_2_, ...), custom_call_target="tpu_custom_call" | custom-call | tf_op jit(solution)/shard_map/pallas_call | solution.py:375
  207.0 8.1 %shard_map.111.rest_a = bf16[768,704]{1,0:T(8,128)(2,1)S(1)} custom-call(bf16[768,2048]{1,0:T(8,128)(2,1)S(1)} %bitcast.29, bf16[256,1408]{1,0:T(8,128)(2,1)S(1)} %copy-done.11, bf16[384,1408]{1,0:T(8,128)(2,1)S(1)} %copy-done.7, bf16[448,1408]{1,0:T(8,128)(2,1)S(1)} %copy-done.3, bf16[960,1408]{1,0:T(8,128)(2,1)} %collective-permute-done.3.refs_3_), custom_call_target="tpu_custom_call" | custom-call | tf_op jit(solution)/shard_map/pallas_call | solution.py:375
  215.2 7.9 %shard_map.112.rest_b = bf16[768,704]{1,0:T(8,128)(2,1)S(1)} custom-call(bf16[768,2048]{1,0:T(8,128)(2,1)S(1)} %bitcast.30, bf16[256,1408]{1,0:T(8,128)(2,1)S(1)} %copy-done.13, bf16[384,1408]{1,0:T(8,128)(2,1)S(1)} %copy-done.9, bf16[448,1408]{1,0:T(8,128)(2,1)S(1)} %copy-done.5, bf16[960,1408]{1,0:T(8,128)(2,1)} %collective-permute-done.7.refs_3_), custom_call_target="tpu_custom_call" | custom-call | tf_op jit(solution)/shard_map/pallas_call | solution.py:375
  223.1 10.3 %down.1 = bf16[4,2,4,2,16,2048]{5,4,3,2,1,0:T(8,128)(2,1)S(1)} custom-call(s32[1]{0:T(128)} %bitcast.y_ref, bf16[256,704]{1,0:T(8,128)(2,1)S(1)} %shard_map.109.own_a, bf16[256,704]{1,0:T(8,128)(2,1)S(1)} %copy-done.15, bf16[768,704]{1,0:T(8,128)(2,1)S(1)} %shard_map.111.rest_a, bf16[768,704]{1,0:T(8,128)(2,1)S(1)} %shard_map.112.rest_b, ...), custom_call_target="tpu_custom_call" | custom-call | tf_op jit(solution)/shard_map/down/pallas_call | solution.py:391
  233.5 62.3 %all_to_all.25 = bf16[64,16,2048]{2,1,0:T(8,128)(2,1)S(1)} all-to-all(bf16[64,16,2048]{2,1,0:T(8,128)(2,1)S(1)} %bitcast.31), channel_id=1, replica_groups=mesh['z'=4,'yl'=2,'c'=2,'x'=4,'yh'=2] {'z','yl','x','yh'}, dimensions={0} | all-to-all | bytes 8388608 | tf_op jit(solution)/shard_map/all_to_all | solution.py:400
  295.8 1.8 combine.1
  (67 shorter events, 12.8 us)
Async XLA Ops:
  2.9 29.9 %all-to-all-start = ((bf16[16,400,128]{2,1,0:T(8,128)(2,1)}), bf16[16,400,128]{2,1,0:T(8,128)(2,1)S(1)}, u32[]{:S(2)}, u32[]{:S(2)}) async-start(bf16[16,400,128]{2,1,0:T(8,128)(2,1)} %pack.1), calls=%async_computation | async-start | bytes 3276800 | tf_op jit(solution)/shard_map/all_to_all | solution.py:300
  10.7 133.6 %collective-permute-start.11 = (bf16[704,2048]{1,0:T(8,128)(2,1)}, bf16[704,2048]{1,0:T(8,128)(2,1)}, u32[]{:S(2)}, u32[]{:S(2)}) collective-permute-start(bf16[704,2048]{1,0:T(8,128)(2,1)} %bitcast.41), channel_id=1, source_target_pairs={{0,16},{1,24},{2,18},{3,26},{4,20},{5,28},{6,22},{7,30},{8,17},{9,... | collective-permute-start | bytes 8650760 | tf_op jit(solution)/shard_map/ppermute | solution.py:290
  17.3 25.0 %copy-start.22 = (s32[1,128,6]{1,0,2:T(1,128)S(1)}, s32[1,128,6]{1,0,2:T(1,128)}, u32[]{:S(2)}) copy-start(s32[1,128,6]{1,0,2:T(1,128)} %param.19) | copy-start | bytes 9220
  17.3 25.0 %copy-start.23 = (s32[1,128,6]{1,0,2:T(1,128)S(1)}, s32[1,128,6]{1,0,2:T(1,128)}, u32[]{:S(2)}) copy-start(s32[1,128,6]{1,0,2:T(1,128)} %param.18) | copy-start | bytes 9220
  17.3 81.1 %copy-start.16 = (bf16[1,128,2048]{2,1,0:T(8,128)(2,1)S(1)}, bf16[1,128,2048]{2,1,0:T(8,128)(2,1)}, u32[]{:S(2)}) copy-start(bf16[1,128,2048]{2,1,0:T(8,128)(2,1)} %param.15) | copy-start | bytes 1572868
  17.3 81.1 %copy-start.21 = (f32[2048]{0:T(1024)S(1)}, f32[2048]{0:T(1024)}, u32[]{:S(2)}) copy-start(f32[2048]{0:T(1024)} %param.17) | copy-start | bytes 24580
  17.3 125.4 %collective-permute-start.3 = (bf16[960,1408]{1,0:T(8,128)(2,1)}, bf16[960,1408]{1,0:T(8,128)(2,1)}, u32[]{:S(2)}, u32[]{:S(2)}) collective-permute-start(bf16[960,1408]{1,0:T(8,128)(2,1)} %slice_bitcast_fusion), channel_id=1, source_target_pairs={{0,16},{1,24},{2,18},{3,26},{4,20},{5,28},{6,22},{7,30},{8,17},{9,... | collective-permute-start | bytes 8110088 | tf_op jit(solution)/shard_map/ppermute | solution.py:287
  38.0 60.4 %all-to-all-start.1 = ((bf16[16,128,128]{2,1,0:T(8,128)(2,1)}), bf16[16,128,128]{2,1,0:T(8,128)(2,1)S(1)}, u32[]{:S(2)}, u32[]{:S(2)}) async-start(bf16[16,128,128]{2,1,0:T(8,128)(2,1)} %attend.1), calls=%async_computation.1 | async-start | bytes 1048576 | tf_op jit(solution)/shard_map/all_to_all | solution.py:309
  107.0 37.5 %all-to-all-start.2 = ((bf16[16,16,2048]{2,1,0:T(8,128)(2,1)}), bf16[16,16,2048]{2,1,0:T(8,128)(2,1)S(1)}, u32[]{:S(2)}, u32[]{:S(2)}) async-start(bf16[16,16,2048]{2,1,0:T(8,128)(2,1)} %get-tuple-element.13), calls=%async_computation.2 | async-start | bytes 2097152 | tf_op jit(solution)/shard_map/all_to_all | solution.py:354
  111.8 15.0 %collective-permute-start.8 = (bf16[144,2048]{1,0:T(8,128)(2,1)S(1)}, bf16[144,2048]{1,0:T(8,128)(2,1)S(1)}, u32[]{:S(2)}, u32[]{:S(2)}) collective-permute-start(bf16[144,2048]{1,0:T(8,128)(2,1)S(1)} %get-tuple-element.14), channel_id=1, source_target_pairs={{0,16},{1,17},{2,18},{3,19},{4,20},{5,21},{6,22},{7,23},{8,24},{9,... | collective-permute-start | bytes 1769480 | tf_op jit(solution)/shard_map/ppermute | solution.py:353
  112.4 28.3 %collective-permute-start.9 = (bf16[144,2048]{1,0:T(8,128)(2,1)S(1)}, bf16[144,2048]{1,0:T(8,128)(2,1)S(1)}, u32[]{:S(2)}, u32[]{:S(2)}) collective-permute-start(bf16[144,2048]{1,0:T(8,128)(2,1)S(1)} %get-tuple-element.15), channel_id=1, source_target_pairs={{0,1},{1,0},{2,3},{3,2},{4,5},{5,4},{6,7},{7,6},{8,9},{9,8},{10,11... | collective-permute-start | bytes 1769480 | tf_op jit(solution)/shard_map/ppermute | solution.py:353
  115.3 25.4 %collective-permute-start.10 = (bf16[144,2048]{1,0:T(8,128)(2,1)S(1)}, bf16[144,2048]{1,0:T(8,128)(2,1)S(1)}, u32[]{:S(2)}, u32[]{:S(2)}) collective-permute-start(bf16[144,2048]{1,0:T(8,128)(2,1)S(1)} %get-tuple-element.16), channel_id=1, source_target_pairs={{0,17},{1,16},{2,19},{3,18},{4,21},{5,20},{6,23},{7,22},{8,25},{9,... | collective-permute-start | bytes 1769480 | tf_op jit(solution)/shard_map/ppermute | solution.py:353
  142.7 52.5 %collective-permute-start.7 = (bf16[960,1408]{1,0:T(8,128)(2,1)}, bf16[960,1408]{1,0:T(8,128)(2,1)}, u32[]{:S(2)}, u32[]{:S(2)}) collective-permute-start(bf16[960,1408]{1,0:T(8,128)(2,1)} %collective-permute-done.3.refs_3_), channel_id=1, source_target_pairs={{0,8},{1,9},{2,10},{3,11},{4,12},{5,13},{6,14},{7,15},{8,0},{9,1},... | collective-permute-start | bytes 8110088 | tf_op jit(solution)/shard_map/ppermute | solution.py:288
  144.4 78.8 %collective-permute-start.12 = (bf16[704,2048]{1,0:T(8,128)(2,1)}, bf16[704,2048]{1,0:T(8,128)(2,1)}, u32[]{:S(2)}, u32[]{:S(2)}) collective-permute-start(bf16[704,2048]{1,0:T(8,128)(2,1)} %collective-permute-done.11.down_any), channel_id=1, source_target_pairs={{0,8},{1,9},{2,10},{3,11},{4,12},{5,13},{6,14},{7,15},{8,0},{9,1},... | collective-permute-start | bytes 8650760 | tf_op jit(solution)/shard_map/ppermute | solution.py:291
  145.4 57.9 %all-to-all-start.3 = ((bf16[16,48,2048]{2,1,0:T(8,128)(2,1)}), bf16[16,48,2048]{2,1,0:T(8,128)(2,1)S(1)}, u32[]{:S(2)}, u32[]{:S(2)}) async-start(bf16[16,48,2048]{2,1,0:T(8,128)(2,1)} %bitcast.37), calls=%async_computation.3 | async-start | bytes 6291456 | tf_op jit(solution)/shard_map/all_to_all | solution.py:368
  152.0 38.7 %copy-start.1 = (bf16[16,16,2048]{2,1,0:T(8,128)(2,1)S(1)}, bf16[16,16,2048]{2,1,0:T(8,128)(2,1)}, u32[]{:S(2)}) copy-start(bf16[16,16,2048]{2,1,0:T(8,128)(2,1)} %copy-done) | copy-start | bytes 3145732
  153.5 18.1 %collective-permute-start.2 = (bf16[448,1408]{1,0:T(8,128)(2,1)S(1)}, bf16[448,1408]{1,0:T(8,128)(2,1)S(1)}, u32[]{:S(2)}, u32[]{:S(2)}) collective-permute-start(bf16[448,1408]{1,0:T(8,128)(2,1)S(1)} %slice_bitcast_fusion.1), channel_id=1, source_target_pairs={{0,16},{1,24},{2,18},{3,26},{4,20},{5,28},{6,22},{7,30},{8,17},{9,... | collective-permute-start | bytes 3784712 | tf_op jit(solution)/shard_map/ppermute | solution.py:287
  157.7 25.5 %collective-permute-start.1 = (bf16[384,1408]{1,0:T(8,128)(2,1)S(1)}, bf16[384,1408]{1,0:T(8,128)(2,1)S(1)}, u32[]{:S(2)}, u32[]{:S(2)}) collective-permute-start(bf16[384,1408]{1,0:T(8,128)(2,1)S(1)} %slice_bitcast_fusion.2), channel_id=1, source_target_pairs={{0,16},{1,24},{2,18},{3,26},{4,20},{5,28},{6,22},{7,30},{8,17},{9,... | collective-permute-start | bytes 3244040 | tf_op jit(solution)/shard_map/ppermute | solution.py:287
  159.1 31.6 %collective-permute-start = (bf16[256,1408]{1,0:T(8,128)(2,1)S(1)}, bf16[256,1408]{1,0:T(8,128)(2,1)S(1)}, u32[]{:S(2)}, u32[]{:S(2)}) collective-permute-start(bf16[256,1408]{1,0:T(8,128)(2,1)S(1)} %slice_bitcast_fusion.3), channel_id=1, source_target_pairs={{0,16},{1,24},{2,18},{3,26},{4,20},{5,28},{6,22},{7,30},{8,17},{9,... | collective-permute-start | bytes 2162696 | tf_op jit(solution)/shard_map/ppermute | solution.py:287
  171.6 23.5 %copy-start.2 = (bf16[448,1408]{1,0:T(8,128)(2,1)}, bf16[448,1408]{1,0:T(8,128)(2,1)S(1)}, u32[]{:S(2)}) copy-start(bf16[448,1408]{1,0:T(8,128)(2,1)S(1)} %collective-permute-done.2.refs_2_) | copy-start | bytes 3784708
  171.6 23.6 %collective-permute-start.6 = (bf16[448,1408]{1,0:T(8,128)(2,1)S(1)}, bf16[448,1408]{1,0:T(8,128)(2,1)S(1)}, u32[]{:S(2)}, u32[]{:S(2)}) collective-permute-start(bf16[448,1408]{1,0:T(8,128)(2,1)S(1)} %collective-permute-done.2.refs_2_), channel_id=1, source_target_pairs={{0,8},{1,9},{2,10},{3,11},{4,12},{5,13},{6,14},{7,15},{8,0},{9,1},... | collective-permute-start | bytes 3784712 | tf_op jit(solution)/shard_map/ppermute | solution.py:288
  183.2 12.0 %copy-start.6 = (bf16[384,1408]{1,0:T(8,128)(2,1)}, bf16[384,1408]{1,0:T(8,128)(2,1)S(1)}, u32[]{:S(2)}) copy-start(bf16[384,1408]{1,0:T(8,128)(2,1)S(1)} %collective-permute-done.1.refs_1_) | copy-start | bytes 3244036
  183.2 12.0 %collective-permute-start.5 = (bf16[384,1408]{1,0:T(8,128)(2,1)S(1)}, bf16[384,1408]{1,0:T(8,128)(2,1)S(1)}, u32[]{:S(2)}, u32[]{:S(2)}) collective-permute-start(bf16[384,1408]{1,0:T(8,128)(2,1)S(1)} %collective-permute-done.1.refs_1_), channel_id=1, source_target_pairs={{0,8},{1,9},{2,10},{3,11},{4,12},{5,13},{6,14},{7,15},{8,0},{9,1},... | collective-permute-start | bytes 3244040 | tf_op jit(solution)/shard_map/ppermute | solution.py:288
  190.7 4.5 %copy-start.10 = (bf16[256,1408]{1,0:T(8,128)(2,1)}, bf16[256,1408]{1,0:T(8,128)(2,1)S(1)}, u32[]{:S(2)}) copy-start(bf16[256,1408]{1,0:T(8,128)(2,1)S(1)} %collective-permute-done.refs_0_) | copy-start | bytes 2162692
  190.7 4.5 %collective-permute-start.4 = (bf16[256,1408]{1,0:T(8,128)(2,1)S(1)}, bf16[256,1408]{1,0:T(8,128)(2,1)S(1)}, u32[]{:S(2)}, u32[]{:S(2)}) collective-permute-start(bf16[256,1408]{1,0:T(8,128)(2,1)S(1)} %collective-permute-done.refs_0_), channel_id=1, source_target_pairs={{0,8},{1,9},{2,10},{3,11},{4,12},{5,13},{6,14},{7,15},{8,0},{9,1},... | collective-permute-start | bytes 2162696 | tf_op jit(solution)/shard_map/ppermute | solution.py:288
  203.3 1.3 copy-start.3
  207.0 8.2 %copy-start.5 = (bf16[448,1408]{1,0:T(8,128)(2,1)S(1)}, bf16[448,1408]{1,0:T(8,128)(2,1)}, u32[]{:S(2)}) copy-start(bf16[448,1408]{1,0:T(8,128)(2,1)} %copy-done.4) | copy-start | bytes 3784708
  207.0 8.2 %copy-start.9 = (bf16[384,1408]{1,0:T(8,128)(2,1)S(1)}, bf16[384,1408]{1,0:T(8,128)(2,1)}, u32[]{:S(2)}) copy-start(bf16[384,1408]{1,0:T(8,128)(2,1)} %copy-done.8) | copy-start | bytes 3244036
  207.0 8.2 %copy-start.13 = (bf16[256,1408]{1,0:T(8,128)(2,1)S(1)}, bf16[256,1408]{1,0:T(8,128)(2,1)}, u32[]{:S(2)}) copy-start(bf16[256,1408]{1,0:T(8,128)(2,1)} %copy-done.12) | copy-start | bytes 2162692
  215.2 8.0 %copy-start.15 = (bf16[256,704]{1,0:T(8,128)(2,1)S(1)}, bf16[256,704]{1,0:T(8,128)(2,1)}, u32[]{:S(2)}) copy-start(bf16[256,704]{1,0:T(8,128)(2,1)} %copy-done.14) | copy-start | bytes 1081348
  233.5 62.3 %copy-start.18 = (bf16[128,2048]{1,0:T(8,128)(2,1)S(1)}, bf16[128,2048]{1,0:T(8,128)(2,1)}, u32[]{:S(2)}) copy-start(bf16[128,2048]{1,0:T(8,128)(2,1)} %copy-done.17) | copy-start | bytes 1572868
  233.5 62.3 %copy-start.20 = (bf16[1024,128]{1,0:T(8,128)(2,1)S(1)}, bf16[1024,128]{1,0:T(8,128)(2,1)}, u32[]{:S(2)}) copy-start(bf16[1024,128]{1,0:T(8,128)(2,1)} %get-tuple-element.17.weight_ref) | copy-start | bytes 786436
  (9 other events, 8.7 us)
